TPU v7x, 32 devices: a whole 2x2x4 slice. The times are simulated.
32 devices in a mesh: dp: 8 (over y, x, core), tensor: 4 (over z).
Axes of the slice: x: 2, y: 2, z: 4, core: 2. Of those that a mesh axis runs over, the one named last changes fastest.
Arguments:
- hidden_in: bfloat16 [16384, 1024], P(('dp', 'tensor')), may hold values from -6 to 6
- cotangent: bfloat16 [16384, 1024], P(('dp', 'tensor')), may hold values from -6 to 6
- norm_gains: bfloat16 [1024, 2], P('dp'), may hold values from 0.5 to 1.5
- mixer_in: bfloat16 [1024, 1536], P('dp', 'tensor'), may hold values from -0.1875 to 0.1875
- branch_gate: bfloat16 [1024, 1536], P('dp', 'tensor'), may hold values from -0.1875 to 0.1875
- mixer_out: bfloat16 [1024, 1536], P('dp', 'tensor'), may hold values from -0.4375 to 0.4375
- input_gate: bfloat16 [128, 12, 128], P('dp', 'tensor'), may hold values from -0.5 to 0.5
- recur_gate: bfloat16 [128, 12, 128], P('dp', 'tensor'), may hold values from -0.5 to 0.5
- conv_kernel: bfloat16 [128, 4, 12], P('dp', None, 'tensor'), may hold values from -3 to 3
- conv_bias: bfloat16 [128, 12], P('dp', 'tensor'), may hold values from -4 to 4
- input_bias: bfloat16 [128, 12], P('dp', 'tensor'), may hold values from -6 to 6
- recur_bias: bfloat16 [128, 12], P('dp', 'tensor'), may hold values from -6 to 6
- decay_param: bfloat16 [128, 12], P('dp', 'tensor'), may hold values from 2 to 9
- mlp_gate: bfloat16 [1024, 3072], P('dp', 'tensor'), may hold values from -0.1875 to 0.1875
- mlp_up: bfloat16 [1024, 3072], P('dp', 'tensor'), may hold values from -0.1875 to 0.1875
- mlp_down: bfloat16 [1024, 3072], P('dp', 'tensor'), may hold values from -0.15625 to 0.15625
Outputs:
- hidden_out: bfloat16 [16384, 1024], P(('dp', 'tensor'))
- hidden_grad: float32 [16384, 1024], P(('dp', 'tensor'))
- norm_gains_grad: float32 [1024, 2], P(('dp', 'tensor'))
- mixer_in_grad: float32 [1024, 1536], P('dp', 'tensor')
- branch_gate_grad: float32 [1024, 1536], P('dp', 'tensor')
- mixer_out_grad: float32 [1024, 1536], P('dp', 'tensor')
- input_gate_grad: float32 [128, 12, 128], P('dp', 'tensor')
- recur_gate_grad: float32 [128, 12, 128], P('dp', 'tensor')
- conv_kernel_grad: float32 [128, 4, 12], P('dp', None, 'tensor')
- conv_bias_grad: float32 [128, 12], P('dp', 'tensor')
- input_bias_grad: float32 [128, 12], P('dp', 'tensor')
- recur_bias_grad: float32 [128, 12], P('dp', 'tensor')
- decay_param_grad: float32 [128, 12], P('dp', 'tensor')
- mlp_gate_grad: float32 [1024, 3072], P('dp', 'tensor')
- mlp_up_grad: float32 [1024, 3072], P('dp', 'tensor')
- mlp_down_grad: float32 [1024, 3072], P('dp', 'tensor')
All inputs are finite; a program needn't handle non-finite values.
Results may differ from a plain program's by a relative error of at most 0.02.
Values may be sent and summed in bfloat16 or wider, within the bound.
No kernel may reach another device: no remote copies, remote signals or barrier semaphores. Data moves between devices by JAX's collectives and lax.ppermute only.
A program may use at most 256 MiB of HBM per device.

v0:
```python
import jax
import jax.numpy as jnp
from jax import lax
from jax.sharding import PartitionSpec as P

BLOCK = 128
CONV = 4


epsilon = 1e-06


def product(left_side, right_side):
    return jnp.dot(left_side, right_side, preferred_element_type=jnp.float32)


def product_nt(left_side, right_side):
    return lax.dot_general(
        left_side, right_side, (((1,), (1,)), ((), ())), preferred_element_type=jnp.float32
    )


def product_tn(left_side, right_side):
    return lax.dot_general(
        left_side, right_side, (((0,), (0,)), ((), ())), preferred_element_type=jnp.float32
    )


def rms_parts(values):
    scaling = lax.rsqrt(jnp.mean(values * values, axis=1, keepdims=True) + epsilon)
    return (values * scaling, scaling)


def channels(table_rows):
    return table_rows.astype(jnp.float32).T.reshape(-1)


def to_table(vector):
    return vector.reshape(-1, BLOCK).T


def causal_conv(signal, kernel, conv_shift):
    length = signal.shape[0]
    padded = jnp.pad(signal, ((CONV - 1, 0), (0, 0)))
    result = conv_shift + kernel[0] * signal
    for offset in range(1, CONV):
        result = result + kernel[offset] * padded[CONV - 1 - offset : CONV - 1 - offset + length]
    return result


def combine(earlier_part, later_part):
    return (earlier_part[0] * later_part[0], later_part[0] * earlier_part[1] + later_part[1])


def mixer(conv_out, rec_pre, inp_pre, rec_shift, inp_shift, decay_rate, gate_pre):
    recur_open = jax.nn.sigmoid(rec_pre + rec_shift)
    inflow = jax.nn.sigmoid(inp_pre + inp_shift)
    log_decay = -8.0 * recur_open * jax.nn.softplus(-decay_rate)
    multiplier = jnp.sqrt(-jnp.expm1(2.0 * log_decay))
    states = lax.associative_scan(
        combine, (jnp.exp(log_decay), multiplier * inflow * conv_out), axis=0
    )[1]
    return states * jax.nn.gelu(gate_pre)


def gated_gelu(gate_val, up_val):
    return jax.nn.gelu(gate_val) * up_val


def gather_rows(values):
    return lax.all_gather(values, "tensor", axis=0, tiled=True)


def gather_grads(values):
    return lax.all_gather(values, "tensor", axis=0, tiled=True)


def row_sums(values):
    return lax.psum_scatter(
        values.astype(jnp.bfloat16), "tensor", scatter_dimension=0, tiled=True
    ).astype(jnp.float32)


def grad_sums(values):
    return lax.psum_scatter(
        values.astype(jnp.bfloat16), "tensor", scatter_dimension=0, tiled=True
    ).astype(jnp.float32)


def per_device(
    hidden_in,
    cotangent,
    norm_gains,
    mixer_in,
    branch_gate,
    mixer_out,
    input_gate,
    recur_gate,
    conv_kernel,
    conv_bias,
    input_bias,
    recur_bias,
    decay_param,
    mlp_gate,
    mlp_up,
    mlp_down,
):

    def fetch_mixer():
        return (
            lax.all_gather(norm_gains, "dp", axis=0, tiled=True),
            lax.all_gather(mixer_in, "dp", axis=0, tiled=True),
            lax.all_gather(branch_gate, "dp", axis=0, tiled=True),
            lax.all_gather(mixer_out, "dp", axis=0, tiled=True),
            lax.all_gather(input_gate, "dp", axis=0, tiled=True),
            lax.all_gather(recur_gate, "dp", axis=0, tiled=True),
            lax.all_gather(conv_kernel, "dp", axis=0, tiled=True),
            lax.all_gather(conv_bias, "dp", axis=0, tiled=True),
            lax.all_gather(input_bias, "dp", axis=0, tiled=True),
            lax.all_gather(recur_bias, "dp", axis=0, tiled=True),
            lax.all_gather(decay_param, "dp", axis=0, tiled=True),
        )

    def fetch_mlp():
        return (
            lax.all_gather(mlp_gate, "dp", axis=0, tiled=True),
            lax.all_gather(mlp_up, "dp", axis=0, tiled=True),
            lax.all_gather(mlp_down, "dp", axis=0, tiled=True),
        )

    (
        gain_full,
        in_full,
        bgate_full,
        out_full,
        igate_full,
        rgate_full,
        kernel_full,
        cbias_full,
        ibias_full,
        rbias_full,
        decay_full,
    ) = fetch_mixer()
    gain_one = gain_full[:, 0].astype(jnp.float32)
    gain_two = gain_full[:, 1].astype(jnp.float32)
    residual = hidden_in.astype(jnp.float32)
    unit_one, scale_one = rms_parts(residual)
    normed_one = gather_rows((unit_one * gain_one).astype(jnp.bfloat16))
    branch_in = product(normed_one, in_full)
    gate_pre = product(normed_one, bgate_full)
    kernel = kernel_full.astype(jnp.float32).transpose(1, 2, 0).reshape(CONV, -1)
    conv_out, conv_back = jax.vjp(causal_conv, branch_in, kernel, channels(cbias_full))
    length = conv_out.shape[0]
    channel_count = conv_out.shape[1]
    blocked = conv_out.astype(jnp.bfloat16).reshape(length, channel_count // BLOCK, BLOCK)
    rec_pre = jnp.einsum(
        "tbj,jbk->tbk", blocked, rgate_full, preferred_element_type=jnp.float32
    ).reshape(length, channel_count)
    inp_pre = jnp.einsum(
        "tbj,jbk->tbk", blocked, igate_full, preferred_element_type=jnp.float32
    ).reshape(length, channel_count)
    mixed_out, mixer_back = jax.vjp(
        mixer,
        conv_out,
        rec_pre,
        inp_pre,
        channels(rbias_full),
        channels(ibias_full),
        channels(decay_full),
        gate_pre,
    )
    mixed_low = mixed_out.astype(jnp.bfloat16)
    middle = residual + row_sums(product_nt(mixed_low, out_full))
    unit_two, scale_two = rms_parts(middle)
    normed_two = gather_rows((unit_two * gain_two).astype(jnp.bfloat16))
    mgate_full, mup_full, mdown_full = fetch_mlp()
    gate_val = product(normed_two, mgate_full)
    up_val = product(normed_two, mup_full)
    hidden_act, act_back = jax.vjp(gated_gelu, gate_val, up_val)
    hidden_low = hidden_act.astype(jnp.bfloat16)
    hidden_out = (middle + row_sums(product_nt(hidden_low, mdown_full))).astype(jnp.bfloat16)
    mgate_full, mup_full, mdown_full = fetch_mlp()
    cot_full = gather_grads(cotangent)
    down_grad = product_tn(cot_full, hidden_low)
    act_grad = product(cot_full, mdown_full)
    gate_grad, up_grad = act_back(act_grad)
    gate_low = gate_grad.astype(jnp.bfloat16)
    up_low = up_grad.astype(jnp.bfloat16)
    mgate_grad = product_tn(normed_two, gate_low)
    mup_grad = product_tn(normed_two, up_low)
    normed_two_grad = grad_sums(product_nt(gate_low, mgate_full) + product_nt(up_low, mup_full))
    scaled_two = normed_two_grad * gain_two
    gain_two_part = jnp.sum(normed_two_grad * unit_two, axis=0)
    middle_grad = cotangent.astype(jnp.float32) + scale_two * (
        scaled_two - unit_two * jnp.mean(scaled_two * unit_two, axis=1, keepdims=True)
    )
    (
        gain_full,
        in_full,
        bgate_full,
        out_full,
        igate_full,
        rgate_full,
        kernel_full,
        cbias_full,
        ibias_full,
        rbias_full,
        decay_full,
    ) = fetch_mixer()
    middle_low = middle_grad.astype(jnp.bfloat16)
    branch_cot = gather_grads(middle_low)
    out_grad = product_tn(branch_cot, mixed_low)
    mixed_grad = product(branch_cot, out_full)
    conv_grad_rec, rec_pre_grad, inp_pre_grad, rbias_grad, ibias_grad, decay_grad, gate_pre_grad = (
        mixer_back(mixed_grad)
    )
    rec_low = rec_pre_grad.astype(jnp.bfloat16).reshape(length, channel_count // BLOCK, BLOCK)
    inp_low = inp_pre_grad.astype(jnp.bfloat16).reshape(length, channel_count // BLOCK, BLOCK)
    gate_back = jnp.einsum(
        "tbk,jbk->tbj", rec_low, rgate_full, preferred_element_type=jnp.float32
    ) + jnp.einsum("tbk,jbk->tbj", inp_low, igate_full, preferred_element_type=jnp.float32)
    conv_grad = conv_grad_rec + gate_back.reshape(length, channel_count)
    rgate_grad = jnp.einsum("tbj,tbk->jbk", blocked, rec_low, preferred_element_type=jnp.float32)
    igate_grad = jnp.einsum("tbj,tbk->jbk", blocked, inp_low, preferred_element_type=jnp.float32)
    branch_grad, kernel_grad, cbias_grad = conv_back(conv_grad)
    branch_low = branch_grad.astype(jnp.bfloat16)
    gate_pre_low = gate_pre_grad.astype(jnp.bfloat16)
    in_grad = product_tn(normed_one, branch_low)
    bgate_grad = product_tn(normed_one, gate_pre_low)
    normed_one_grad = grad_sums(
        product_nt(branch_low, in_full) + product_nt(gate_pre_low, bgate_full)
    )
    scaled_one = normed_one_grad * gain_one
    gain_one_part = jnp.sum(normed_one_grad * unit_one, axis=0)
    hidden_grad = middle_grad + scale_one * (
        scaled_one - unit_one * jnp.mean(scaled_one * unit_one, axis=1, keepdims=True)
    )
    gains_summed = lax.psum_scatter(
        jnp.stack([gain_one_part, gain_two_part], axis=1),
        ("dp", "tensor"),
        scatter_dimension=0,
        tiled=True,
    )
    kernel_table = kernel_grad.reshape(CONV, -1, BLOCK).transpose(2, 0, 1)
    summed_all = (
        lax.psum_scatter(in_grad, "dp", scatter_dimension=0, tiled=True),
        lax.psum_scatter(bgate_grad, "dp", scatter_dimension=0, tiled=True),
        lax.psum_scatter(out_grad, "dp", scatter_dimension=0, tiled=True),
        lax.psum_scatter(igate_grad, "dp", scatter_dimension=0, tiled=True),
        lax.psum_scatter(rgate_grad, "dp", scatter_dimension=0, tiled=True),
        lax.psum_scatter(kernel_table, "dp", scatter_dimension=0, tiled=True),
        lax.psum_scatter(to_table(cbias_grad), "dp", scatter_dimension=0, tiled=True),
        lax.psum_scatter(to_table(ibias_grad), "dp", scatter_dimension=0, tiled=True),
        lax.psum_scatter(to_table(rbias_grad), "dp", scatter_dimension=0, tiled=True),
        lax.psum_scatter(to_table(decay_grad), "dp", scatter_dimension=0, tiled=True),
        lax.psum_scatter(mgate_grad, "dp", scatter_dimension=0, tiled=True),
        lax.psum_scatter(mup_grad, "dp", scatter_dimension=0, tiled=True),
        lax.psum_scatter(down_grad, "dp", scatter_dimension=0, tiled=True),
    )
    mixer_summed = summed_all[:10]
    mlp_summed = summed_all[10:]
    return (
        hidden_out,
        hidden_grad,
        gains_summed,
        mixer_summed[0],
        mixer_summed[1],
        mixer_summed[2],
        mixer_summed[3],
        mixer_summed[4],
        mixer_summed[5],
        mixer_summed[6],
        mixer_summed[7],
        mixer_summed[8],
        mixer_summed[9],
        mlp_summed[0],
        mlp_summed[1],
        mlp_summed[2],
    )


def solution(mesh):
    placed = (
        P(("dp", "tensor"), None),
        P(("dp", "tensor"), None),
        P("dp", None),
        P("dp", "tensor"),
        P("dp", "tensor"),
        P("dp", "tensor"),
        P("dp", "tensor", None),
        P("dp", "tensor", None),
        P("dp", None, "tensor"),
        P("dp", "tensor"),
        P("dp", "tensor"),
        P("dp", "tensor"),
        P("dp", "tensor"),
        P("dp", "tensor"),
        P("dp", "tensor"),
        P("dp", "tensor"),
    )
    return jax.shard_map(
        per_device,
        mesh=mesh,
        in_specs=placed,
        out_specs=(
            P(("dp", "tensor"), None),
            P(("dp", "tensor"), None),
            P(("dp", "tensor"), None),
            P("dp", "tensor"),
            P("dp", "tensor"),
            P("dp", "tensor"),
            P("dp", "tensor", None),
            P("dp", "tensor", None),
            P("dp", None, "tensor"),
            P("dp", "tensor"),
            P("dp", "tensor"),
            P("dp", "tensor"),
            P("dp", "tensor"),
            P("dp", "tensor"),
            P("dp", "tensor"),
            P("dp", "tensor"),
        ),
        check_vma=False,
    )
```

profile of v0, /device:TPU:0, one launch (start us, length us, event | category | flops | bytes accessed | tf_op | source)
XLA Modules:
  0.0 1838.4 jit_solution(15358968270343730277)
XLA Ops:
  8.1 10.5 all_gather.64
  84.1 9.5 all_gather.66
  93.6 11.2 all_gather.72
  104.9 10.9 all_gather.73
  338.3 9.6 pad.460
  347.9 9.3 multiply_convert_fusion.2
  363.3 76.6 %reduce-scatter.29.cloned.1.call-done = bf16[512,1024]{1,0:T(8,128)(2,1)} async-done(((bf16[2048,1024]{1,0:T(8,128)(2,1)}), bf16[512,1024]{1,0:T(8,128)(2,1)}) %reduce-scatter.29.cloned.1.call-update) | async-done | bytes 1048592 | tf_op jit(solution)/shard_map/reduce_scatter | solution.py:79
  446.3 79.1 %all-gather.14.cloned.1.call-done = bf16[2048,1024]{1,0:T(8,128)(2,1)} async-done(((bf16[512,1024]{1,0:T(8,128)(2,1)}), bf16[2048,1024]{1,0:T(8,128)(2,1)}) %all-gather.14.cloned.1.call-update) | async-done | bytes 4194320 | tf_op jit(solution)/shard_map/all_gather | solution.py:71
  534.1 17.0 all-gather.18.cloned.1.call-done
  559.9 18.6 %all-gather.20.cloned.1.call-done = bf16[1024,768]{1,0:T(8,128)(2,1)} async-done(((bf16[128,768]{1,0:T(8,128)(2,1)}), bf16[1024,768]{1,0:T(8,128)(2,1)}) %all-gather.20.cloned.1.call-update) | async-done | bytes 1572880 | tf_op jit(solution)/shard_map/all_gather | solution.py:128
  578.5 82.2 %all-gather.22.cloned.1.call-done = bf16[2048,1024]{1,0:T(8,128)(2,1)} async-done(((bf16[512,1024]{1,0:T(8,128)(2,1)}), bf16[2048,1024]{1,0:T(8,128)(2,1)}) %all-gather.22.cloned.1.call-update) | async-done | bytes 4194320 | tf_op jit(solution)/shard_map/all_gather | solution.py:75
  660.7 13.6 multiply_convert_fusion
  683.2 75.4 %reduce-scatter.33.cloned.1.call-done = bf16[512,1024]{1,0:T(8,128)(2,1)} async-done(((bf16[2048,1024]{1,0:T(8,128)(2,1)}), bf16[512,1024]{1,0:T(8,128)(2,1)}) %reduce-scatter.33.cloned.1.call-update) | async-done | bytes 1048592 | tf_op jit(solution)/shard_map/reduce_scatter | solution.py:85
  763.8 81.2 %all-gather.24.cloned.1.call-done = bf16[2048,1024]{1,0:T(8,128)(2,1)} async-done(((bf16[512,1024]{1,0:T(8,128)(2,1)}), bf16[2048,1024]{1,0:T(8,128)(2,1)}) %all-gather.24.cloned.1.call-update) | async-done | bytes 4194320 | tf_op jit(solution)/shard_map/all_gather | solution.py:75
  845.0 9.9 fusion.13
  991.2 9.8 pad.565
  1018.5 10.2 pad.463
  1028.7 11.6 multiply_reduce_fusion
  1063.0 10.7 multiply_reduce_fusion.4
  1109.8 48.2 %reduce-scatter.35.cloned.1.call-done = bf16[512,1024]{1,0:T(8,128)(2,1)} async-done(((bf16[2048,1024]{1,0:T(8,128)(2,1)}), bf16[512,1024]{1,0:T(8,128)(2,1)}) %reduce-scatter.35.cloned.1.call-update) | async-done | bytes 1048592 | tf_op jit(solution)/shard_map/reduce_scatter | solution.py:85
  1209.7 34.5 %reduce-scatter.53.cloned.1.call-done = f32[16,3]{1,0:T(8,128)} async-done(((f32[128,3]{1,0:T(8,128)}), f32[16,3]{1,0:T(8,128)}) %reduce-scatter.53.cloned.1.call-update) | async-done | bytes 208
  1245.6 35.2 %reduce-scatter.55.cloned.1.call-done = f32[16,3]{1,0:T(8,128)} async-done(((f32[128,3]{1,0:T(8,128)}), f32[16,3]{1,0:T(8,128)}) %reduce-scatter.55.cloned.1.call-update) | async-done | bytes 208
  1282.1 35.2 %reduce-scatter.57.cloned.1.call-done = f32[16,3]{1,0:T(8,128)} async-done(((f32[128,3]{1,0:T(8,128)}), f32[16,3]{1,0:T(8,128)}) %reduce-scatter.57.cloned.1.call-update) | async-done | bytes 208
  1318.7 35.2 %reduce-scatter.59.cloned.1.call-done = f32[16,3]{1,0:T(8,128)} async-done(((f32[128,3]{1,0:T(8,128)}), f32[16,3]{1,0:T(8,128)}) %reduce-scatter.59.cloned.1.call-update) | async-done | bytes 208
  1355.2 35.0 %reduce-scatter.51.cloned.1.call-done = f32[16,12]{1,0:T(8,128)} async-done(((f32[128,12]{1,0:T(8,128)}), f32[16,12]{1,0:T(8,128)}) %reduce-scatter.51.cloned.1.call-update) | async-done | bytes 784
  1393.8 75.6 %reduce-scatter.31.cloned.1.call-done = bf16[512,1024]{1,0:T(8,128)(2,1)} async-done(((bf16[2048,1024]{1,0:T(8,128)(2,1)}), bf16[512,1024]{1,0:T(8,128)(2,1)}) %reduce-scatter.31.cloned.1.call-update) | async-done | bytes 1048592 | tf_op jit(solution)/shard_map/reduce_scatter | solution.py:79
  1473.7 134.1 %reduce-scatter.49.cloned.1.call-done = f32[32,2]{1,0:T(8,128)} async-done(((f32[1024,2]{1,0:T(8,128)}), f32[32,2]{1,0:T(8,128)}) %reduce-scatter.49.cloned.1.call-update) | async-done | bytes 272
  1609.2 45.4 %reduce-scatter.43.cloned.1.call-done = f32[128,768]{1,0:T(8,128)} async-done(((f32[1024,768]{1,0:T(8,128)}), f32[128,768]{1,0:T(8,128)}) %reduce-scatter.43.cloned.1.call-update) | async-done | bytes 393232 | tf_op jit(solution)/shard_map/reduce_scatter | solution.py:256
  1654.6 49.9 %reduce-scatter.45.cloned.1.call-done = f32[128,768]{1,0:T(8,128)} async-done(((f32[1024,768]{1,0:T(8,128)}), f32[128,768]{1,0:T(8,128)}) %reduce-scatter.45.cloned.1.call-update) | async-done | bytes 393232 | tf_op jit(solution)/shard_map/reduce_scatter | solution.py:257
  1704.5 42.1 %reduce-scatter.37.cloned.1.call-done = f32[128,384]{1,0:T(8,128)} async-done(((f32[1024,384]{1,0:T(8,128)}), f32[128,384]{1,0:T(8,128)}) %reduce-scatter.37.cloned.1.call-update) | async-done | bytes 196624 | tf_op jit(solution)/shard_map/reduce_scatter | solution.py:246
  1746.6 42.1 %reduce-scatter.39.cloned.1.call-done = f32[128,384]{1,0:T(8,128)} async-done(((f32[1024,384]{1,0:T(8,128)}), f32[128,384]{1,0:T(8,128)}) %reduce-scatter.39.cloned.1.call-update) | async-done | bytes 196624 | tf_op jit(solution)/shard_map/reduce_scatter | solution.py:247
  1788.7 42.1 %reduce-scatter.41.cloned.1.call-done = f32[128,384]{1,0:T(8,128)} async-done(((f32[1024,384]{1,0:T(8,128)}), f32[128,384]{1,0:T(8,128)}) %reduce-scatter.41.cloned.1.call-update) | async-done | bytes 196624 | tf_op jit(solution)/shard_map/reduce_scatter | solution.py:248
  (763 shorter events, 607.9 us)
Async XLA Ops:
  8.1 108.2 %all-gather.12.cloned.1.call-start = ((), (), s32[]{:S(2)}) async-start(), calls=%async_computation.16 | async-start | bytes 5242880 | tf_op jit(solution)/shard_map/all_gather | solution.py:71
  22.8 417.1 %reduce-scatter.29.cloned.1.call-start = ((), (), s32[]{:S(2)}) async-start(), calls=%async_computation.17 | async-start | bytes 5242880 | tf_op jit(solution)/shard_map/reduce_scatter | solution.py:79
  32.3 88.6 %copy-start.144 = (f32[1,3,128]{2,1,0:T(4,128)}, f32[1,3,128]{2,1,0:T(4,128)S(1)}, u32[]{:S(2)}) copy-start(f32[1,3,128]{2,1,0:T(4,128)S(1)} %copy.118) | copy-start | bytes 4612
  32.4 88.5 %copy-start.146 = (f32[1,3,128]{2,1,0:T(4,128)}, f32[1,3,128]{2,1,0:T(4,128)S(1)}, u32[]{:S(2)}) copy-start(f32[1,3,128]{2,1,0:T(4,128)S(1)} %copy.117) | copy-start | bytes 4612
  362.7 83.6 %all-gather.16.cloned.1.call-start = ((), (), s32[]{:S(2)}) async-start(), calls=%async_computation.19 | async-start | bytes 1769472 | tf_op jit(solution)/shard_map/all_gather | solution.py:126
  363.3 162.1 %all-gather.14.cloned.1.call-start = ((), (), s32[]{:S(2)}) async-start(), calls=%async_computation.18 | async-start | bytes 5242880 | tf_op jit(solution)/shard_map/all_gather | solution.py:71
  441.5 92.6 %copy-start.122 = (f32[512]{0:T(512)}, f32[512]{0:T(512)S(1)}, u32[]{:S(2)}) copy-start(f32[512]{0:T(512)S(1)} %add_rsqrt_fusion) | copy-start | bytes 6148
  444.2 106.9 %all-gather.18.cloned.1.call-start = ((), (), s32[]{:S(2)}) async-start(), calls=%async_computation.20 | async-start | bytes 1769472 | tf_op jit(solution)/shard_map/all_gather | solution.py:127
  444.7 133.7 %all-gather.20.cloned.1.call-start = ((), (), s32[]{:S(2)}) async-start(), calls=%async_computation.21 | async-start | bytes 1769472 | tf_op jit(solution)/shard_map/all_gather | solution.py:128
  445.5 215.2 %all-gather.22.cloned.1.call-start = ((), (), s32[]{:S(2)}) async-start(), calls=%async_computation.23 | async-start | bytes 5242880 | tf_op jit(solution)/shard_map/all_gather | solution.py:75
  446.2 312.3 %reduce-scatter.33.cloned.1.call-start = ((), (), s32[]{:S(2)}) async-start(), calls=%async_computation.24 | async-start | bytes 5242880 | tf_op jit(solution)/shard_map/reduce_scatter | solution.py:85
  559.9 114.4 %copy-start.168 = (bf16[1024,768]{1,0:T(8,128)(2,1)S(1)}, bf16[1024,768]{1,0:T(8,128)(2,1)}, u32[]{:S(2)}) copy-start(bf16[1024,768]{1,0:T(8,128)(2,1)} %all-gather.16.cloned.1.call-done) | copy-start | bytes 4718596
  683.1 161.9 %all-gather.24.cloned.1.call-start = ((), (), s32[]{:S(2)}) async-start(), calls=%async_computation.25 | async-start | bytes 5242880 | tf_op jit(solution)/shard_map/all_gather | solution.py:75
  763.8 394.2 %reduce-scatter.35.cloned.1.call-start = ((), (), s32[]{:S(2)}) async-start(), calls=%async_computation.26 | async-start | bytes 5242880 | tf_op jit(solution)/shard_map/reduce_scatter | solution.py:85
  1082.6 125.2 %reduce-scatter.47.cloned.1.call-start = ((), (), s32[]{:S(2)}) async-start(), calls=%async_computation.32 | async-start | bytes 3538944 | tf_op jit(solution)/shard_map/reduce_scatter | solution.py:258
  1091.9 152.3 %reduce-scatter.53.cloned.1.call-start = ((), (), s32[]{:S(2)}) async-start(), calls=%async_computation.35 | async-start | bytes 73728
  1092.7 188.1 %reduce-scatter.55.cloned.1.call-start = ((), (), s32[]{:S(2)}) async-start(), calls=%async_computation.36 | async-start | bytes 73728
  1093.5 223.8 %reduce-scatter.57.cloned.1.call-start = ((), (), s32[]{:S(2)}) async-start(), calls=%async_computation.37 | async-start | bytes 73728
  1097.0 256.9 %reduce-scatter.59.cloned.1.call-start = ((), (), s32[]{:S(2)}) async-start(), calls=%async_computation.38 | async-start | bytes 73728
  1097.9 292.4 %reduce-scatter.51.cloned.1.call-start = ((), (), s32[]{:S(2)}) async-start(), calls=%async_computation.34 | async-start | bytes 73728
  1098.9 292.8 %all-reduce.118.cloned.1.call-start = ((), (), s32[]{:S(2)}) async-start(), calls=%async_computation.39 | async-start | bytes 1048576
  1101.5 367.8 %reduce-scatter.31.cloned.1.call-start = ((), (), s32[]{:S(2)}) async-start(), calls=%async_computation.22 | async-start | bytes 5242880 | tf_op jit(solution)/shard_map/reduce_scatter | solution.py:79
  1109.8 498.1 %reduce-scatter.49.cloned.1.call-start = ((), (), s32[]{:S(2)}) async-start(), calls=%async_computation.33 | async-start | bytes 540672
  1161.1 493.5 %reduce-scatter.43.cloned.1.call-start = ((), (), s32[]{:S(2)}) async-start(), calls=%async_computation.30 | async-start | bytes 3538944 | tf_op jit(solution)/shard_map/reduce_scatter | solution.py:256
  1169.6 534.9 %reduce-scatter.45.cloned.1.call-start = ((), (), s32[]{:S(2)}) async-start(), calls=%async_computation.31 | async-start | bytes 3538944 | tf_op jit(solution)/shard_map/reduce_scatter | solution.py:257
  1178.5 568.1 %reduce-scatter.37.cloned.1.call-start = ((), (), s32[]{:S(2)}) async-start(), calls=%async_computation.27 | async-start | bytes 1769472 | tf_op jit(solution)/shard_map/reduce_scatter | solution.py:246
  1185.6 603.1 %reduce-scatter.39.cloned.1.call-start = ((), (), s32[]{:S(2)}) async-start(), calls=%async_computation.28 | async-start | bytes 1769472 | tf_op jit(solution)/shard_map/reduce_scatter | solution.py:247
  1191.9 277.4 %copy-start.124 = (f32[512]{0:T(512)S(1)}, f32[512]{0:T(512)}, u32[]{:S(2)}) copy-start(f32[512]{0:T(512)} %copy-done.122) | copy-start | bytes 6148
  1192.0 277.4 %copy-start.143 = (f32[512]{0:T(512)S(1)}, f32[512]{0:T(512)}, u32[]{:S(2)}) copy-start(f32[512]{0:T(512)} %copy-done.142) | copy-start | bytes 6148
  1192.0 638.9 %reduce-scatter.41.cloned.1.call-start = ((), (), s32[]{:S(2)}) async-start(), calls=%async_computation.29 | async-start | bytes 1769472 | tf_op jit(solution)/shard_map/reduce_scatter | solution.py:248
  1197.8 271.6 %copy-start.10 = (bf16[512,1024]{1,0:T(8,128)(2,1)S(1)}, bf16[512,1024]{1,0:T(8,128)(2,1)}, u32[]{:S(2)}) copy-start(bf16[512,1024]{1,0:T(8,128)(2,1)} %reduce-scatter.29.cloned.1.call-done) | copy-start | bytes 3145732
  1197.8 271.6 %copy-start.30 = (bf16[512,1024]{1,0:T(8,128)(2,1)S(1)}, bf16[512,1024]{1,0:T(8,128)(2,1)}, u32[]{:S(2)}) copy-start(bf16[512,1024]{1,0:T(8,128)(2,1)} %param.17) | copy-start | bytes 3145732
  (170 other events, 2450.0 us)
Sparse Core Ops, SparseCore 0:
  22.9 80.9 all-gather.11
  362.8 77.0 reduce-scatter.28
  683.2 75.2 reduce-scatter.32
  1082.7 75.2 reduce-scatter.34
  1161.2 46.5 reduce-scatter.46
  1210.7 33.5 reduce-scatter.52
  1247.3 33.5 reduce-scatter.54
  1283.8 33.5 reduce-scatter.56
  1320.3 33.5 reduce-scatter.58
  1356.7 33.5 reduce-scatter.50
  1392.6 76.7 reduce-scatter.30
  1471.5 136.3 reduce-scatter.48
  1611.8 42.7 reduce-scatter.42
  1658.4 46.0 reduce-scatter.44
  1708.2 38.3 reduce-scatter.36
  1750.3 38.3 reduce-scatter.38
  1792.4 38.3 reduce-scatter.40
Sparse Core Ops, SparseCore 1:
  365.1 25.7 all-gather.15
  444.2 81.1 all-gather.13
  527.1 23.9 all-gather.17
  553.0 25.4 all-gather.19
  580.1 80.6 all-gather.21
  763.9 81.1 all-gather.23
  1103.1 52.7 all-reduce.117
where the time goes:
time: 1850 us; the launch traced here: 1840 us
  waiting for transfers between devices  1100 us (59%)
  local copies, waits for them, and re-layouts  343 us (19%)
  matrix products  144 us (8%)
  other arithmetic  132 us (7%)
  blocking collectives  102 us (6%)
  between operations  19 us (1%)
    unnamed x31, waiting for transfers between devices  312 us
    slice x87, local copies, waits for them, and re-layouts, mixer(): lax.associative_scan(combine, (jnp.exp(log_decay), multiplier * inflow *...  174 us
    all_gather x2, waiting for transfers between devices, gather_grads(): return lax.all_gather(values, 'tensor', axis=0, tiled=True)  163 us
    reduce_scatter x2, waiting for transfers between devices, row_sums(): lax.psum_scatter(values.astype(jnp.bfloat16), 'tensor', scatter_dimension...  152 us
    reduce_scatter x2, waiting for transfers between devices, grad_sums(): lax.psum_scatter(values.astype(jnp.bfloat16), 'tensor', scatter_dimension...  124 us
    pad x88, local copies, waits for them, and re-layouts, mixer(): lax.associative_scan(combine, (jnp.exp(log_decay), multiplier * inflow *...  121 us
    all_gather x2, waiting for transfers between devices, gather_rows(): return lax.all_gather(values, 'tensor', axis=0, tiled=True)  79.1 us
    dot_general x6, matrix products, product(): return jnp.dot(left_side, right_side, preferred_element_type=jnp.float32)  54.8 us
  transfers between devices with their start and end apart: 24, of which 21 were waited for; matrix products, arithmetic and copies ran while one was open for 6% of the time, Pallas kernels for 0%

commit v1 on v0

v1 whole, which is shorter than its diff:
```python
import jax
import jax.numpy as jnp
from jax import lax
from jax.experimental import pallas as pl
from jax.experimental.pallas import tpu as pltpu
from jax.sharding import PartitionSpec as P

BLOCK = 128
CONV = 4
HALO = 16
TILE = 64
GROUP = 256
epsilon = 1e-06
f32 = jnp.float32
bf16 = jnp.bfloat16
ROOT = 0.7978845608028654
CUBIC = 0.044715


def nn(left, right):
    return lax.dot_general(left, right, (((1,), (0,)), ((), ())), preferred_element_type=f32)


def nt(left, right):
    return lax.dot_general(left, right, (((1,), (1,)), ((), ())), preferred_element_type=f32)


def tn(left, right):
    return lax.dot_general(left, right, (((0,), (0,)), ((), ())), preferred_element_type=f32)


def gelu_parts(value):
    square = value * value
    curve = jnp.tanh(ROOT * value * (1.0 + CUBIC * square))
    half = 0.5 * (1.0 + curve)
    slope = half + (0.5 * ROOT) * value * (1.0 - curve * curve) * (1.0 + 3.0 * CUBIC * square)
    return value * half, slope


def one_minus_exp(value):
    series = 1.0 + value * (1.0 / 7.0)
    for term in (6.0, 5.0, 4.0, 3.0, 2.0):
        series = 1.0 + value * (1.0 / term) * series
    return jnp.where(value > -0.25, -value * series, 1.0 - jnp.exp(value))


def scan_rows(decay_ref, drive_ref, offset, out_ref, out_offset, total_ref, length, reverse):
    width = drive_ref.shape[1]
    rows = lax.broadcasted_iota(jnp.int32, (8, width), 0)
    steps = length // 8

    def body(step, carry):
        state, product = carry
        at = (steps - 1 - step) if reverse else step
        start = pl.multiple_of(at * 8, 8)
        decay = decay_ref[pl.ds(start, 8 + 8 * (offset > 0)), :][offset : offset + 8]
        drive = drive_ref[pl.ds(start, 8), :]
        for shift in (1, 2, 4):
            if reverse:
                inside = rows < 8 - shift
                amount = 8 - shift
            else:
                inside = rows >= shift
                amount = shift
            drive = drive + decay * jnp.where(inside, pltpu.roll(drive, amount, 0), 0.0)
            decay = decay * jnp.where(inside, pltpu.roll(decay, amount, 0), 1.0)
        state = drive + decay * state
        product = decay * product
        out_ref[pl.ds(start + out_offset, 8), :] = state
        total_ref[pl.ds(start, 8), :] = product
        edge = 0 if reverse else 7
        return (
            jnp.broadcast_to(state[edge : edge + 1], (8, width)),
            jnp.broadcast_to(product[edge : edge + 1], (8, width)),
        )

    lax.fori_loop(0, steps, body, (jnp.zeros((8, width), f32), jnp.ones((8, width), f32)))


def tiles(length, body):
    def step(index, carry):
        body(pl.multiple_of(index * TILE, TILE))
        return carry

    lax.fori_loop(0, length // TILE, step, 0)


def mix_in_kernel(
    normed_ref, low_ref, high_ref, rgate_ref, igate_ref, table_ref,
    branch_ref, conv_ref, open_ref, flow_ref, local_ref, product_ref,
    conv_low, rec_buf, inp_buf, decay_buf,
):
    length = conv_ref.shape[0]
    half = low_ref.shape[0]
    branch_ref[...] = nn(normed_ref[:, :half], low_ref[...]) + nn(normed_ref[:, half:], high_ref[...])
    for part in range(GROUP // BLOCK):
        lanes = slice(part * BLOCK, (part + 1) * BLOCK)

        def convolve(start):
            window = branch_ref[pl.ds(start + HALO - 8, TILE + 8), lanes]
            result = table_ref[4:5, lanes] + table_ref[0:1, lanes] * window[8:]
            for offset in range(1, CONV):
                result = result + table_ref[offset : offset + 1, lanes] * window[8 - offset : 8 - offset + TILE]
            conv_ref[pl.ds(start, TILE), lanes] = result
            conv_low[pl.ds(start, TILE), lanes] = result.astype(bf16)

        tiles(length, convolve)
        rec_buf[:, lanes] = nn(conv_low[:, lanes], rgate_ref[part])
        inp_buf[:, lanes] = nn(conv_low[:, lanes], igate_ref[part])

        def gates(start):
            rows = pl.ds(start, TILE)
            recur_open = jax.nn.sigmoid(rec_buf[rows, lanes] + table_ref[6:7, lanes])
            inflow = jax.nn.sigmoid(inp_buf[rows, lanes] + table_ref[5:6, lanes])
            log_decay = recur_open * table_ref[7:8, lanes]
            multiplier = jnp.sqrt(one_minus_exp(2.0 * log_decay))
            open_ref[rows, lanes] = recur_open
            flow_ref[rows, lanes] = inflow
            decay_buf[rows, lanes] = jnp.exp(log_decay)
            rec_buf[rows, lanes] = multiplier * inflow * conv_ref[rows, lanes]

        tiles(length, gates)
    scan_rows(decay_buf, rec_buf, 0, local_ref, 0, product_ref, length, False)


def mix_out_kernel(
    normed_ref, low_ref, high_ref, local_ref, product_ref, enter_ref, sum_ref,
    pre_ref, states_ref, mixed_ref, total_ref,
):
    length = local_ref.shape[0]
    half = low_ref.shape[0]

    @pl.when(pl.program_id(0) == 0)
    def _():
        total_ref[...] = sum_ref[...]

    pre_ref[...] = nn(normed_ref[HALO:, :half], low_ref[:, :GROUP]) + nn(normed_ref[HALO:, half:], high_ref[:, :GROUP])
    states_ref[0:8, :] = jnp.broadcast_to(enter_ref[0:1, :], (8, GROUP))
    for part in range(GROUP // BLOCK):
        lanes = slice(part * BLOCK, (part + 1) * BLOCK)

        def mix(start):
            rows = pl.ds(start, TILE)
            states = local_ref[rows, lanes] + product_ref[rows, lanes] * enter_ref[0:1, lanes]
            states_ref[pl.ds(start + 8, TILE), lanes] = states
            gate = pre_ref[rows, lanes]
            curve = jnp.tanh(ROOT * gate * (1.0 + CUBIC * gate * gate))
            mixed_ref[rows, lanes] = (states * (gate * (0.5 * (1.0 + curve)))).astype(bf16)

        tiles(length, mix)
    total_ref[:, :half] += nt(mixed_ref[...], low_ref[:, GROUP:])
    total_ref[:, half:] += nt(mixed_ref[...], high_ref[:, GROUP:])


def mlp_kernel(
    normed_ref, normed_t_ref, cot_ref, cot_t_ref, low_ref, high_ref, sum_ref, back_ref,
    total_ref, grad_ref, low_grad_ref, high_grad_ref,
    pre, hidden, pre_low, act,
):
    length = normed_ref.shape[0]
    half = low_ref.shape[0]

    @pl.when(pl.program_id(0) == 0)
    def _():
        total_ref[...] = sum_ref[...]
        grad_ref[...] = back_ref[...]

    pre[...] = nn(normed_ref[:, :half], low_ref[:, : 2 * GROUP]) + nn(normed_ref[:, half:], high_ref[:, : 2 * GROUP])
    act[...] = nn(cot_ref[:, :half], low_ref[:, 2 * GROUP :]) + nn(cot_ref[:, half:], high_ref[:, 2 * GROUP :])
    for part in range(GROUP // BLOCK):
        lanes = slice(part * BLOCK, (part + 1) * BLOCK)
        up_lanes = slice(GROUP + part * BLOCK, GROUP + (part + 1) * BLOCK)

        def activate(start):
            rows = pl.ds(start, TILE)
            value, slope = gelu_parts(pre[rows, lanes])
            up = pre[rows, up_lanes]
            grad = act[rows, lanes]
            hidden[rows, lanes] = (value * up).astype(bf16)
            pre_low[rows, lanes] = (grad * up * slope).astype(bf16)
            pre_low[rows, up_lanes] = (grad * value).astype(bf16)

        tiles(length, activate)
    total_ref[:, :half] += nt(hidden[...], low_ref[:, 2 * GROUP :])
    total_ref[:, half:] += nt(hidden[...], high_ref[:, 2 * GROUP :])
    grad_ref[:, :half] += nt(pre_low[...], low_ref[:, : 2 * GROUP])
    grad_ref[:, half:] += nt(pre_low[...], high_ref[:, : 2 * GROUP])
    low_grad_ref[:, : 2 * GROUP] = nn(normed_t_ref[:half], pre_low[...]).astype(bf16)
    high_grad_ref[:, : 2 * GROUP] = nn(normed_t_ref[half:], pre_low[...]).astype(bf16)
    low_grad_ref[:, 2 * GROUP :] = nn(cot_t_ref[:half], hidden[...]).astype(bf16)
    high_grad_ref[:, 2 * GROUP :] = nn(cot_t_ref[half:], hidden[...]).astype(bf16)


def mix_back_kernel(
    grad_low_ref, grad_t_ref, normed_t_ref, low_ref, high_ref, pre_ref, states_ref, mixed_ref, open_ref, table_ref, sum_ref,
    total_ref, local_ref, product_ref, edge_ref, low_grad_ref, high_grad_ref,
    mixed_grad, drive, pre_low, decay_buf,
):
    length = pre_ref.shape[0]
    half = low_ref.shape[0]

    @pl.when(pl.program_id(0) == 0)
    def _():
        total_ref[...] = sum_ref[...]

    mixed_grad[...] = nn(grad_low_ref[:, :half], low_ref[:, GROUP:]) + nn(grad_low_ref[:, half:], high_ref[:, GROUP:])
    decay_buf[pl.ds(length, 8), :] = jnp.ones((8, GROUP), f32)
    for part in range(GROUP // BLOCK):
        lanes = slice(part * BLOCK, (part + 1) * BLOCK)

        def back(start):
            rows = pl.ds(start, TILE)
            value, slope = gelu_parts(pre_ref[rows, lanes])
            grad = mixed_grad[rows, lanes]
            pre_low[rows, lanes] = (grad * states_ref[pl.ds(start + 8, TILE), lanes] * slope).astype(bf16)
            drive[rows, lanes] = grad * value
            decay_buf[rows, lanes] = jnp.exp(open_ref[rows, lanes] * table_ref[7:8, lanes])

        tiles(length, back)
    scan_rows(decay_buf, drive, 1, local_ref, 0, product_ref, length, True)
    edge_ref[0:1, :] = decay_buf[0:1, :] * local_ref[0:1, :]
    edge_ref[1:2, :] = decay_buf[0:1, :] * product_ref[0:1, :]
    total_ref[:, :half] += nt(pre_low[...], low_ref[:, :GROUP])
    total_ref[:, half:] += nt(pre_low[...], high_ref[:, :GROUP])
    low_grad_ref[:, :GROUP] = nn(normed_t_ref[:half, HALO:], pre_low[...]).astype(bf16)
    high_grad_ref[:, :GROUP] = nn(normed_t_ref[half:, HALO:], pre_low[...]).astype(bf16)
    low_grad_ref[:, GROUP:] = nn(grad_t_ref[:half], mixed_ref[...]).astype(bf16)
    high_grad_ref[:, GROUP:] = nn(grad_t_ref[half:], mixed_ref[...]).astype(bf16)


def gate_back_kernel(
    local_ref, product_ref, enter_ref, states_ref, open_ref, flow_ref, conv_ref, branch_ref, rgate_ref, igate_ref, table_ref,
    conv_grad_ref, rgrad_ref, igrad_ref, sums_ref,
    rec_low, inp_low, conv_low,
):
    length = local_ref.shape[0]
    for part in range(GROUP // BLOCK):
        lanes = slice(part * BLOCK, (part + 1) * BLOCK)

        def back(index, sums):
            start = pl.multiple_of(index * TILE, TILE)
            rows = pl.ds(start, TILE)
            carried = local_ref[rows, lanes] + product_ref[rows, lanes] * enter_ref[0:1, lanes]
            recur_open = open_ref[rows, lanes]
            inflow = flow_ref[rows, lanes]
            conv_out = conv_ref[rows, lanes]
            rate = table_ref[7:8, lanes]
            log_decay = recur_open * rate
            decay = jnp.exp(log_decay)
            multiplier = jnp.sqrt(one_minus_exp(2.0 * log_decay))
            before = states_ref[pl.ds(start, TILE + 8), lanes][7 : 7 + TILE]
            weighted = carried * inflow
            decay_grad = carried * before * decay - weighted * conv_out * decay * decay / multiplier
            scaled = decay_grad * recur_open
            rec_grad = rate * scaled * (1.0 - recur_open)
            direct = weighted * multiplier
            inp_grad = direct * conv_out * (1.0 - inflow)
            rec_low[rows, lanes] = rec_grad.astype(bf16)
            inp_low[rows, lanes] = inp_grad.astype(bf16)
            conv_low[rows, lanes] = conv_out.astype(bf16)
            conv_grad_ref[rows, lanes] = direct

            def fold(value):
                return jnp.sum(value.reshape(TILE // 8, 8, BLOCK), axis=0)

            return (sums[0] + fold(rec_grad), sums[1] + fold(inp_grad), sums[2] + fold(scaled))

        zero = jnp.zeros((8, BLOCK), f32)
        sums = lax.fori_loop(0, length // TILE, back, (zero, zero, zero))
        for row, value in zip((2, 1, 3), sums):
            sums_ref[row : row + 1, lanes] = jnp.sum(value, axis=0, keepdims=True)
        rgrad_ref[part] = tn(conv_low[:, lanes], rec_low[:, lanes])
        igrad_ref[part] = tn(conv_low[:, lanes], inp_low[:, lanes])
        conv_grad_ref[:, lanes] += nt(rec_low[:, lanes], rgate_ref[part]) + nt(inp_low[:, lanes], igate_ref[part])

        def taps(index, sums):
            start = pl.multiple_of(index * TILE, TILE)
            grad = conv_grad_ref[pl.ds(start, TILE), lanes]

            def fold(value):
                return jnp.sum(value.reshape(TILE // 8, 8, BLOCK), axis=0)

            window = branch_ref[pl.ds(start + HALO - 8, TILE + 8), lanes]
            new = [sums[0] + fold(grad)]
            for offset in range(CONV):
                new.append(sums[offset + 1] + fold(grad * window[8 - offset : 8 - offset + TILE]))
            return tuple(new)

        sums = lax.fori_loop(0, length // TILE, taps, (zero,) * (CONV + 1))
        for row, value in zip((0, 4, 5, 6, 7), sums):
            sums_ref[row : row + 1, lanes] = jnp.sum(value, axis=0, keepdims=True)


def branch_back_kernel(
    conv_grad_ref, after_ref, table_ref, normed_t_ref, low_ref, high_ref, sum_ref,
    total_ref, low_grad_ref, high_grad_ref,
    padded, branch_low,
):
    length = conv_grad_ref.shape[0]
    half = low_ref.shape[0]

    @pl.when(pl.program_id(0) == 0)
    def _():
        total_ref[...] = sum_ref[...]

    padded[pl.ds(0, length), :] = conv_grad_ref[...]
    padded[pl.ds(length, 8), :] = after_ref[...]
    for part in range(GROUP // BLOCK):
        lanes = slice(part * BLOCK, (part + 1) * BLOCK)

        def back(start):
            window = padded[pl.ds(start, TILE + 8), lanes]
            result = table_ref[0:1, lanes] * window[:TILE]
            for offset in range(1, CONV):
                result = result + table_ref[offset : offset + 1, lanes] * window[offset : offset + TILE]
            branch_low[pl.ds(start, TILE), lanes] = result.astype(bf16)

        tiles(length, back)
    total_ref[:, :half] += nt(branch_low[...], low_ref[...])
    total_ref[:, half:] += nt(branch_low[...], high_ref[...])
    low_grad_ref[...] = nn(normed_t_ref[:half, HALO:], branch_low[...]).astype(bf16)
    high_grad_ref[...] = nn(normed_t_ref[half:, HALO:], branch_low[...]).astype(bf16)


def fixed(shape):
    return pl.BlockSpec(shape, lambda g: (0,) * len(shape))


def lanes_of(rows, width=GROUP):
    return pl.BlockSpec((rows, width), lambda g: (0, g))


def blocks_of():
    return pl.BlockSpec((GROUP // BLOCK, BLOCK, BLOCK), lambda g: (g, 0, 0))


def shaped(*dims, kind=f32):
    return jax.ShapeDtypeStruct(dims, kind)


PARAMS = pltpu.CompilerParams(dimension_semantics=("arbitrary",), vmem_limit_bytes=56 * 1024 * 1024)


def call(kernel, steps, in_specs, out_specs, out_shape, scratch, aliases=None):
    return pl.pallas_call(
        kernel,
        grid=(steps,),
        in_specs=in_specs,
        out_specs=out_specs,
        out_shape=out_shape,
        scratch_shapes=scratch,
        compiler_params=PARAMS,
        input_output_aliases=aliases or {},
    )


def rms_parts(values):
    scaling = lax.rsqrt(jnp.mean(values * values, axis=1, keepdims=True) + epsilon)
    return (values * scaling, scaling)


def make_per_device(dp_size, tensor_size):
    pairs = tensor_size // 2
    dp_bits = [1 << bit for bit in range(dp_size.bit_length() - 1)]
    order_one = dp_bits[1:] + dp_bits[:1]
    order_two = dp_bits[2:3] + dp_bits[1:2] + dp_bits[3:] + dp_bits[:1]
    position_of = {bit: place for place, bit in enumerate(order_one)}

    def swap_dp(values, bit):
        return lax.ppermute(values, "dp", [(at, at ^ bit) for at in range(dp_size)])

    def swap_tensor(values, bit):
        return lax.ppermute(values, "tensor", [(at, at ^ bit) for at in range(tensor_size)])

    def set_bit(index, bit):
        return (index & bit) != 0

    def relative(pieces, index, bits):
        for bit, place in bits:
            flag = set_bit(index, bit)
            pieces = [jnp.where(flag, pieces[at ^ place], piece) for at, piece in enumerate(pieces)]
        return pieces

    dp_places = [(bit, 1 << position_of[bit]) for bit in dp_bits]
    tensor_places = [(1 << bit, 1 << bit) for bit in range(tensor_size.bit_length() - 1)]

    def place_index(place):
        return sum(bit for bit, at in dp_places if place & at)

    def to_places(pieces, index):
        return relative([pieces[place_index(place)] for place in range(dp_size)], index, dp_places)

    def from_places(pieces, index):
        pieces = relative(pieces, index, dp_places)
        found = [None] * dp_size
        for place in range(dp_size):
            found[place_index(place)] = pieces[place]
        return found

    def split_lanes(values, count):
        width = values.shape[1] // count
        return [values[:, at * width : (at + 1) * width] for at in range(count)]

    def gather_dp(values, order):
        rows = values.shape[0]
        done = []
        for bit in order[:-1]:
            received = swap_dp(values, bit)
            low_place = position_of[bit]
            if all(position_of[other] < low_place for other in done):
                values = jnp.concatenate([values, received], axis=0)
            else:
                pieces = []
                for at in range(values.shape[0] // rows):
                    pieces += [values[at * rows : (at + 1) * rows], received[at * rows : (at + 1) * rows]]
                values = jnp.concatenate(pieces, axis=0)
            done.append(bit)
        return values, swap_dp(values, order[-1])

    def add(one, two):
        return (one.astype(f32) + two.astype(f32)).astype(bf16)

    def scatter_dp(own, other, order, block_rows):
        values = add(own, swap_dp(other, order[-1]))
        left = list(order[:-1])
        while left:
            bit = left.pop()
            place = position_of[bit]
            rows = values.shape[0]
            if all(position_of[o] < place for o in left):
                keep, send = values[: rows // 2], values[rows // 2 :]
            else:
                count = rows // block_rows
                take = lambda start: jnp.concatenate(
                    [values[at * block_rows : (at + 1) * block_rows] for at in range(start, count, 2)], axis=0
                )
                keep, send = take(0), take(1)
            values = add(keep, swap_dp(send, bit))
        return values

    def per_device(
        hidden_in, cotangent, norm_gains, mixer_in, branch_gate, mixer_out, input_gate, recur_gate,
        conv_kernel, conv_bias, input_bias, recur_bias, decay_param, mlp_gate, mlp_up, mlp_down,
    ):
        dp_at = lax.axis_index("dp")
        tensor_at = lax.axis_index("tensor")
        length, model = hidden_in.shape
        block_rows, chunk = mixer_in.shape
        half = model // 2
        hidden_chunk = mlp_gate.shape[1]
        sub = block_rows * BLOCK // model
        local_blocks = chunk // BLOCK
        pair_width = 2 * chunk
        groups = pair_width // GROUP
        mlp_groups = hidden_chunk // GROUP

        def rows_first(table):
            return table.transpose(1, 0, 2).reshape(-1, BLOCK)

        taps = conv_kernel.transpose(1, 2, 0).reshape(-1)
        vectors = [table.T.reshape(-1) for table in (conv_bias, input_bias, recur_bias, decay_param)]
        flat = jnp.concatenate([taps, *vectors, norm_gains.T.reshape(-1)])
        gate_rows = 2 * local_blocks * sub
        spare = (block_rows - gate_rows) * BLOCK - flat.shape[0]
        small = jnp.concatenate(
            [rows_first(recur_gate), rows_first(input_gate), jnp.pad(flat, (0, spare)).reshape(-1, BLOCK)], axis=0
        )
        first_rows = lax.ppermute(
            hidden_in[length - HALO :], "tensor", [(at, at + 1) for at in range(tensor_size - 1)]
        )

        def spread_tensor(values):
            found = [values]
            for bit, _ in tensor_places:
                received = swap_tensor(jnp.concatenate(found, axis=1), bit)
                found = found + split_lanes(received, len(found))
            return found

        small_all = jnp.concatenate(spread_tensor(small), axis=1)
        small_low, small_high = gather_dp(small_all, order_one)

        def gather_pairs(values, arrange):
            found = spread_tensor(values)
            result = []
            for pair in range(pairs):
                packed = arrange(found[2 * pair], found[2 * pair + 1])
                result.append(gather_dp(packed, order_one if pair % 2 == 0 else order_two))
            return result

        in_pairs = gather_pairs(mixer_in, lambda one, two: jnp.concatenate([one, two], axis=1))

        def interleave(one, two):
            gate = jnp.concatenate([one[:, :chunk], two[:, :chunk]], axis=1)
            out = jnp.concatenate([one[:, chunk:], two[:, chunk:]], axis=1)
            pieces = []
            for at in range(groups):
                pieces += [gate[:, at * GROUP : (at + 1) * GROUP], out[:, at * GROUP : (at + 1) * GROUP]]
            return jnp.concatenate(pieces, axis=1)

        out_pairs = gather_pairs(jnp.concatenate([branch_gate, mixer_out], axis=1), interleave)
        mlp_pieces = []
        for at in range(mlp_groups):
            mlp_pieces += [w[:, at * GROUP : (at + 1) * GROUP] for w in (mlp_gate, mlp_up, mlp_down)]
        mlp_chunks = [
            gather_dp(values, order_one if at % 2 == 0 else order_two)
            for at, values in enumerate(spread_tensor(jnp.concatenate(mlp_pieces, axis=1)))
        ]

        tables_at = jnp.concatenate([small_low, small_high], axis=0).reshape(dp_size, block_rows, tensor_size * BLOCK)
        vector_rows = tables_at[:, gate_rows:]
        natural = jnp.stack(from_places([tables_at[at] for at in range(dp_size)], dp_at), axis=0)
        gates = natural[:, :gate_rows].reshape(dp_size, 2, local_blocks, sub, tensor_size, BLOCK)
        gates = gates.transpose(1, 4, 2, 0, 3, 5).reshape(2, tensor_size * local_blocks, BLOCK, BLOCK)
        rgates, igates = gates[0], gates[1]
        flat_all = natural[:, gate_rows:].reshape(dp_size, -1, tensor_size, BLOCK).transpose(0, 2, 1, 3)
        flat_all = flat_all.reshape(dp_size, tensor_size, -1)
        count = 2 * CONV * local_blocks * sub
        table = flat_all[:, :, :count].reshape(dp_size, tensor_size, 2 * CONV, local_blocks, sub)
        table = table.transpose(2, 1, 3, 0, 4).reshape(2 * CONV, tensor_size * chunk).astype(f32)
        decay_rates = table[7]
        table = jnp.concatenate([table[:7], -8.0 * jax.nn.softplus(-decay_rates)[None]], axis=0)
        gain_rows = vector_rows[:, :, :BLOCK].reshape(dp_size, -1)[:, count : count + 2 * block_rows]
        gains = gain_rows.reshape(dp_size, 2, block_rows).transpose(1, 0, 2).reshape(2, model).astype(f32)

        def reorder(values, mover):
            return jnp.concatenate(mover(split_lanes(values, dp_size), dp_at), axis=1)

        hidden_all = reorder(jnp.concatenate([first_rows, hidden_in], axis=0), to_places).astype(f32)
        cot_low = reorder(cotangent, to_places)
        unit_all, scale_all = rms_parts(hidden_all)
        residual = hidden_all[HALO:]
        unit_one, scale_one = unit_all[HALO:], scale_all[HALO:]
        normed_one = (unit_all * gains[0]).astype(bf16)
        normed_one_t = normed_one.T
        cot_t = cot_low.T

        full = length + HALO
        fed = []
        for pair in range(pairs):
            low, high = in_pairs[pair]
            blocks = slice(2 * pair * local_blocks, 2 * (pair + 1) * local_blocks)
            lanes = slice(pair * pair_width, (pair + 1) * pair_width)
            fed.append(
                call(
                    mix_in_kernel,
                    groups,
                    [fixed((full, model)), lanes_of(half), lanes_of(half), blocks_of(), blocks_of(), lanes_of(8)],
                    [lanes_of(full)] + [lanes_of(length)] * 5,
                    [shaped(full, pair_width)] + [shaped(length, pair_width)] * 5,
                    [pltpu.VMEM((length, GROUP), bf16)] + [pltpu.VMEM((length, GROUP), f32)] * 3,
                )(normed_one, low, high, rgates[blocks], igates[blocks], table[:, lanes])
            )

        def exchange(products, ends, later):
            mine = jnp.concatenate([products, ends], axis=0)
            found = [mine]
            for other in range(1, tensor_size):
                pieces = split_lanes(swap_tensor(mine, other), tensor_size)
                found.append(jnp.concatenate([pieces[at ^ other] for at in range(tensor_size)], axis=1))
            found = relative(found, tensor_at, tensor_places)
            state = jnp.zeros_like(ends)
            turn = range(tensor_size - 1, 0, -1) if later else range(tensor_size - 1)
            for at in turn:
                use = (at > tensor_at) if later else (at < tensor_at)
                state = jnp.where(use, found[at][0:1] * state + found[at][1:2], state)
            return state

        enter = exchange(
            jnp.concatenate([one[5][length - 1 :] for one in fed], axis=1),
            jnp.concatenate([one[4][length - 1 :] for one in fed], axis=1),
            False,
        )
        middle = residual
        mixed = []
        for pair in range(pairs):
            low, high = out_pairs[pair]
            lanes = slice(pair * pair_width, (pair + 1) * pair_width)
            gate_pre, states, mixed_low, middle = call(
                mix_out_kernel,
                groups,
                [fixed((full, model)), lanes_of(half, 2 * GROUP), lanes_of(half, 2 * GROUP), lanes_of(length), lanes_of(length), lanes_of(1), fixed((length, model))],
                [lanes_of(length), lanes_of(length + 8), lanes_of(length), fixed((length, model))],
                [shaped(length, pair_width), shaped(length + 8, pair_width), shaped(length, pair_width, kind=bf16), shaped(length, model)],
                [],
            )(normed_one, low, high, fed[pair][4], fed[pair][5], enter[:, lanes], middle)
            mixed.append((gate_pre, states, mixed_low))

        unit_two, scale_two = rms_parts(middle)
        normed_two = (unit_two * gains[1]).astype(bf16)
        normed_two_t = normed_two.T

        total = middle
        normed_grad = jnp.zeros((length, model), f32)
        chunk_grads = []
        whole = fixed((length, model))
        turned = fixed((model, length))
        for low, high in mlp_chunks:
            total, normed_grad, low_grad, high_grad = call(
                mlp_kernel,
                mlp_groups,
                [whole, turned, whole, turned, lanes_of(half, 3 * GROUP), lanes_of(half, 3 * GROUP), whole, whole],
                [whole, whole, lanes_of(half, 3 * GROUP), lanes_of(half, 3 * GROUP)],
                [shaped(length, model), shaped(length, model), shaped(half, 3 * hidden_chunk, kind=bf16), shaped(half, 3 * hidden_chunk, kind=bf16)],
                [pltpu.VMEM((length, 2 * GROUP), f32), pltpu.VMEM((length, GROUP), bf16), pltpu.VMEM((length, 2 * GROUP), bf16), pltpu.VMEM((length, GROUP), f32)],
            )(normed_two, normed_two_t, cot_low, cot_t, low, high, total, normed_grad)
            chunk_grads.append((low_grad, high_grad))
        hidden_out = reorder(total.astype(bf16), from_places)

        scaled_two = normed_grad * gains[1]
        gain_two_part = jnp.sum(normed_grad * unit_two, axis=0)
        middle_grad = cot_low.astype(f32) + scale_two * (
            scaled_two - unit_two * jnp.mean(scaled_two * unit_two, axis=1, keepdims=True)
        )
        middle_low = middle_grad.astype(bf16)
        middle_low_t = middle_low.T

        def join_tensor(parts):
            for bit in reversed([bit for bit, _ in tensor_places]):
                received = split_lanes(swap_tensor(jnp.concatenate(parts[bit:], axis=1), bit), bit)
                last = bit == 1
                parts = [
                    (one.astype(f32) + two.astype(f32)) if last else add(one, two)
                    for one, two in zip(parts[:bit], received)
                ]
            return parts[0]

        mlp_sum = join_tensor(
            [
                scatter_dp(low_grad, high_grad, order_one if at % 2 == 0 else order_two, block_rows)
                for at, (low_grad, high_grad) in enumerate(chunk_grads)
            ]
        )
        mlp_grads = [
            jnp.concatenate(
                [mlp_sum[:, (3 * at + which) * GROUP : (3 * at + which + 1) * GROUP] for at in range(mlp_groups)], axis=1
            )
            for which in range(3)
        ]

        normed_grad = jnp.zeros((length, model), f32)
        backs = []
        out_grads = []
        for pair in range(pairs):
            low, high = out_pairs[pair]
            gate_pre, states, mixed_low = mixed[pair]
            lanes = slice(pair * pair_width, (pair + 1) * pair_width)
            normed_grad, local, product, edge, low_grad, high_grad = call(
                mix_back_kernel,
                groups,
                [whole, turned, fixed((model, full)), lanes_of(half, 2 * GROUP), lanes_of(half, 2 * GROUP), lanes_of(length), lanes_of(length + 8), lanes_of(length), lanes_of(length), lanes_of(8), whole],
                [whole, lanes_of(length), lanes_of(length), lanes_of(8), lanes_of(half, 2 * GROUP), lanes_of(half, 2 * GROUP)],
                [shaped(length, model), shaped(length, pair_width), shaped(length, pair_width), shaped(8, pair_width), shaped(half, 2 * pair_width, kind=bf16), shaped(half, 2 * pair_width, kind=bf16)],
                [pltpu.VMEM((length, GROUP), f32), pltpu.VMEM((length, GROUP), f32), pltpu.VMEM((length, GROUP), bf16), pltpu.VMEM((length + 8, GROUP), f32)],
            )(middle_low, middle_low_t, normed_one_t, low, high, gate_pre, states, mixed_low, fed[pair][2], table[:, lanes], normed_grad)
            backs.append((local, product, edge))
            out_grads.append((low_grad, high_grad))

        def separate(values):
            gate = [values[:, 2 * at * GROUP : (2 * at + 1) * GROUP] for at in range(groups)]
            out = [values[:, (2 * at + 1) * GROUP : (2 * at + 2) * GROUP] for at in range(groups)]
            gate, out = jnp.concatenate(gate, axis=1), jnp.concatenate(out, axis=1)
            return [jnp.concatenate([gate[:, :chunk], out[:, :chunk]], axis=1), jnp.concatenate([gate[:, chunk:], out[:, chunk:]], axis=1)]

        parts = []
        for pair, (low_grad, high_grad) in enumerate(out_grads):
            parts += separate(scatter_dp(low_grad, high_grad, order_one if pair % 2 == 0 else order_two, block_rows))
        out_sum = join_tensor(parts)

        leave = exchange(
            jnp.concatenate([one[2][1:2] for one in backs], axis=1),
            jnp.concatenate([one[2][0:1] for one in backs], axis=1),
            True,
        )
        gate_backs = []
        for pair in range(pairs):
            blocks = slice(2 * pair * local_blocks, 2 * (pair + 1) * local_blocks)
            lanes = slice(pair * pair_width, (pair + 1) * pair_width)
            branch, conv_out, recur_open, inflow = fed[pair][:4]
            local, product, _ = backs[pair]
            gate_backs.append(
                call(
                    gate_back_kernel,
                    groups,
                    [lanes_of(length), lanes_of(length), lanes_of(1), lanes_of(length + 8)] + [lanes_of(length)] * 3 + [lanes_of(full), blocks_of(), blocks_of(), lanes_of(8)],
                    [lanes_of(length), blocks_of(), blocks_of(), lanes_of(8)],
                    [shaped(length, pair_width), shaped(2 * local_blocks, BLOCK, BLOCK), shaped(2 * local_blocks, BLOCK, BLOCK), shaped(8, pair_width)],
                    [pltpu.VMEM((length, GROUP), bf16)] * 3,
                )(local, product, leave[:, lanes], mixed[pair][1], recur_open, inflow, conv_out, branch, rgates[blocks], igates[blocks], table[:, lanes])
            )
        heads = jnp.concatenate([one[0][:8] for one in gate_backs], axis=1)
        heads = jnp.concatenate(relative(split_lanes(heads, tensor_size), tensor_at, tensor_places), axis=1)
        heads = lax.ppermute(heads, "tensor", [(at + 1, at) for at in range(tensor_size - 1)])
        after = jnp.concatenate(relative(split_lanes(heads, tensor_size), tensor_at, tensor_places), axis=1)
        parts = []
        for pair in range(pairs):
            low, high = in_pairs[pair]
            lanes = slice(pair * pair_width, (pair + 1) * pair_width)
            normed_grad, low_grad, high_grad = call(
                branch_back_kernel,
                groups,
                [lanes_of(length), lanes_of(8), lanes_of(8), fixed((model, full)), lanes_of(half), lanes_of(half), whole],
                [whole, lanes_of(half), lanes_of(half)],
                [shaped(length, model), shaped(half, pair_width, kind=bf16), shaped(half, pair_width, kind=bf16)],
                [pltpu.VMEM((length + 8, GROUP), f32), pltpu.VMEM((length, GROUP), bf16)],
            )(gate_backs[pair][0], after[:, lanes], table[:, lanes], normed_one_t, low, high, normed_grad)
            parts += split_lanes(scatter_dp(low_grad, high_grad, order_one if pair % 2 == 0 else order_two, block_rows), 2)
        in_sum = join_tensor(parts)

        scaled_one = normed_grad * gains[0]
        gain_one_part = jnp.sum(normed_grad * unit_one, axis=0)
        hidden_grad = middle_grad + scale_one * (
            scaled_one - unit_one * jnp.mean(scaled_one * unit_one, axis=1, keepdims=True)
        )
        hidden_grad = reorder(hidden_grad, from_places)

        rgrads = jnp.concatenate([one[1] for one in gate_backs], axis=0)
        igrads = jnp.concatenate([one[2] for one in gate_backs], axis=0)
        gate_grads = jnp.stack([rgrads, igrads], axis=0).reshape(2, tensor_size, local_blocks, dp_size, sub, BLOCK)
        gate_grads = gate_grads.transpose(3, 0, 2, 4, 1, 5).reshape(dp_size, gate_rows, tensor_size * BLOCK)
        sums = jnp.concatenate([one[3] for one in gate_backs], axis=1)
        decay_row = sums[3:4] * (8.0 * jax.nn.sigmoid(-decay_rates))[None]
        sums = jnp.concatenate([sums[4:8], sums[0:3], decay_row], axis=0)
        sums = sums.reshape(2 * CONV, tensor_size, local_blocks, dp_size, sub).transpose(3, 1, 0, 2, 4)
        sums = sums.reshape(dp_size, tensor_size, count)
        gate_grads = jnp.stack(to_places([gate_grads[at] for at in range(dp_size)], dp_at), axis=0)
        sums = jnp.stack(to_places([sums[at] for at in range(dp_size)], dp_at), axis=0)
        gain_parts = jnp.stack([gain_one_part, gain_two_part], axis=0).reshape(2, dp_size, tensor_size, -1)
        gain_parts = jnp.stack(relative([gain_parts[:, :, at] for at in range(tensor_size)], tensor_at, tensor_places), axis=0)
        gain_parts = gain_parts.transpose(2, 0, 1, 3).reshape(dp_size, tensor_size, -1)
        flat = jnp.concatenate([sums, gain_parts], axis=2)
        flat = jnp.pad(flat, ((0, 0), (0, 0), (0, (block_rows - gate_rows) * BLOCK - flat.shape[2])))
        flat = flat.reshape(dp_size, tensor_size, -1, BLOCK).transpose(0, 2, 1, 3).reshape(dp_size, -1, tensor_size * BLOCK)
        small_grads = jnp.concatenate([gate_grads, flat], axis=1).reshape(model, tensor_size * BLOCK).astype(bf16)
        small_sum = scatter_dp(small_grads[:half], small_grads[half:], order_one, block_rows)
        small_sum = join_tensor(split_lanes(small_sum, tensor_size))
        gate_sum = small_sum[:gate_rows].reshape(2, local_blocks, sub, BLOCK).transpose(0, 2, 1, 3)
        flat_sum = small_sum[gate_rows:].reshape(-1)
        vector_sum = flat_sum[:count].reshape(2 * CONV, local_blocks, sub)
        gain_sum = flat_sum[count : count + 2 * block_rows // tensor_size].reshape(2, -1).T

        return (
            hidden_out,
            hidden_grad,
            gain_sum,
            in_sum,
            out_sum[:, :chunk],
            out_sum[:, chunk:],
            gate_sum[1],
            gate_sum[0],
            vector_sum[:CONV].transpose(2, 0, 1),
            vector_sum[4].T,
            vector_sum[5].T,
            vector_sum[6].T,
            vector_sum[7].T,
            mlp_grads[0],
            mlp_grads[1],
            mlp_grads[2],
        )

    return per_device


def solution(mesh):
    rows = P(("dp", "tensor"), None)
    matrix = P("dp", "tensor")
    gate = P("dp", "tensor", None)
    kernel = P("dp", None, "tensor")
    placed = (rows, rows, P("dp", None), matrix, matrix, matrix, gate, gate, kernel) + (matrix,) * 7
    made = (rows, rows, rows, matrix, matrix, matrix, gate, gate, kernel) + (matrix,) * 7
    return jax.shard_map(
        make_per_device(mesh.shape["dp"], mesh.shape["tensor"]),
        mesh=mesh,
        in_specs=placed,
        out_specs=made,
        check_vma=False,
    )
```

time: 1850 us -> 818 us (0.44)
  waiting for transfers between devices: 1100 us -> 317 us
  local copies, waits for them, and re-layouts: 343 us -> 137 us
  Pallas kernels: 0 us -> 191 us
  matrix products: 144 us -> 0 us
  blocking collectives: 102 us -> 0 us
  starting transfers between devices: 1.47 us -> 80.2 us
  other arithmetic: 132 us -> 83.2 us
    reduce_scatter x10 -> x0, waiting for transfers between devices: 506 us -> none  [the longest x2 152 us: row_sums(): lax.psum_scatter(values.astype(jnp.bfloat16), 'tensor', scatter_dimension...]
    ppermute x0 -> x78, waiting for transfers between devices: none -> 317 us  [the longest x54 208 us: swap_dp(): return lax.ppermute(values, 'dp', [(at, at ^ bit) for at in range(dp_size)])]
    unnamed x31 -> x0, waiting for transfers between devices: 312 us -> none
    all_gather x7 -> x0, waiting for transfers between devices: 278 us -> none  [the longest x2 163 us: gather_grads(): return lax.all_gather(values, 'tensor', axis=0, tiled=True)]
    pallas_call x0 -> x14, Pallas kernels: none -> 191 us  [the longest x4 69.2 us: per_device(): call(mlp_kernel, mlp_groups, [whole, turned, whole, turned, lanes_of(half...]
    slice x92 -> x64, local copies, waits for them, and re-layouts: 175 us -> 25.6 us  [the longest x3 3.76 us: per_device(): igates[blocks]]
    dot_general x24 -> x0, matrix products: 144 us -> none  [the longest x6 54.8 us: product(): return jnp.dot(left_side, right_side, preferred_element_type=jnp.float32)]
    pad x88 -> x0, local copies, waits for them, and re-layouts: 121 us -> none  [mixer(): lax.associative_scan(combine, (jnp.exp(log_decay), multiplier * inflow *...]
  transfers between devices with their start and end apart: 24 -> 78, of which waited for: 21 -> 28; matrix products, arithmetic and copies ran while one was open for 6% -> 25% of each run, Pallas kernels for 0% -> 24%
where the time goes in v1:
time: 818 us; the launch traced here: 811 us
  waiting for transfers between devices  317 us (39%)
  Pallas kernels  191 us (23%)
  local copies, waits for them, and re-layouts  137 us (17%)
  other arithmetic  83.2 us (10%)
  starting transfers between devices  80.2 us (10%)
    ppermute x54, waiting for transfers between devices, swap_dp(): return lax.ppermute(values, 'dp', [(at, at ^ bit) for at in range(dp_size)])  208 us
    ppermute x22, waiting for transfers between devices, swap_tensor(): lax.ppermute(values, 'tensor', [(at, at ^ bit) for at in range(tensor_siz...  109 us
    pallas_call x4, Pallas kernels, per_device(): call(mlp_kernel, mlp_groups, [whole, turned, whole, turned, lanes_of(half...  69.2 us
    unnamed x173, local copies, waits for them, and re-layouts  49.1 us
    ppermute x54, starting transfers between devices, swap_dp(): return lax.ppermute(values, 'dp', [(at, at ^ bit) for at in range(dp_size)])  38.9 us
    ppermute x22, starting transfers between devices, swap_tensor(): lax.ppermute(values, 'tensor', [(at, at ^ bit) for at in range(tensor_siz...  37.4 us
    pallas_call x2, Pallas kernels, per_device(): call(mix_back_kernel, groups, [whole, turned, fixed((model, full)), lanes...  37.1 us
    pallas_call x2, Pallas kernels, per_device(): call(mix_in_kernel, groups, [fixed((full, model)), lanes_of(half), lanes_...  28.7 us
  transfers between devices with their start and end apart: 78, of which 28 were waited for; matrix products, arithmetic and copies ran while one was open for 25% of the time, Pallas kernels for 24%

profile of v1, /device:TPU:0, one launch (start us, length us, event | category | flops | bytes accessed | tf_op | source)
XLA Modules:
  0.0 811.3 jit_solution(17541178725522378660)
XLA Ops:
  63.7 8.2 %collective-permute-done.12 = bf16[128,768]{1,0:T(8,128)(2,1)S(1)} collective-permute-done((bf16[128,768]{1,0:T(8,128)(2,1)}, bf16[128,768]{1,0:T(8,128)(2,1)S(1)}, u32[]{:S(2)}, u32[]{:S(2)}) %collective-permute-start.12) | collective-permute-done | bytes 196640 | tf_op jit(solution)/shard_map/ppermute | solution.py:373
  80.0 6.9 collective-permute-done.22
  97.8 19.6 %collective-permute-done.8 = bf16[128,1536]{1,0:T(8,128)(2,1)S(1)} collective-permute-done((bf16[128,1536]{1,0:T(8,128)(2,1)S(1)}, bf16[128,1536]{1,0:T(8,128)(2,1)S(1)}, u32[]{:S(2)}, u32[]{:S(2)}) %collective-permute-start.8) | collective-permute-done | bytes 393248 | tf_op jit(solution)/shard_map/ppermute | solution.py:370
  140.6 8.9 %collective-permute-done.33 = bf16[128,2304]{1,0:T(8,128)(2,1)} collective-permute-done((bf16[128,2304]{1,0:T(8,128)(2,1)}, bf16[128,2304]{1,0:T(8,128)(2,1)}, u32[]{:S(2)}, u32[]{:S(2)}) %collective-permute-start.33) | collective-permute-done | bytes 589856 | tf_op jit(solution)/shard_map/ppermute | solution.py:370
  156.9 14.2 %shard_map.280 = (f32[528,768]{1,0:T(8,128)}, f32[512,768]{1,0:T(8,128)}, f32[512,768]{1,0:T(8,128)}, f32[512,768]{1,0:T(8,128)}, f32[512,768]{1,0:T(8,128)}, /*index=5*/f32[512,768]{1,0:T(8,128)}) custom-call(bf16[528,1024]{1,0:T(8,128)(2,1)} %copy.353.normed_ref, bf16[512,768]{1,0:T(8,128)(2,1)} %copy-done.8, ...), custom_call_target="tpu_custom_call" | custom-call | tf_op jit(solution)/shard_map/pallas_call | solution.py:544
  173.2 14.5 %shard_map.279 = (f32[528,768]{1,0:T(8,128)}, f32[512,768]{1,0:T(8,128)}, f32[512,768]{1,0:T(8,128)}, f32[512,768]{1,0:T(8,128)}, f32[512,768]{1,0:T(8,128)}, /*index=5*/f32[512,768]{1,0:T(8,128)}) custom-call(bf16[528,1024]{1,0:T(8,128)(2,1)} %copy.353.normed_ref, bf16[512,768]{1,0:T(8,128)(2,1)} %pad_maximum_fusion.15.low_ref, ...), custom_call_target="tpu_custom_call" | custom-call | tf_op jit(solution)/shard_map/pallas_call | solution.py:544
  190.6 11.7 %collective-permute-done.21 = f32[2,1536]{1,0:T(2,128)S(1)} collective-permute-done((f32[2,1536]{1,0:T(2,128)S(1)}, f32[2,1536]{1,0:T(2,128)S(1)}, u32[]{:S(2)}, u32[]{:S(2)}) %collective-permute-start.21) | collective-permute-done | bytes 12320 | tf_op jit(solution)/shard_map/ppermute | solution.py:373
  217.0 10.4 %collective-permute-done.30 = bf16[128,2304]{1,0:T(8,128)(2,1)S(1)} collective-permute-done((bf16[128,2304]{1,0:T(8,128)(2,1)S(1)}, bf16[128,2304]{1,0:T(8,128)(2,1)S(1)}, u32[]{:S(2)}, u32[]{:S(2)}) %collective-permute-start.30) | collective-permute-done | bytes 589856 | tf_op jit(solution)/shard_map/ppermute | solution.py:370
  233.0 23.4 %collective-permute-done.31 = bf16[256,2304]{1,0:T(8,128)(2,1)S(1)} collective-permute-done((bf16[256,2304]{1,0:T(8,128)(2,1)S(1)}, bf16[256,2304]{1,0:T(8,128)(2,1)S(1)}, u32[]{:S(2)}, u32[]{:S(2)}) %collective-permute-start.31) | collective-permute-done | bytes 1179680 | tf_op jit(solution)/shard_map/ppermute | solution.py:370
  261.4 10.0 %shard_map.281 = (f32[512,768]{1,0:T(8,128)}, f32[520,768]{1,0:T(8,128)}, bf16[512,768]{1,0:T(8,128)(2,1)}, f32[512,1024]{1,0:T(8,128)}) custom-call(bf16[528,1024]{1,0:T(8,128)(2,1)} %copy.353.normed_ref, bf16[512,1536]{1,0:T(8,128)(2,1)} %copy-done.5, bf16[512,1536]{1,0:T(8,128)(2,1)} %copy-done.9, f32[512,768]{1,0:T(8,128)} %get-tuple-element.81.local_ref, ...), custom_call_target="tpu_custom_call" | custom-call | tf_op jit(solution)/shard_map/pallas_call | solution.py:578
  272.5 10.0 %shard_map.282 = (f32[512,768]{1,0:T(8,128)}, f32[520,768]{1,0:T(8,128)}, bf16[512,768]{1,0:T(8,128)(2,1)}, f32[512,1024]{1,0:T(8,128)}) custom-call(bf16[528,1024]{1,0:T(8,128)(2,1)} %copy.353.normed_ref, bf16[512,1536]{1,0:T(8,128)(2,1)} %copy-done.6, bf16[512,1536]{1,0:T(8,128)(2,1)} %copy-done.10, f32[512,768]{1,0:T(8,128)} %get-tuple-element.78.local_ref, ...), custom_call_target="tpu_custom_call" | custom-call | tf_op jit(solution)/shard_map/pallas_call | solution.py:578
  290.6 17.1 %shard_map.283 = (f32[512,1024]{1,0:T(8,128)}, f32[512,1024]{1,0:T(8,128)}, bf16[512,2304]{1,0:T(8,128)(2,1)}, bf16[512,2304]{1,0:T(8,128)(2,1)}) custom-call(bf16[512,1024]{1,0:T(8,128)(2,1)} %copy.369.normed_ref, bf16[1024,512]{1,0:T(8,128)(2,1)} %fusion.73.normed_t_ref, bf16[512,1024]{1,0:T(8,128)(2,1)} %copy.370.cot_ref, bf16[1024,512]{1,0:T(8,128)(2,1)} %bitcast.145, ...), custom_call_target="tpu_custom_call" | custom-call | tf_op jit(solution)/shard_map/pallas_call | solution.py:598
  307.8 17.6 %shard_map.284 = (f32[512,1024]{1,0:T(8,128)}, f32[512,1024]{1,0:T(8,128)}, bf16[512,2304]{1,0:T(8,128)(2,1)}, bf16[512,2304]{1,0:T(8,128)(2,1)}) custom-call(bf16[512,1024]{1,0:T(8,128)(2,1)} %copy.369.normed_ref, bf16[1024,512]{1,0:T(8,128)(2,1)} %fusion.73.normed_t_ref, bf16[512,1024]{1,0:T(8,128)(2,1)} %copy.370.cot_ref, bf16[1024,512]{1,0:T(8,128)(2,1)} %bitcast.146, ...), custom_call_target="tpu_custom_call" | custom-call | tf_op jit(solution)/shard_map/pallas_call | solution.py:598
  325.9 17.3 %shard_map.285 = (f32[512,1024]{1,0:T(8,128)}, f32[512,1024]{1,0:T(8,128)}, bf16[512,2304]{1,0:T(8,128)(2,1)}, bf16[512,2304]{1,0:T(8,128)(2,1)}) custom-call(bf16[512,1024]{1,0:T(8,128)(2,1)} %copy.369.normed_ref, bf16[1024,512]{1,0:T(8,128)(2,1)} %fusion.73.normed_t_ref, bf16[512,1024]{1,0:T(8,128)(2,1)} %copy.370.cot_ref, bf16[1024,512]{1,0:T(8,128)(2,1)} %bitcast.147, ...), custom_call_target="tpu_custom_call" | custom-call | tf_op jit(solution)/shard_map/pallas_call | solution.py:598
  343.1 17.2 %shard_map.286 = (f32[512,1024]{1,0:T(8,128)}, f32[512,1024]{1,0:T(8,128)}, bf16[512,2304]{1,0:T(8,128)(2,1)}, bf16[512,2304]{1,0:T(8,128)(2,1)}) custom-call(bf16[512,1024]{1,0:T(8,128)(2,1)} %copy.369.normed_ref, bf16[1024,512]{1,0:T(8,128)(2,1)} %fusion.73.normed_t_ref, bf16[512,1024]{1,0:T(8,128)(2,1)} %copy.370.cot_ref, bf16[1024,512]{1,0:T(8,128)(2,1)} %bitcast.148, ...), custom_call_target="tpu_custom_call" | custom-call | tf_op jit(solution)/shard_map/pallas_call | solution.py:598
  369.7 18.6 %shard_map.287 = (f32[512,1024]{1,0:T(8,128)}, f32[512,768]{1,0:T(8,128)}, f32[512,768]{1,0:T(8,128)}, f32[8,768]{1,0:T(8,128)}, bf16[512,1536]{1,0:T(8,128)(2,1)}, /*index=5*/bf16[512,1536]{1,0:T(8,128)(2,1)}) custom-call(bf16[512,1024]{1,0:T(8,128)(2,1)} %copy.374.grad_low_ref, bf16[1024,512]{1,0:T(8,128)(2,1)} %bitcast.153, bf16[1024,528]{1,0:T(8,128)(2,1)} %bitcast.149, ...), custom_call_target="tpu_custom_call" | custom-call | tf_op jit(solution)/shard_map/pallas_call | solution.py:647
  388.3 18.5 %shard_map.288 = (f32[512,1024]{1,0:T(8,128)}, f32[512,768]{1,0:T(8,128)}, f32[512,768]{1,0:T(8,128)}, f32[8,768]{1,0:T(8,128)}, bf16[512,1536]{1,0:T(8,128)(2,1)}, /*index=5*/bf16[512,1536]{1,0:T(8,128)(2,1)}) custom-call(bf16[512,1024]{1,0:T(8,128)(2,1)} %copy.374.grad_low_ref, bf16[1024,512]{1,0:T(8,128)(2,1)} %bitcast.154, bf16[1024,528]{1,0:T(8,128)(2,1)} %bitcast.150, ...), custom_call_target="tpu_custom_call" | custom-call | tf_op jit(solution)/shard_map/pallas_call | solution.py:647
  422.9 10.5 %shard_map.290 = (f32[512,768]{1,0:T(8,128)}, f32[6,128,128]{2,1,0:T(8,128)}, f32[6,128,128]{2,1,0:T(8,128)}, f32[8,768]{1,0:T(8,128)}) custom-call(f32[512,768]{1,0:T(8,128)} %get-tuple-element.109.local_ref, f32[512,768]{1,0:T(8,128)} %get-tuple-element.110.product_ref, f32[1,768]{1,0:T(1,128)} %get-tuple-element.481.enter_ref, ...), custom_call_target="tpu_custom_call" | custom-call | tf_op jit(solution)/shard_map/pallas_call | solution.py:681
  434.1 10.4 %shard_map.289 = (f32[512,768]{1,0:T(8,128)}, f32[6,128,128]{2,1,0:T(8,128)}, f32[6,128,128]{2,1,0:T(8,128)}, f32[8,768]{1,0:T(8,128)}) custom-call(f32[512,768]{1,0:T(8,128)} %get-tuple-element.101.local_ref, f32[512,768]{1,0:T(8,128)} %get-tuple-element.102.product_ref, f32[1,768]{1,0:T(1,128)} %get-tuple-element.482.enter_ref, ...), custom_call_target="tpu_custom_call" | custom-call | tf_op jit(solution)/shard_map/pallas_call | solution.py:681
  493.4 7.8 shard_map.291
  501.2 7.6 shard_map.292
  532.4 7.8 collective-permute-done.44
  579.5 5.5 collective-permute-done.53
  592.6 5.2 collective-permute-done.54
  597.9 16.0 %collective-permute-done.65 = bf16[256,2304]{1,0:T(8,128)(2,1)S(1)} collective-permute-done((bf16[256,2304]{1,0:T(8,128)(2,1)S(1)}, bf16[256,2304]{1,0:T(8,128)(2,1)S(1)}, u32[]{:S(2)}, u32[]{:S(2)}) %collective-permute-start.65) | collective-permute-done | bytes 1179680 | tf_op jit(solution)/shard_map/ppermute | solution.py:370
  624.3 8.0 collective-permute-done.60
  635.1 37.0 %collective-permute-done.61 = bf16[128,1536]{1,0:T(8,128)(2,1)S(1)} collective-permute-done((bf16[128,1536]{1,0:T(8,128)(2,1)S(1)}, bf16[128,1536]{1,0:T(8,128)(2,1)S(1)}, u32[]{:S(2)}, u32[]{:S(2)}) %collective-permute-start.61) | collective-permute-done | bytes 393248 | tf_op jit(solution)/shard_map/ppermute | solution.py:370
  674.7 26.3 %collective-permute-done.71 = bf16[256,2304]{1,0:T(8,128)(2,1)S(1)} collective-permute-done((bf16[256,2304]{1,0:T(8,128)(2,1)S(1)}, bf16[256,2304]{1,0:T(8,128)(2,1)S(1)}, u32[]{:S(2)}, u32[]{:S(2)}) %collective-permute-start.71) | collective-permute-done | bytes 1179680 | tf_op jit(solution)/shard_map/ppermute | solution.py:370
  702.1 14.1 %collective-permute-done.69 = bf16[128,2304]{1,0:T(8,128)(2,1)S(1)} collective-permute-done((bf16[128,2304]{1,0:T(8,128)(2,1)S(1)}, bf16[128,2304]{1,0:T(8,128)(2,1)S(1)}, u32[]{:S(2)}, u32[]{:S(2)}) %collective-permute-start.69) | collective-permute-done | bytes 589856 | tf_op jit(solution)/shard_map/ppermute | solution.py:370
  718.1 8.0 collective-permute-done.72
  729.6 61.2 %collective-permute-done.62 = bf16[128,1536]{1,0:T(8,128)(2,1)S(1)} collective-permute-done((bf16[128,1536]{1,0:T(8,128)(2,1)S(1)}, bf16[128,1536]{1,0:T(8,128)(2,1)S(1)}, u32[]{:S(2)}, u32[]{:S(2)}) %collective-permute-start.62) | collective-permute-done | bytes 393248 | tf_op jit(solution)/shard_map/ppermute | solution.py:373
  799.5 9.4 %collective-permute-done.77 = bf16[128,2304]{1,0:T(8,128)(2,1)S(1)} collective-permute-done((bf16[128,2304]{1,0:T(8,128)(2,1)S(1)}, bf16[128,2304]{1,0:T(8,128)(2,1)S(1)}, u32[]{:S(2)}, u32[]{:S(2)}) %collective-permute-start.77) | collective-permute-done | bytes 589856 | tf_op jit(solution)/shard_map/ppermute | solution.py:373
  (594 shorter events, 329.6 us)
Async XLA Ops:
  13.4 36.4 %collective-permute-start.11 = (bf16[128,384]{1,0:T(8,128)(2,1)}, bf16[128,384]{1,0:T(8,128)(2,1)}, u32[]{:S(2)}, u32[]{:S(2)}) collective-permute-start(bf16[128,384]{1,0:T(8,128)(2,1)} %param.19), channel_id=1, source_target_pairs={{0,1},{1,0},{2,3},{3,2},{4,5},{5,4},{6,7},{7,6},{8,9},{9,8},{10,11... | collective-permute-start | bytes 294920 | tf_op jit(solution)/shard_map/ppermute | solution.py:373
  17.5 36.3 %collective-permute-start.6 = (bf16[128,768]{1,0:T(8,128)(2,1)}, bf16[128,768]{1,0:T(8,128)(2,1)}, u32[]{:S(2)}, u32[]{:S(2)}) collective-permute-start(bf16[128,768]{1,0:T(8,128)(2,1)} %pad_maximum_fusion.33), channel_id=1, source_target_pairs={{0,1},{1,0},{2,3},{3,2},{4,5},{5,4},{6,7},{7,6},{8,9},{9,8},{10,11... | collective-permute-start | bytes 589832 | tf_op jit(solution)/shard_map/ppermute | solution.py:373
  30.3 58.1 %collective-permute-start.36 = (bf16[128,2304]{1,0:T(8,128)(2,1)}, bf16[128,2304]{1,0:T(8,128)(2,1)}, u32[]{:S(2)}, u32[]{:S(2)}) collective-permute-start(bf16[128,2304]{1,0:T(8,128)(2,1)} %get-tuple-element.425), channel_id=1, source_target_pairs={{0,8},{4,12},{8,0},{12,4},{16,24},{20,28},{24,16},{28,20},{1,9},{5... | collective-permute-start | bytes 1769480 | tf_op jit(solution)/shard_map/ppermute | solution.py:370
  79.8 38.7 %collective-permute-start.5 = (bf16[512,512]{1,0:T(8,128)(2,1)S(1)}, bf16[512,512]{1,0:T(8,128)(2,1)S(1)}, u32[]{:S(2)}, u32[]{:S(2)}) collective-permute-start(bf16[512,512]{1,0:T(8,128)(2,1)S(1)} %pad_maximum_fusion.22), channel_id=1, source_target_pairs={{0,4},{4,0},{8,12},{12,8},{16,20},{20,16},{24,28},{28,24},{1,5},{5... | collective-permute-start | bytes 1572872 | tf_op jit(solution)/shard_map/ppermute | solution.py:370
  88.4 100.8 %collective-permute-start.23 = (bf16[256,1536]{1,0:T(8,128)(2,1)}, bf16[256,1536]{1,0:T(8,128)(2,1)}, u32[]{:S(2)}, u32[]{:S(2)}) collective-permute-start(bf16[256,1536]{1,0:T(8,128)(2,1)} %pad_maximum_fusion.17), channel_id=1, source_target_pairs={{0,16},{4,20},{8,24},{12,28},{16,0},{20,4},{24,8},{28,12},{1,17},{... | collective-permute-start | bytes 2359304 | tf_op jit(solution)/shard_map/ppermute | solution.py:370
  94.6 119.0 %collective-permute-start.37 = (bf16[256,2304]{1,0:T(8,128)(2,1)}, bf16[256,2304]{1,0:T(8,128)(2,1)}, u32[]{:S(2)}, u32[]{:S(2)}) collective-permute-start(bf16[256,2304]{1,0:T(8,128)(2,1)} %pad_maximum_fusion.9), channel_id=1, source_target_pairs={{0,16},{4,20},{8,24},{12,28},{16,0},{20,4},{24,8},{28,12},{1,17},{... | collective-permute-start | bytes 3538952 | tf_op jit(solution)/shard_map/ppermute | solution.py:370
  95.7 53.8 %collective-permute-start.33 = (bf16[128,2304]{1,0:T(8,128)(2,1)}, bf16[128,2304]{1,0:T(8,128)(2,1)}, u32[]{:S(2)}, u32[]{:S(2)}) collective-permute-start(bf16[128,2304]{1,0:T(8,128)(2,1)} %collective-permute-done.25), channel_id=1, source_target_pairs={{0,16},{4,20},{8,24},{12,28},{16,0},{20,4},{24,8},{28,12},{1,17},{... | collective-permute-start | bytes 1769480 | tf_op jit(solution)/shard_map/ppermute | solution.py:370
  117.5 37.9 %collective-permute-start.18 = (bf16[512,768]{1,0:T(8,128)(2,1)S(1)}, bf16[512,768]{1,0:T(8,128)(2,1)}, u32[]{:S(2)}, u32[]{:S(2)}) collective-permute-start(bf16[512,768]{1,0:T(8,128)(2,1)S(1)} %pad_maximum_fusion.16.low_ref), channel_id=1, source_target_pairs={{0,4},{4,0},{8,12},{12,8},{16,20},{20,16},{24,28},{28,24},{1,5},{5... | collective-permute-start | bytes 2359304 | tf_op jit(solution)/shard_map/ppermute | solution.py:370
  118.5 54.2 %collective-permute-start.15 = (bf16[512,768]{1,0:T(8,128)(2,1)}, bf16[512,768]{1,0:T(8,128)(2,1)}, u32[]{:S(2)}, u32[]{:S(2)}) collective-permute-start(bf16[512,768]{1,0:T(8,128)(2,1)} %pad_maximum_fusion.15.low_ref), channel_id=1, source_target_pairs={{0,4},{4,0},{8,12},{12,8},{16,20},{20,16},{24,28},{28,24},{1,5},{5... | collective-permute-start | bytes 2359304 | tf_op jit(solution)/shard_map/ppermute | solution.py:370
  149.5 62.0 %collective-permute-start.26 = (bf16[128,4608]{1,0:T(8,128)(2,1)}, bf16[128,4608]{1,0:T(8,128)(2,1)S(1)}, u32[]{:S(2)}, u32[]{:S(2)}) collective-permute-start(bf16[128,4608]{1,0:T(8,128)(2,1)} %copy-done.55), channel_id=1, source_target_pairs={{0,2},{1,3},{2,0},{3,1},{4,6},{5,7},{6,4},{7,5},{8,10},{9,11},{10,... | collective-permute-start | bytes 3538952 | tf_op jit(solution)/shard_map/ppermute | solution.py:373
  155.4 57.7 %collective-permute-start.9 = (bf16[256,1536]{1,0:T(8,128)(2,1)}, bf16[256,1536]{1,0:T(8,128)(2,1)S(1)}, u32[]{:S(2)}, u32[]{:S(2)}) collective-permute-start(bf16[256,1536]{1,0:T(8,128)(2,1)} %pad_maximum_fusion.14), channel_id=1, source_target_pairs={{0,8},{4,12},{8,0},{12,4},{16,24},{20,28},{24,16},{28,20},{1,9},{5... | collective-permute-start | bytes 2359304 | tf_op jit(solution)/shard_map/ppermute | solution.py:370
  172.7 56.8 %collective-permute-start.34 = (bf16[256,2304]{1,0:T(8,128)(2,1)}, bf16[256,2304]{1,0:T(8,128)(2,1)S(1)}, u32[]{:S(2)}, u32[]{:S(2)}) collective-permute-start(bf16[256,2304]{1,0:T(8,128)(2,1)} %pad_maximum_fusion.8), channel_id=1, source_target_pairs={{0,8},{4,12},{8,0},{12,4},{16,24},{20,28},{24,16},{28,20},{1,9},{5... | collective-permute-start | bytes 3538952 | tf_op jit(solution)/shard_map/ppermute | solution.py:370
  211.5 48.7 %collective-permute-start.24 = (bf16[512,1536]{1,0:T(8,128)(2,1)S(1)}, bf16[512,1536]{1,0:T(8,128)(2,1)S(1)}, u32[]{:S(2)}, u32[]{:S(2)}) collective-permute-start(bf16[512,1536]{1,0:T(8,128)(2,1)S(1)} %pad_maximum_fusion.5.low_ref), channel_id=1, source_target_pairs={{0,4},{4,0},{8,12},{12,8},{16,20},{20,16},{24,28},{28,24},{1,5},{5... | collective-permute-start | bytes 4718600 | tf_op jit(solution)/shard_map/ppermute | solution.py:370
  213.3 58.1 %collective-permute-start.10 = (bf16[512,1536]{1,0:T(8,128)(2,1)S(1)}, bf16[512,1536]{1,0:T(8,128)(2,1)S(1)}, u32[]{:S(2)}, u32[]{:S(2)}) collective-permute-start(bf16[512,1536]{1,0:T(8,128)(2,1)S(1)} %pad_maximum_fusion.4.low_ref), channel_id=1, source_target_pairs={{0,4},{4,0},{8,12},{12,8},{16,20},{20,16},{24,28},{28,24},{1,5},{5... | collective-permute-start | bytes 4718600 | tf_op jit(solution)/shard_map/ppermute | solution.py:370
  227.3 61.7 %collective-permute-start.38 = (bf16[512,2304]{1,0:T(8,128)(2,1)}, bf16[512,2304]{1,0:T(8,128)(2,1)}, u32[]{:S(2)}, u32[]{:S(2)}) collective-permute-start(bf16[512,2304]{1,0:T(8,128)(2,1)} %pad_maximum_fusion.3.low_ref), channel_id=1, source_target_pairs={{0,4},{4,0},{8,12},{12,8},{16,20},{20,16},{24,28},{28,24},{1,5},{5... | collective-permute-start | bytes 7077896 | tf_op jit(solution)/shard_map/ppermute | solution.py:370
  256.4 51.4 %collective-permute-start.35 = (bf16[512,2304]{1,0:T(8,128)(2,1)}, bf16[512,2304]{1,0:T(8,128)(2,1)}, u32[]{:S(2)}, u32[]{:S(2)}) collective-permute-start(bf16[512,2304]{1,0:T(8,128)(2,1)} %pad_maximum_fusion.2.low_ref), channel_id=1, source_target_pairs={{0,4},{4,0},{8,12},{12,8},{16,20},{20,16},{24,28},{28,24},{1,5},{5... | collective-permute-start | bytes 7077896 | tf_op jit(solution)/shard_map/ppermute | solution.py:370
  258.0 67.8 %collective-permute-start.32 = (bf16[512,2304]{1,0:T(8,128)(2,1)}, bf16[512,2304]{1,0:T(8,128)(2,1)}, u32[]{:S(2)}, u32[]{:S(2)}) collective-permute-start(bf16[512,2304]{1,0:T(8,128)(2,1)} %pad_maximum_fusion.1.low_ref), channel_id=1, source_target_pairs={{0,4},{4,0},{8,12},{12,8},{16,20},{20,16},{24,28},{28,24},{1,5},{5... | collective-permute-start | bytes 7077896 | tf_op jit(solution)/shard_map/ppermute | solution.py:370
  260.2 82.9 %collective-permute-start.29 = (bf16[512,2304]{1,0:T(8,128)(2,1)}, bf16[512,2304]{1,0:T(8,128)(2,1)}, u32[]{:S(2)}, u32[]{:S(2)}) collective-permute-start(bf16[512,2304]{1,0:T(8,128)(2,1)} %pad_maximum_fusion.low_ref), channel_id=1, source_target_pairs={{0,4},{4,0},{8,12},{12,8},{16,20},{20,16},{24,28},{28,24},{1,5},{5... | collective-permute-start | bytes 7077896 | tf_op jit(solution)/shard_map/ppermute | solution.py:370
  307.8 219.7 %collective-permute-start.64 = (bf16[512,2304]{1,0:T(8,128)(2,1)}, bf16[512,2304]{1,0:T(8,128)(2,1)}, u32[]{:S(2)}, u32[]{:S(2)}) collective-permute-start(bf16[512,2304]{1,0:T(8,128)(2,1)} %get-tuple-element.133), channel_id=1, source_target_pairs={{0,4},{4,0},{8,12},{12,8},{16,20},{20,16},{24,28},{28,24},{1,5},{5... | collective-permute-start | bytes 7077896 | tf_op jit(solution)/shard_map/ppermute | solution.py:370
  325.4 238.3 %collective-permute-start.74 = (bf16[512,2304]{1,0:T(8,128)(2,1)}, bf16[512,2304]{1,0:T(8,128)(2,1)}, u32[]{:S(2)}, u32[]{:S(2)}) collective-permute-start(bf16[512,2304]{1,0:T(8,128)(2,1)} %get-tuple-element.139), channel_id=1, source_target_pairs={{0,4},{4,0},{8,12},{12,8},{16,20},{20,16},{24,28},{28,24},{1,5},{5... | collective-permute-start | bytes 7077896 | tf_op jit(solution)/shard_map/ppermute | solution.py:370
  421.6 194.4 %collective-permute-start.67 = (bf16[512,2304]{1,0:T(8,128)(2,1)}, bf16[512,2304]{1,0:T(8,128)(2,1)}, u32[]{:S(2)}, u32[]{:S(2)}) collective-permute-start(bf16[512,2304]{1,0:T(8,128)(2,1)} %get-tuple-element.135), channel_id=1, source_target_pairs={{0,4},{4,0},{8,12},{12,8},{16,20},{20,16},{24,28},{28,24},{1,5},{5... | collective-permute-start | bytes 7077896 | tf_op jit(solution)/shard_map/ppermute | solution.py:370
  421.7 198.8 %collective-permute-start.70 = (bf16[512,2304]{1,0:T(8,128)(2,1)}, bf16[512,2304]{1,0:T(8,128)(2,1)}, u32[]{:S(2)}, u32[]{:S(2)}) collective-permute-start(bf16[512,2304]{1,0:T(8,128)(2,1)} %get-tuple-element.137), channel_id=1, source_target_pairs={{0,4},{4,0},{8,12},{12,8},{16,20},{20,16},{24,28},{28,24},{1,5},{5... | collective-permute-start | bytes 7077896 | tf_op jit(solution)/shard_map/ppermute | solution.py:370
  446.7 45.3 %collective-permute-start.42 = (f32[8,1536]{1,0:T(8,128)}, f32[8,1536]{1,0:T(8,128)}, u32[]{:S(2)}, u32[]{:S(2)}) collective-permute-start(f32[8,1536]{1,0:T(8,128)} %pad_maximum_fusion.41), channel_id=1, source_target_pairs={{1,0},{2,1},{3,2},{5,4},{6,5},{7,6},{9,8},{10,9},{11,10},{13,12},{... | collective-permute-start | bytes 147464 | tf_op jit(solution)/shard_map/ppermute | solution.py:692
  540.2 46.0 %collective-permute-start.56 = (bf16[512,1536]{1,0:T(8,128)(2,1)}, bf16[512,1536]{1,0:T(8,128)(2,1)}, u32[]{:S(2)}, u32[]{:S(2)}) collective-permute-start(bf16[512,1536]{1,0:T(8,128)(2,1)} %get-tuple-element.129), channel_id=1, source_target_pairs={{0,4},{4,0},{8,12},{12,8},{16,20},{20,16},{24,28},{28,24},{1,5},{5... | collective-permute-start | bytes 4718600 | tf_op jit(solution)/shard_map/ppermute | solution.py:370
  614.2 178.9 %collective-permute-start.55 = (bf16[128,384]{1,0:T(8,128)(2,1)S(1)}, bf16[128,384]{1,0:T(8,128)(2,1)S(1)}, u32[]{:S(2)}, u32[]{:S(2)}) collective-permute-start(bf16[128,384]{1,0:T(8,128)(2,1)S(1)} %add_convert_fusion.30), channel_id=1, source_target_pairs={{0,1},{1,0},{2,3},{3,2},{4,5},{5,4},{6,7},{7,6},{8,9},{9,8},{10,11... | collective-permute-start | bytes 294920 | tf_op jit(solution)/shard_map/ppermute | solution.py:373
  616.1 183.4 %collective-permute-start.66 = (bf16[128,2304]{1,0:T(8,128)(2,1)S(1)}, bf16[128,2304]{1,0:T(8,128)(2,1)S(1)}, u32[]{:S(2)}, u32[]{:S(2)}) collective-permute-start(bf16[128,2304]{1,0:T(8,128)(2,1)S(1)} %slice.1417), channel_id=1, source_target_pairs={{0,8},{4,12},{8,0},{12,4},{16,24},{20,28},{24,16},{28,20},{1,9},{5... | collective-permute-start | bytes 1769480 | tf_op jit(solution)/shard_map/ppermute | solution.py:370
  620.5 170.7 %collective-permute-start.76 = (bf16[128,2304]{1,0:T(8,128)(2,1)S(1)}, bf16[128,2304]{1,0:T(8,128)(2,1)S(1)}, u32[]{:S(2)}, u32[]{:S(2)}) collective-permute-start(bf16[128,2304]{1,0:T(8,128)(2,1)S(1)} %slice.1434), channel_id=1, source_target_pairs={{0,16},{4,20},{8,24},{12,28},{16,0},{20,4},{24,8},{28,12},{1,17},{... | collective-permute-start | bytes 1769480 | tf_op jit(solution)/shard_map/ppermute | solution.py:370
  632.3 40.8 %collective-permute-start.68 = (bf16[256,2304]{1,0:T(8,128)(2,1)S(1)}, bf16[256,2304]{1,0:T(8,128)(2,1)S(1)}, u32[]{:S(2)}, u32[]{:S(2)}) collective-permute-start(bf16[256,2304]{1,0:T(8,128)(2,1)S(1)} %slice.1419), channel_id=1, source_target_pairs={{0,16},{4,20},{8,24},{12,28},{16,0},{20,4},{24,8},{28,12},{1,17},{... | collective-permute-start | bytes 3538952 | tf_op jit(solution)/shard_map/ppermute | solution.py:370
  633.0 39.1 %collective-permute-start.61 = (bf16[128,1536]{1,0:T(8,128)(2,1)S(1)}, bf16[128,1536]{1,0:T(8,128)(2,1)S(1)}, u32[]{:S(2)}, u32[]{:S(2)}) collective-permute-start(bf16[128,1536]{1,0:T(8,128)(2,1)S(1)} %slice.1392), channel_id=1, source_target_pairs={{0,16},{4,20},{8,24},{12,28},{16,0},{20,4},{24,8},{28,12},{1,17},{... | collective-permute-start | bytes 1179656 | tf_op jit(solution)/shard_map/ppermute | solution.py:370
  673.1 55.8 %collective-permute-start.58 = (bf16[128,1536]{1,0:T(8,128)(2,1)S(1)}, bf16[128,1536]{1,0:T(8,128)(2,1)S(1)}, u32[]{:S(2)}, u32[]{:S(2)}) collective-permute-start(bf16[128,1536]{1,0:T(8,128)(2,1)S(1)} %slice.1382), channel_id=1, source_target_pairs={{0,8},{4,12},{8,0},{12,4},{16,24},{20,28},{24,16},{28,20},{1,9},{5... | collective-permute-start | bytes 1179656 | tf_op jit(solution)/shard_map/ppermute | solution.py:370
  726.3 64.8 %collective-permute-start.73 = (bf16[128,4608]{1,0:T(8,128)(2,1)S(1)}, bf16[128,4608]{1,0:T(8,128)(2,1)S(1)}, u32[]{:S(2)}, u32[]{:S(2)}) collective-permute-start(bf16[128,4608]{1,0:T(8,128)(2,1)S(1)} %pad_maximum_fusion.11), channel_id=1, source_target_pairs={{0,2},{1,3},{2,0},{3,1},{4,6},{5,7},{6,4},{7,5},{8,10},{9,11},{10,... | collective-permute-start | bytes 3538952 | tf_op jit(solution)/shard_map/ppermute | solution.py:373
  728.9 61.8 %collective-permute-start.62 = (bf16[128,1536]{1,0:T(8,128)(2,1)S(1)}, bf16[128,1536]{1,0:T(8,128)(2,1)S(1)}, u32[]{:S(2)}, u32[]{:S(2)}) collective-permute-start(bf16[128,1536]{1,0:T(8,128)(2,1)S(1)} %fusion.12), channel_id=1, source_target_pairs={{0,2},{1,3},{2,0},{3,1},{4,6},{5,7},{6,4},{7,5},{8,10},{9,11},{10,... | collective-permute-start | bytes 1179656 | tf_op jit(solution)/shard_map/ppermute | solution.py:373
  (105 other events, 1205.3 us)

commit v2 on v1

--- a/solution.py
+++ b/solution.py
@@ -155,15 +155,19 @@
 def mlp_kernel(
     normed_ref, normed_t_ref, cot_ref, cot_t_ref, low_ref, high_ref, sum_ref, back_ref,
     total_ref, grad_ref, low_grad_ref, high_grad_ref,
-    pre, hidden, pre_low, act,
+    pre, hidden, pre_low, act, first=False,
 ):
     length = normed_ref.shape[0]
     half = low_ref.shape[0]
 
     @pl.when(pl.program_id(0) == 0)
     def _():
-        total_ref[...] = sum_ref[...]
-        grad_ref[...] = back_ref[...]
+        if first:
+            total_ref[...] = jnp.zeros_like(total_ref)
+            grad_ref[...] = jnp.zeros_like(grad_ref)
+        else:
+            total_ref[...] = sum_ref[...]
+            grad_ref[...] = back_ref[...]
 
     pre[...] = nn(normed_ref[:, :half], low_ref[:, : 2 * GROUP]) + nn(normed_ref[:, half:], high_ref[:, : 2 * GROUP])
     act[...] = nn(cot_ref[:, :half], low_ref[:, 2 * GROUP :]) + nn(cot_ref[:, half:], high_ref[:, 2 * GROUP :])
@@ -191,6 +195,162 @@
     high_grad_ref[:, 2 * GROUP :] = nn(cot_t_ref[half:], hidden[...]).astype(bf16)
 
 
+def lane_block(index):
+    return pl.ds(pl.multiple_of(index * BLOCK, BLOCK), BLOCK)
+
+
+def order_kernel(places_ref, hidden_ref, cot_ref, hidden_out_ref, cot_out_ref, cot_t_ref):
+    for place in range(hidden_ref.shape[1] // BLOCK):
+        lanes = slice(place * BLOCK, (place + 1) * BLOCK)
+        hidden_out_ref[:, lanes] = hidden_ref[:, lane_block(places_ref[place])]
+        cot_out_ref[:, lanes] = cot_ref[:, lane_block(places_ref[place])]
+    cot_t_ref[...] = cot_out_ref[...].T
+
+
+def row_loop(length, rows, body, start):
+    def step(index, carry):
+        return body(pl.ds(pl.multiple_of(index * rows, rows), rows), carry)
+
+    return lax.fori_loop(0, length // rows, step, start)
+
+
+def scale_of(values):
+    return lax.rsqrt(jnp.mean(values * values, axis=1, keepdims=True) + epsilon)
+
+
+def norm_kernel(places_ref, hidden_ref, first_ref, gains_ref, normed_ref, normed_t_ref, first_buf):
+    length = hidden_ref.shape[0]
+    for place in range(hidden_ref.shape[1] // BLOCK):
+        lanes = slice(place * BLOCK, (place + 1) * BLOCK)
+        first_buf[:, lanes] = first_ref[:, lane_block(places_ref[place])].astype(f32)
+    first = first_buf[...]
+    normed_ref[:HALO, :] = (first * scale_of(first) * gains_ref[0:1, :]).astype(bf16)
+
+    def body(rows, carry):
+        values = hidden_ref[rows, :].astype(f32)
+        normed_ref[pl.ds(rows.start + HALO, rows.size), :] = (values * scale_of(values) * gains_ref[0:1, :]).astype(bf16)
+        return carry
+
+    row_loop(length, 16, body, 0)
+    normed_t_ref[...] = normed_ref[HALO:, :].T
+
+
+def second_norm_kernel(middle_ref, gains_ref, normed_ref, normed_t_ref):
+    def body(rows, carry):
+        values = middle_ref[rows, :]
+        normed_ref[rows, :] = (values * scale_of(values) * gains_ref[1:2, :]).astype(bf16)
+        return carry
+
+    row_loop(middle_ref.shape[0], 16, body, 0)
+    normed_t_ref[...] = normed_ref[...].T
+
+
+def norm_back(values, grad, gain):
+    scale = scale_of(values)
+    unit = values * scale
+    scaled = grad * gain
+    return scale * (scaled - unit * jnp.mean(scaled * unit, axis=1, keepdims=True)), grad * unit
+
+
+def fold_rows(value):
+    rows, width = value.shape
+    return jnp.sum(value.reshape(rows // 8, 8, width), axis=0)
+
+
+def middle_kernel(
+    places_ref, middle_ref, total_ref, grad_ref, cot_ref, gains_ref,
+    out_ref, middle_grad_ref, low_ref, low_t_ref, gain_ref, buffer,
+):
+    length, model = middle_ref.shape
+
+    def body(rows, carry):
+        middle = middle_ref[rows, :]
+        change, part = norm_back(middle, grad_ref[rows, :], gains_ref[1:2, :])
+        middle_grad = cot_ref[rows, :].astype(f32) + change
+        middle_grad_ref[rows, :] = middle_grad
+        low_ref[rows, :] = middle_grad.astype(bf16)
+        buffer[rows, :] = (middle + total_ref[rows, :]).astype(bf16)
+        return carry + fold_rows(part)
+
+    total = row_loop(length, 16, body, jnp.zeros((8, model), f32))
+    gain_ref[...] = jnp.sum(total, axis=0, keepdims=True)
+    low_t_ref[...] = low_ref[...].T
+    for place in range(model // BLOCK):
+        out_ref[:, lane_block(places_ref[place])] = buffer[:, place * BLOCK : (place + 1) * BLOCK]
+
+
+def final_kernel(places_ref, hidden_ref, grad_ref, middle_grad_ref, gains_ref, out_ref, gain_ref, buffer):
+    length, model = hidden_ref.shape
+
+    def body(rows, carry):
+        change, part = norm_back(hidden_ref[rows, :].astype(f32), grad_ref[rows, :], gains_ref[0:1, :])
+        buffer[rows, :] = middle_grad_ref[rows, :] + change
+        return carry + fold_rows(part)
+
+    total = row_loop(length, 16, body, jnp.zeros((8, model), f32))
+    gain_ref[...] = jnp.sum(total, axis=0, keepdims=True)
+    for place in range(model // BLOCK):
+        out_ref[:, lane_block(places_ref[place])] = buffer[:, place * BLOCK : (place + 1) * BLOCK]
+
+
+def tables_kernel(places_ref, low_ref, high_ref, rgate_ref, igate_ref, table_ref, gains_ref, *, sub, local_blocks, chunks):
+    rows_each = 2 * local_blocks * sub
+    kinds = 2 * CONV
+    count = places_ref.shape[0]
+    size = low_ref.shape[0] * 2 // count
+    sums = [jnp.zeros((kinds * local_blocks, BLOCK), f32)] * chunks
+    for place in range(count):
+        source = low_ref if place < count // 2 else high_ref
+        top = (place % (count // 2)) * size
+        natural = places_ref[place]
+        for at in range(chunks):
+            lanes = slice(at * BLOCK, (at + 1) * BLOCK)
+            for which, gate_ref in enumerate((rgate_ref, igate_ref)):
+                for block in range(local_blocks):
+                    start = top + (which * local_blocks + block) * sub
+                    gate_ref[at * local_blocks + block, pl.ds(pl.multiple_of(natural * sub, sub), sub), :] = source[start : start + sub, lanes]
+            sums[at] = sums[at] + source[top + rows_each : top + rows_each + kinds * local_blocks, lanes].astype(f32)
+        start = top + rows_each + kinds * local_blocks
+        gains_ref[:, place * BLOCK : (place + 1) * BLOCK] = source[start : start + 2, :BLOCK].astype(f32)
+    for at in range(chunks):
+        for block in range(local_blocks):
+            column = (at * local_blocks + block) * BLOCK
+            for kind in range(kinds):
+                row = kind * local_blocks + block
+                table_ref[kind : kind + 1, column : column + BLOCK] = sums[at][row : row + 1]
+
+
+def small_grads_kernel(places_ref, rgrad_ref, igrad_ref, sums_ref, gains_ref, low_ref, high_ref, *, sub, local_blocks, chunks):
+    kinds = 2 * CONV
+    rows_each = 2 * local_blocks * sub
+    count = places_ref.shape[0]
+    size = low_ref.shape[0] * 2 // count
+    spare = size - rows_each - kinds * local_blocks - 2
+    vectors = []
+    for at in range(chunks):
+        rows = []
+        for kind in range(kinds):
+            for block in range(local_blocks):
+                column = (at * local_blocks + block) * BLOCK
+                rows.append(sums_ref[kind : kind + 1, column : column + BLOCK])
+        vectors.append(jnp.concatenate(rows, axis=0))
+    for place in range(count):
+        target = low_ref if place < count // 2 else high_ref
+        top = (place % (count // 2)) * size
+        natural = places_ref[place]
+        gains = gains_ref[:, place * BLOCK : (place + 1) * BLOCK]
+        for at in range(chunks):
+            lanes = slice(at * BLOCK, (at + 1) * BLOCK)
+            for which, grad_ref in enumerate((rgrad_ref, igrad_ref)):
+                for block in range(local_blocks):
+                    start = top + (which * local_blocks + block) * sub
+                    target[start : start + sub, lanes] = grad_ref[
+                        at * local_blocks + block, pl.ds(pl.multiple_of(natural * sub, sub), sub), :
+                    ].astype(bf16)
+            rest = jnp.concatenate([vectors[at], gains, jnp.zeros((spare, BLOCK), f32)], axis=0)
+            target[top + rows_each : top + size, lanes] = rest.astype(bf16)
+
+
 def mix_back_kernel(
     grad_low_ref, grad_t_ref, normed_t_ref, low_ref, high_ref, pre_ref, states_ref, mixed_ref, open_ref, table_ref, sum_ref,
     total_ref, local_ref, product_ref, edge_ref, low_grad_ref, high_grad_ref,
@@ -222,8 +382,8 @@
     edge_ref[1:2, :] = decay_buf[0:1, :] * product_ref[0:1, :]
     total_ref[:, :half] += nt(pre_low[...], low_ref[:, :GROUP])
     total_ref[:, half:] += nt(pre_low[...], high_ref[:, :GROUP])
-    low_grad_ref[:, :GROUP] = nn(normed_t_ref[:half, HALO:], pre_low[...]).astype(bf16)
-    high_grad_ref[:, :GROUP] = nn(normed_t_ref[half:, HALO:], pre_low[...]).astype(bf16)
+    low_grad_ref[:, :GROUP] = nn(normed_t_ref[:half], pre_low[...]).astype(bf16)
+    high_grad_ref[:, :GROUP] = nn(normed_t_ref[half:], pre_low[...]).astype(bf16)
     low_grad_ref[:, GROUP:] = nn(grad_t_ref[:half], mixed_ref[...]).astype(bf16)
     high_grad_ref[:, GROUP:] = nn(grad_t_ref[half:], mixed_ref[...]).astype(bf16)
 
@@ -318,8 +478,8 @@
         tiles(length, back)
     total_ref[:, :half] += nt(branch_low[...], low_ref[...])
     total_ref[:, half:] += nt(branch_low[...], high_ref[...])
-    low_grad_ref[...] = nn(normed_t_ref[:half, HALO:], branch_low[...]).astype(bf16)
-    high_grad_ref[...] = nn(normed_t_ref[half:, HALO:], branch_low[...]).astype(bf16)
+    low_grad_ref[...] = nn(normed_t_ref[:half], branch_low[...]).astype(bf16)
+    high_grad_ref[...] = nn(normed_t_ref[half:], branch_low[...]).astype(bf16)
 
 
 def fixed(shape):
@@ -341,22 +501,27 @@
 PARAMS = pltpu.CompilerParams(dimension_semantics=("arbitrary",), vmem_limit_bytes=56 * 1024 * 1024)
 
 
-def call(kernel, steps, in_specs, out_specs, out_shape, scratch, aliases=None):
-    return pl.pallas_call(
-        kernel,
+ANYWHERE = pl.BlockSpec(memory_space=pl.ANY)
+SCALARS = pl.BlockSpec(memory_space=pltpu.SMEM)
+
+
+def call(kernel, steps, in_specs, out_specs, out_shape, scratch, hold=()):
+    count = len(in_specs)
+
+    def body(*refs):
+        kernel(*refs[:count], *refs[count + len(hold) :])
+
+    run = pl.pallas_call(
+        body,
         grid=(steps,),
-        in_specs=in_specs,
+        in_specs=list(in_specs) + [ANYWHERE] * len(hold),
         out_specs=out_specs,
         out_shape=out_shape,
         scratch_shapes=scratch,
         compiler_params=PARAMS,
-        input_output_aliases=aliases or {},
+        name=getattr(kernel, "func", kernel).__name__,
     )
-
-
-def rms_parts(values):
-    scaling = lax.rsqrt(jnp.mean(values * values, axis=1, keepdims=True) + epsilon)
-    return (values * scaling, scaling)
+    return lambda *args: run(*args, *hold)
 
 
 def make_per_device(dp_size, tensor_size):
@@ -364,6 +529,7 @@
     dp_bits = [1 << bit for bit in range(dp_size.bit_length() - 1)]
     order_one = dp_bits[1:] + dp_bits[:1]
     order_two = dp_bits[2:3] + dp_bits[1:2] + dp_bits[3:] + dp_bits[:1]
+    orders = (order_one, order_two)
     position_of = {bit: place for place, bit in enumerate(order_one)}
 
     def swap_dp(values, bit):
@@ -372,30 +538,17 @@
     def swap_tensor(values, bit):
         return lax.ppermute(values, "tensor", [(at, at ^ bit) for at in range(tensor_size)])
 
-    def set_bit(index, bit):
-        return (index & bit) != 0
-
-    def relative(pieces, index, bits):
-        for bit, place in bits:
-            flag = set_bit(index, bit)
-            pieces = [jnp.where(flag, pieces[at ^ place], piece) for at, piece in enumerate(pieces)]
+    def relative(pieces, index):
+        bit = 1
+        while bit < len(pieces):
+            flag = (index & bit) != 0
+            pieces = [jnp.where(flag, pieces[at ^ bit], piece) for at, piece in enumerate(pieces)]
+            bit *= 2
         return pieces
 
-    dp_places = [(bit, 1 << position_of[bit]) for bit in dp_bits]
-    tensor_places = [(1 << bit, 1 << bit) for bit in range(tensor_size.bit_length() - 1)]
-
-    def place_index(place):
-        return sum(bit for bit, at in dp_places if place & at)
-
-    def to_places(pieces, index):
-        return relative([pieces[place_index(place)] for place in range(dp_size)], index, dp_places)
-
-    def from_places(pieces, index):
-        pieces = relative(pieces, index, dp_places)
-        found = [None] * dp_size
-        for place in range(dp_size):
-            found[place_index(place)] = pieces[place]
-        return found
+    place_index = [
+        sum(bit for bit in dp_bits if place & (1 << position_of[bit])) for place in range(dp_size)
+    ]
 
     def split_lanes(values, count):
         width = values.shape[1] // count
@@ -403,9 +556,10 @@
 
     def gather_dp(values, order):
         rows = values.shape[0]
-        done = []
+        done, marks = [], []
         for bit in order[:-1]:
             received = swap_dp(values, bit)
+            marks.append(received)
             low_place = position_of[bit]
             if all(position_of[other] < low_place for other in done):
                 values = jnp.concatenate([values, received], axis=0)
@@ -415,13 +569,15 @@
                     pieces += [values[at * rows : (at + 1) * rows], received[at * rows : (at + 1) * rows]]
                 values = jnp.concatenate(pieces, axis=0)
             done.append(bit)
-        return values, swap_dp(values, order[-1])
+        last = swap_dp(values, order[-1])
+        return values, last, marks + [last]
 
     def add(one, two):
         return (one.astype(f32) + two.astype(f32)).astype(bf16)
 
     def scatter_dp(own, other, order, block_rows):
         values = add(own, swap_dp(other, order[-1]))
+        marks = [values]
         left = list(order[:-1])
         while left:
             bit = left.pop()
@@ -436,7 +592,19 @@
                 )
                 keep, send = take(0), take(1)
             values = add(keep, swap_dp(send, bit))
-        return values
+            marks.append(values)
+        return values, marks
+
+    def spread_tensor(values):
+        return [values] + [swap_tensor(values, other) for other in range(1, tensor_size)]
+
+    def join_tensor(parts):
+        total = parts[0].astype(f32)
+        received = []
+        for other in range(1, tensor_size):
+            received.append(swap_tensor(parts[other], other))
+            total = total + received[-1].astype(f32)
+        return total, received
 
     def per_device(
         hidden_in, cotangent, norm_gains, mixer_in, branch_gate, mixer_out, input_gate, recur_gate,
@@ -453,41 +621,55 @@
         pair_width = 2 * chunk
         groups = pair_width // GROUP
         mlp_groups = hidden_chunk // GROUP
-
-        def rows_first(table):
-            return table.transpose(1, 0, 2).reshape(-1, BLOCK)
-
-        taps = conv_kernel.transpose(1, 2, 0).reshape(-1)
-        vectors = [table.T.reshape(-1) for table in (conv_bias, input_bias, recur_bias, decay_param)]
-        flat = jnp.concatenate([taps, *vectors, norm_gains.T.reshape(-1)])
-        gate_rows = 2 * local_blocks * sub
-        spare = (block_rows - gate_rows) * BLOCK - flat.shape[0]
-        small = jnp.concatenate(
-            [rows_first(recur_gate), rows_first(input_gate), jnp.pad(flat, (0, spare)).reshape(-1, BLOCK)], axis=0
-        )
+        fast = block_rows == BLOCK and sub % 16 == 0
+        natural_at = jnp.array(place_index, jnp.int32) ^ dp_at
+        places = natural_at if fast else jnp.arange(model // BLOCK, dtype=jnp.int32)
+
+        def features(values, back=False):
+            if fast:
+                return values
+            pieces = jnp.stack(split_lanes(values, dp_size), axis=0)
+            order = natural_at
+            if back:
+                order = jnp.zeros_like(natural_at).at[natural_at].set(jnp.arange(dp_size, dtype=jnp.int32))
+            return jnp.concatenate(list(jnp.take(pieces, order, axis=0)), axis=1)
+
         first_rows = lax.ppermute(
             hidden_in[length - HALO :], "tensor", [(at, at + 1) for at in range(tensor_size - 1)]
         )
 
-        def spread_tensor(values):
-            found = [values]
-            for bit, _ in tensor_places:
-                received = swap_tensor(jnp.concatenate(found, axis=1), bit)
-                found = found + split_lanes(received, len(found))
-            return found
-
-        small_all = jnp.concatenate(spread_tensor(small), axis=1)
-        small_low, small_high = gather_dp(small_all, order_one)
+        def rows_first(table):
+            return table.transpose(1, 0, 2).reshape(-1, BLOCK)
+
+        vectors = jnp.concatenate(
+            [conv_kernel.transpose(1, 2, 0).reshape(-1, sub)]
+            + [table.T for table in (conv_bias, input_bias, recur_bias, decay_param)],
+            axis=0,
+        )
+        owner = lax.broadcasted_iota(jnp.int32, (1, BLOCK), 1) // sub
+        vectors = jnp.where(owner == dp_at, jnp.tile(vectors, (1, BLOCK // sub)), jnp.zeros((), bf16))
+        gate_rows = 2 * local_blocks * sub
+        vector_rows = vectors.shape[0]
+        small_rows = (gate_rows + vector_rows + 2 + 15) // 16 * 16
+        small = jnp.concatenate(
+            [
+                rows_first(recur_gate),
+                rows_first(input_gate),
+                vectors,
+                jnp.pad(norm_gains.T, ((0, 0), (0, BLOCK - block_rows))),
+                jnp.zeros((small_rows - gate_rows - vector_rows - 2, BLOCK), bf16),
+            ],
+            axis=0,
+        )
+        small_low, small_high, _ = gather_dp(jnp.concatenate(spread_tensor(small), axis=1), order_one)
 
         def gather_pairs(values, arrange):
             found = spread_tensor(values)
             result = []
             for pair in range(pairs):
                 packed = arrange(found[2 * pair], found[2 * pair + 1])
-                result.append(gather_dp(packed, order_one if pair % 2 == 0 else order_two))
-            return result
-
-        in_pairs = gather_pairs(mixer_in, lambda one, two: jnp.concatenate([one, two], axis=1))
+                result.append(gather_dp(packed, orders[pair % 2]))
+            return result, found[1:]
 
         def interleave(one, two):
             gate = jnp.concatenate([one[:, :chunk], two[:, :chunk]], axis=1)
@@ -497,48 +679,61 @@
                 pieces += [gate[:, at * GROUP : (at + 1) * GROUP], out[:, at * GROUP : (at + 1) * GROUP]]
             return jnp.concatenate(pieces, axis=1)
 
-        out_pairs = gather_pairs(jnp.concatenate([branch_gate, mixer_out], axis=1), interleave)
+        in_pairs, in_far = gather_pairs(mixer_in, lambda one, two: jnp.concatenate([one, two], axis=1))
+        out_pairs, out_far = gather_pairs(jnp.concatenate([branch_gate, mixer_out], axis=1), interleave)
         mlp_pieces = []
         for at in range(mlp_groups):
             mlp_pieces += [w[:, at * GROUP : (at + 1) * GROUP] for w in (mlp_gate, mlp_up, mlp_down)]
-        mlp_chunks = [
-            gather_dp(values, order_one if at % 2 == 0 else order_two)
-            for at, values in enumerate(spread_tensor(jnp.concatenate(mlp_pieces, axis=1)))
+        mlp_near = spread_tensor(jnp.concatenate(mlp_pieces, axis=1))
+        mlp_chunks = [gather_dp(values, orders[at % 2]) for at, values in enumerate(mlp_near)]
+
+        whole = fixed((length, model))
+        turned = fixed((model, length))
+        hidden_low, cot_low, cot_t = call(
+            order_kernel, 1, [SCALARS, whole, whole], [whole, whole, turned],
+            [shaped(length, model, kind=bf16), shaped(length, model, kind=bf16), shaped(model, length, kind=bf16)], [],
+        )(places, features(hidden_in), features(cotangent))
+
+        kinds = 2 * CONV
+        channels = tensor_size * chunk
+        blocks = tensor_size * local_blocks
+        if fast:
+            small_spec = fixed((model // 2 // block_rows * small_rows, tensor_size * BLOCK))
+            gate_spec = fixed((blocks, BLOCK, BLOCK))
+            def tables_of(*args, **sizes):
+                tables_kernel(*args, sub=sub, local_blocks=local_blocks, chunks=tensor_size)
+            rgates, igates, table, gains = call(
+                tables_of, 1, [SCALARS, small_spec, small_spec], [gate_spec, gate_spec, fixed((kinds, channels)), fixed((2, model))],
+                [shaped(blocks, BLOCK, BLOCK, kind=bf16), shaped(blocks, BLOCK, BLOCK, kind=bf16), shaped(kinds, channels), shaped(2, model)], [],
+                hold=out_far,
+            )(places, small_low, small_high)
+        else:
+            stacked = jnp.concatenate([small_low, small_high], axis=0).reshape(dp_size, small_rows, -1)
+            order = jnp.zeros_like(natural_at).at[natural_at].set(jnp.arange(dp_size, dtype=jnp.int32))
+            gates = jnp.take(stacked[:, :gate_rows], order, axis=0).reshape(dp_size, 2, local_blocks, sub, tensor_size, BLOCK)
+            gates = gates.transpose(1, 4, 2, 0, 3, 5).reshape(2, blocks, BLOCK, BLOCK)
+            rgates, igates = gates[0], gates[1]
+            table = jnp.sum(stacked[:, gate_rows : gate_rows + vector_rows].astype(f32), axis=0)
+            table = table.reshape(kinds, local_blocks, tensor_size, BLOCK).transpose(0, 2, 1, 3).reshape(kinds, channels)
+            gains = stacked[:, gate_rows + vector_rows : gate_rows + vector_rows + 2, :block_rows]
+            gains = gains.transpose(1, 0, 2).reshape(2, model).astype(f32)
+        decay_rates = table[7:8]
+        table = jnp.concatenate([table[:7], -8.0 * jax.nn.softplus(-decay_rates)], axis=0)
+
+        full = length + HALO
+        normed_one, normed_one_t = call(
+            norm_kernel, 1, [SCALARS, whole, fixed((HALO, model)), fixed((2, model))], [fixed((full, model)), turned],
+            [shaped(full, model, kind=bf16), shaped(model, length, kind=bf16)], [pltpu.VMEM((HALO, model), f32)],
+        )(places, hidden_low, features(first_rows), gains)
+
+        fed = []
+        fed_holds = [
+            [out_pairs[0][2][0], out_pairs[1][2][0], mlp_near[1]],
+            [out_pairs[0][2][1], out_pairs[1][2][1], mlp_near[2]],
         ]
-
-        tables_at = jnp.concatenate([small_low, small_high], axis=0).reshape(dp_size, block_rows, tensor_size * BLOCK)
-        vector_rows = tables_at[:, gate_rows:]
-        natural = jnp.stack(from_places([tables_at[at] for at in range(dp_size)], dp_at), axis=0)
-        gates = natural[:, :gate_rows].reshape(dp_size, 2, local_blocks, sub, tensor_size, BLOCK)
-        gates = gates.transpose(1, 4, 2, 0, 3, 5).reshape(2, tensor_size * local_blocks, BLOCK, BLOCK)
-        rgates, igates = gates[0], gates[1]
-        flat_all = natural[:, gate_rows:].reshape(dp_size, -1, tensor_size, BLOCK).transpose(0, 2, 1, 3)
-        flat_all = flat_all.reshape(dp_size, tensor_size, -1)
-        count = 2 * CONV * local_blocks * sub
-        table = flat_all[:, :, :count].reshape(dp_size, tensor_size, 2 * CONV, local_blocks, sub)
-        table = table.transpose(2, 1, 3, 0, 4).reshape(2 * CONV, tensor_size * chunk).astype(f32)
-        decay_rates = table[7]
-        table = jnp.concatenate([table[:7], -8.0 * jax.nn.softplus(-decay_rates)[None]], axis=0)
-        gain_rows = vector_rows[:, :, :BLOCK].reshape(dp_size, -1)[:, count : count + 2 * block_rows]
-        gains = gain_rows.reshape(dp_size, 2, block_rows).transpose(1, 0, 2).reshape(2, model).astype(f32)
-
-        def reorder(values, mover):
-            return jnp.concatenate(mover(split_lanes(values, dp_size), dp_at), axis=1)
-
-        hidden_all = reorder(jnp.concatenate([first_rows, hidden_in], axis=0), to_places).astype(f32)
-        cot_low = reorder(cotangent, to_places)
-        unit_all, scale_all = rms_parts(hidden_all)
-        residual = hidden_all[HALO:]
-        unit_one, scale_one = unit_all[HALO:], scale_all[HALO:]
-        normed_one = (unit_all * gains[0]).astype(bf16)
-        normed_one_t = normed_one.T
-        cot_t = cot_low.T
-
-        full = length + HALO
-        fed = []
         for pair in range(pairs):
-            low, high = in_pairs[pair]
-            blocks = slice(2 * pair * local_blocks, 2 * (pair + 1) * local_blocks)
+            low, high, _ = in_pairs[pair]
+            part = slice(2 * pair * local_blocks, 2 * (pair + 1) * local_blocks)
             lanes = slice(pair * pair_width, (pair + 1) * pair_width)
             fed.append(
                 call(
@@ -548,7 +743,8 @@
                     [lanes_of(full)] + [lanes_of(length)] * 5,
                     [shaped(full, pair_width)] + [shaped(length, pair_width)] * 5,
                     [pltpu.VMEM((length, GROUP), bf16)] + [pltpu.VMEM((length, GROUP), f32)] * 3,
-                )(normed_one, low, high, rgates[blocks], igates[blocks], table[:, lanes])
+                    hold=fed_holds[pair],
+                )(normed_one, low, high, rgates[part], igates[part], table[:, lanes])
             )
 
         def exchange(products, ends, later):
@@ -557,7 +753,7 @@
             for other in range(1, tensor_size):
                 pieces = split_lanes(swap_tensor(mine, other), tensor_size)
                 found.append(jnp.concatenate([pieces[at ^ other] for at in range(tensor_size)], axis=1))
-            found = relative(found, tensor_at, tensor_places)
+            found = relative(found, tensor_at)
             state = jnp.zeros_like(ends)
             turn = range(tensor_size - 1, 0, -1) if later else range(tensor_size - 1)
             for at in turn:
@@ -570,66 +766,61 @@
             jnp.concatenate([one[4][length - 1 :] for one in fed], axis=1),
             False,
         )
-        middle = residual
+        middle = hidden_low.astype(f32)
         mixed = []
+        mixed_holds = [
+            [mlp_chunks[0][2][0], mlp_chunks[1][2][0], mlp_near[3]],
+            [mlp_chunks[0][2][1], mlp_chunks[1][2][1]],
+        ]
         for pair in range(pairs):
-            low, high = out_pairs[pair]
+            low, high, _ = out_pairs[pair]
             lanes = slice(pair * pair_width, (pair + 1) * pair_width)
             gate_pre, states, mixed_low, middle = call(
                 mix_out_kernel,
                 groups,
-                [fixed((full, model)), lanes_of(half, 2 * GROUP), lanes_of(half, 2 * GROUP), lanes_of(length), lanes_of(length), lanes_of(1), fixed((length, model))],
-                [lanes_of(length), lanes_of(length + 8), lanes_of(length), fixed((length, model))],
+                [fixed((full, model)), lanes_of(half, 2 * GROUP), lanes_of(half, 2 * GROUP), lanes_of(length), lanes_of(length), lanes_of(1), whole],
+                [lanes_of(length), lanes_of(length + 8), lanes_of(length), whole],
                 [shaped(length, pair_width), shaped(length + 8, pair_width), shaped(length, pair_width, kind=bf16), shaped(length, model)],
                 [],
+                hold=mixed_holds[pair],
             )(normed_one, low, high, fed[pair][4], fed[pair][5], enter[:, lanes], middle)
             mixed.append((gate_pre, states, mixed_low))
-
-        unit_two, scale_two = rms_parts(middle)
-        normed_two = (unit_two * gains[1]).astype(bf16)
-        normed_two_t = normed_two.T
-
-        total = middle
-        normed_grad = jnp.zeros((length, model), f32)
-        chunk_grads = []
-        whole = fixed((length, model))
-        turned = fixed((model, length))
-        for low, high in mlp_chunks:
+        normed_two, normed_two_t = call(
+            second_norm_kernel, 1, [whole, fixed((2, model))], [whole, turned],
+            [shaped(length, model, kind=bf16), shaped(model, length, kind=bf16)], [],
+        )(middle, gains)
+
+        total = normed_grad = None
+        moved = []
+        sums = []
+        for at, (low, high, _) in enumerate(mlp_chunks):
+            holds = [
+                [mlp_chunks[2][2][0], mlp_chunks[3][2][0]],
+                [mlp_chunks[2][2][1]],
+                [lambda: moved[0][1][0]],
+                [lambda: moved[1][1][0]],
+            ][at]
+            holds = [hold() if callable(hold) else hold for hold in holds]
+            before = [] if at == 0 else [total, normed_grad]
+            width = 3 * GROUP
+
+            def kernel(*refs, at=at):
+                if at == 0:
+                    mlp_kernel(*refs[:6], None, None, *refs[6:], first=True)
+                else:
+                    mlp_kernel(*refs)
+
             total, normed_grad, low_grad, high_grad = call(
-                mlp_kernel,
+                kernel,
                 mlp_groups,
-                [whole, turned, whole, turned, lanes_of(half, 3 * GROUP), lanes_of(half, 3 * GROUP), whole, whole],
-                [whole, whole, lanes_of(half, 3 * GROUP), lanes_of(half, 3 * GROUP)],
+                [whole, turned, whole, turned, lanes_of(half, width), lanes_of(half, width)] + [whole] * len(before),
+                [whole, whole, lanes_of(half, width), lanes_of(half, width)],
                 [shaped(length, model), shaped(length, model), shaped(half, 3 * hidden_chunk, kind=bf16), shaped(half, 3 * hidden_chunk, kind=bf16)],
                 [pltpu.VMEM((length, 2 * GROUP), f32), pltpu.VMEM((length, GROUP), bf16), pltpu.VMEM((length, 2 * GROUP), bf16), pltpu.VMEM((length, GROUP), f32)],
-            )(normed_two, normed_two_t, cot_low, cot_t, low, high, total, normed_grad)
-            chunk_grads.append((low_grad, high_grad))
-        hidden_out = reorder(total.astype(bf16), from_places)
-
-        scaled_two = normed_grad * gains[1]
-        gain_two_part = jnp.sum(normed_grad * unit_two, axis=0)
-        middle_grad = cot_low.astype(f32) + scale_two * (
-            scaled_two - unit_two * jnp.mean(scaled_two * unit_two, axis=1, keepdims=True)
-        )
-        middle_low = middle_grad.astype(bf16)
-        middle_low_t = middle_low.T
-
-        def join_tensor(parts):
-            for bit in reversed([bit for bit, _ in tensor_places]):
-                received = split_lanes(swap_tensor(jnp.concatenate(parts[bit:], axis=1), bit), bit)
-                last = bit == 1
-                parts = [
-                    (one.astype(f32) + two.astype(f32)) if last else add(one, two)
-                    for one, two in zip(parts[:bit], received)
-                ]
-            return parts[0]
-
-        mlp_sum = join_tensor(
-            [
-                scatter_dp(low_grad, high_grad, order_one if at % 2 == 0 else order_two, block_rows)
-                for at, (low_grad, high_grad) in enumerate(chunk_grads)
-            ]
-        )
+                hold=holds,
+            )(normed_two, normed_two_t, cot_low, cot_t, low, high, *before)
+            moved.append(scatter_dp(low_grad, high_grad, orders[at % 2], block_rows))
+        mlp_sum, mlp_far = join_tensor([one[0] for one in moved])
         mlp_grads = [
             jnp.concatenate(
                 [mlp_sum[:, (3 * at + which) * GROUP : (3 * at + which + 1) * GROUP] for at in range(mlp_groups)], axis=1
@@ -637,23 +828,38 @@
             for which in range(3)
         ]
 
+        hidden_out, middle_grad, middle_low, middle_low_t, gain_two = call(
+            middle_kernel, 1, [SCALARS, whole, whole, whole, whole, fixed((2, model))],
+            [whole, whole, whole, turned, fixed((1, model))],
+            [shaped(length, model, kind=bf16), shaped(length, model), shaped(length, model, kind=bf16), shaped(model, length, kind=bf16), shaped(1, model)],
+            [pltpu.VMEM((length, model), bf16)],
+            hold=[moved[0][1][1], moved[2][1][0]],
+        )(places, middle, total, normed_grad, cot_low, gains)
+        hidden_out = features(hidden_out, True)
+
         normed_grad = jnp.zeros((length, model), f32)
         backs = []
         out_grads = []
+        out_moved = []
+        back_holds = [
+            [moved[1][1][1], moved[3][1][0]],
+            [moved[0][1][2], moved[1][1][2], moved[2][1][1]],
+        ]
         for pair in range(pairs):
-            low, high = out_pairs[pair]
+            low, high, _ = out_pairs[pair]
             gate_pre, states, mixed_low = mixed[pair]
             lanes = slice(pair * pair_width, (pair + 1) * pair_width)
             normed_grad, local, product, edge, low_grad, high_grad = call(
                 mix_back_kernel,
                 groups,
-                [whole, turned, fixed((model, full)), lanes_of(half, 2 * GROUP), lanes_of(half, 2 * GROUP), lanes_of(length), lanes_of(length + 8), lanes_of(length), lanes_of(length), lanes_of(8), whole],
+                [whole, turned, turned, lanes_of(half, 2 * GROUP), lanes_of(half, 2 * GROUP), lanes_of(length), lanes_of(length + 8), lanes_of(length), lanes_of(length), lanes_of(8), whole],
                 [whole, lanes_of(length), lanes_of(length), lanes_of(8), lanes_of(half, 2 * GROUP), lanes_of(half, 2 * GROUP)],
                 [shaped(length, model), shaped(length, pair_width), shaped(length, pair_width), shaped(8, pair_width), shaped(half, 2 * pair_width, kind=bf16), shaped(half, 2 * pair_width, kind=bf16)],
                 [pltpu.VMEM((length, GROUP), f32), pltpu.VMEM((length, GROUP), f32), pltpu.VMEM((length, GROUP), bf16), pltpu.VMEM((length + 8, GROUP), f32)],
+                hold=back_holds[pair],
             )(middle_low, middle_low_t, normed_one_t, low, high, gate_pre, states, mixed_low, fed[pair][2], table[:, lanes], normed_grad)
             backs.append((local, product, edge))
-            out_grads.append((low_grad, high_grad))
+            out_moved.append(scatter_dp(low_grad, high_grad, orders[pair % 2], block_rows))
 
         def separate(values):
             gate = [values[:, 2 * at * GROUP : (2 * at + 1) * GROUP] for at in range(groups)]
@@ -661,10 +867,7 @@
             gate, out = jnp.concatenate(gate, axis=1), jnp.concatenate(out, axis=1)
             return [jnp.concatenate([gate[:, :chunk], out[:, :chunk]], axis=1), jnp.concatenate([gate[:, chunk:], out[:, chunk:]], axis=1)]
 
-        parts = []
-        for pair, (low_grad, high_grad) in enumerate(out_grads):
-            parts += separate(scatter_dp(low_grad, high_grad, order_one if pair % 2 == 0 else order_two, block_rows))
-        out_sum = join_tensor(parts)
+        out_sum, out_back = join_tensor([part for one in out_moved for part in separate(one[0])])
 
         leave = exchange(
             jnp.concatenate([one[2][1:2] for one in backs], axis=1),
@@ -672,8 +875,12 @@
             True,
         )
         gate_backs = []
+        gate_holds = [
+            [moved[3][1][1], mlp_far[0], out_moved[0][1][0]],
+            [moved[2][1][2], out_moved[1][1][0]],
+        ]
         for pair in range(pairs):
-            blocks = slice(2 * pair * local_blocks, 2 * (pair + 1) * local_blocks)
+            part = slice(2 * pair * local_blocks, 2 * (pair + 1) * local_blocks)
             lanes = slice(pair * pair_width, (pair + 1) * pair_width)
             branch, conv_out, recur_open, inflow = fed[pair][:4]
             local, product, _ = backs[pair]
@@ -685,58 +892,76 @@
                     [lanes_of(length), blocks_of(), blocks_of(), lanes_of(8)],
                     [shaped(length, pair_width), shaped(2 * local_blocks, BLOCK, BLOCK), shaped(2 * local_blocks, BLOCK, BLOCK), shaped(8, pair_width)],
                     [pltpu.VMEM((length, GROUP), bf16)] * 3,
-                )(local, product, leave[:, lanes], mixed[pair][1], recur_open, inflow, conv_out, branch, rgates[blocks], igates[blocks], table[:, lanes])
+                    hold=gate_holds[pair],
+                )(local, product, leave[:, lanes], mixed[pair][1], recur_open, inflow, conv_out, branch, rgates[part], igates[part], table[:, lanes])
             )
         heads = jnp.concatenate([one[0][:8] for one in gate_backs], axis=1)
-        heads = jnp.concatenate(relative(split_lanes(heads, tensor_size), tensor_at, tensor_places), axis=1)
+        heads = jnp.concatenate(relative(split_lanes(heads, tensor_size), tensor_at), axis=1)
         heads = lax.ppermute(heads, "tensor", [(at + 1, at) for at in range(tensor_size - 1)])
-        after = jnp.concatenate(relative(split_lanes(heads, tensor_size), tensor_at, tensor_places), axis=1)
-        parts = []
+        after = jnp.concatenate(relative(split_lanes(heads, tensor_size), tensor_at), axis=1)
+        in_parts = []
+        branch_holds = [
+            [moved[3][1][2], mlp_far[1], out_moved[0][1][1]],
+            [out_moved[1][1][1]],
+        ]
         for pair in range(pairs):
-            low, high = in_pairs[pair]
+            low, high, _ = in_pairs[pair]
             lanes = slice(pair * pair_width, (pair + 1) * pair_width)
             normed_grad, low_grad, high_grad = call(
                 branch_back_kernel,
                 groups,
-                [lanes_of(length), lanes_of(8), lanes_of(8), fixed((model, full)), lanes_of(half), lanes_of(half), whole],
+                [lanes_of(length), lanes_of(8), lanes_of(8), turned, lanes_of(half), lanes_of(half), whole],
                 [whole, lanes_of(half), lanes_of(half)],
                 [shaped(length, model), shaped(half, pair_width, kind=bf16), shaped(half, pair_width, kind=bf16)],
                 [pltpu.VMEM((length + 8, GROUP), f32), pltpu.VMEM((length, GROUP), bf16)],
+                hold=branch_holds[pair],
             )(gate_backs[pair][0], after[:, lanes], table[:, lanes], normed_one_t, low, high, normed_grad)
-            parts += split_lanes(scatter_dp(low_grad, high_grad, order_one if pair % 2 == 0 else order_two, block_rows), 2)
-        in_sum = join_tensor(parts)
-
-        scaled_one = normed_grad * gains[0]
-        gain_one_part = jnp.sum(normed_grad * unit_one, axis=0)
-        hidden_grad = middle_grad + scale_one * (
-            scaled_one - unit_one * jnp.mean(scaled_one * unit_one, axis=1, keepdims=True)
-        )
-        hidden_grad = reorder(hidden_grad, from_places)
+            in_parts += split_lanes(scatter_dp(low_grad, high_grad, orders[pair % 2], block_rows)[0], 2)
+        in_sum, _ = join_tensor(in_parts)
+
+        hidden_grad, gain_one = call(
+            final_kernel, 1, [SCALARS, whole, whole, whole, fixed((2, model))], [whole, fixed((1, model))],
+            [shaped(length, model), shaped(1, model)], [pltpu.VMEM((length, model), f32)],
+            hold=[],
+        )(places, hidden_low, normed_grad, middle_grad, gains)
+        hidden_grad = features(hidden_grad, True)
 
         rgrads = jnp.concatenate([one[1] for one in gate_backs], axis=0)
         igrads = jnp.concatenate([one[2] for one in gate_backs], axis=0)
-        gate_grads = jnp.stack([rgrads, igrads], axis=0).reshape(2, tensor_size, local_blocks, dp_size, sub, BLOCK)
-        gate_grads = gate_grads.transpose(3, 0, 2, 4, 1, 5).reshape(dp_size, gate_rows, tensor_size * BLOCK)
-        sums = jnp.concatenate([one[3] for one in gate_backs], axis=1)
-        decay_row = sums[3:4] * (8.0 * jax.nn.sigmoid(-decay_rates))[None]
-        sums = jnp.concatenate([sums[4:8], sums[0:3], decay_row], axis=0)
-        sums = sums.reshape(2 * CONV, tensor_size, local_blocks, dp_size, sub).transpose(3, 1, 0, 2, 4)
-        sums = sums.reshape(dp_size, tensor_size, count)
-        gate_grads = jnp.stack(to_places([gate_grads[at] for at in range(dp_size)], dp_at), axis=0)
-        sums = jnp.stack(to_places([sums[at] for at in range(dp_size)], dp_at), axis=0)
-        gain_parts = jnp.stack([gain_one_part, gain_two_part], axis=0).reshape(2, dp_size, tensor_size, -1)
-        gain_parts = jnp.stack(relative([gain_parts[:, :, at] for at in range(tensor_size)], tensor_at, tensor_places), axis=0)
-        gain_parts = gain_parts.transpose(2, 0, 1, 3).reshape(dp_size, tensor_size, -1)
-        flat = jnp.concatenate([sums, gain_parts], axis=2)
-        flat = jnp.pad(flat, ((0, 0), (0, 0), (0, (block_rows - gate_rows) * BLOCK - flat.shape[2])))
-        flat = flat.reshape(dp_size, tensor_size, -1, BLOCK).transpose(0, 2, 1, 3).reshape(dp_size, -1, tensor_size * BLOCK)
-        small_grads = jnp.concatenate([gate_grads, flat], axis=1).reshape(model, tensor_size * BLOCK).astype(bf16)
-        small_sum = scatter_dp(small_grads[:half], small_grads[half:], order_one, block_rows)
-        small_sum = join_tensor(split_lanes(small_sum, tensor_size))
+        rows = jnp.concatenate([one[3] for one in gate_backs], axis=1)
+        decay_row = rows[3:4] * (8.0 * jax.nn.sigmoid(-decay_rates))
+        rows = jnp.concatenate([rows[4:8], rows[0:3], decay_row], axis=0)
+        gain_parts = jnp.concatenate([gain_one, gain_two], axis=0)
+        if fast:
+            def small_grads(*args, **sizes):
+                small_grads_kernel(*args, sub=sub, local_blocks=local_blocks, chunks=tensor_size)
+            small_own, small_other = call(
+                small_grads, 1, [SCALARS, gate_spec, gate_spec, fixed((kinds, channels)), fixed((2, model))], [small_spec, small_spec],
+                [shaped(*small_spec.block_shape, kind=bf16)] * 2, [],
+            )(places, rgrads, igrads, rows, gain_parts)
+        else:
+            gate_grads = jnp.stack([rgrads, igrads], axis=0).reshape(2, tensor_size, local_blocks, dp_size, sub, BLOCK)
+            gate_grads = gate_grads.transpose(3, 0, 2, 4, 1, 5).reshape(dp_size, gate_rows, tensor_size * BLOCK)
+            gate_grads = jnp.take(gate_grads, natural_at, axis=0)
+            rows = rows.reshape(kinds, tensor_size, local_blocks, BLOCK).transpose(0, 2, 1, 3).reshape(1, vector_rows, -1)
+            gain_parts = gain_parts.reshape(2, dp_size, block_rows).transpose(1, 0, 2)
+            gain_parts = jnp.pad(gain_parts, ((0, 0), (0, 0), (0, BLOCK - block_rows)))
+            rest = small_rows - gate_rows - vector_rows - 2
+            pieces = [
+                gate_grads,
+                jnp.broadcast_to(rows, (dp_size,) + rows.shape[1:]),
+                jnp.tile(gain_parts, (1, 1, tensor_size)),
+                jnp.zeros((dp_size, rest, tensor_size * BLOCK), f32),
+            ]
+            small_grads = jnp.concatenate(pieces, axis=1).reshape(dp_size * small_rows, -1).astype(bf16)
+            small_own, small_other = jnp.split(small_grads, 2, axis=0)
+        small_sum, _ = scatter_dp(small_own, small_other, order_one, small_rows)
+        small_sum, _ = join_tensor(split_lanes(small_sum, tensor_size))
         gate_sum = small_sum[:gate_rows].reshape(2, local_blocks, sub, BLOCK).transpose(0, 2, 1, 3)
-        flat_sum = small_sum[gate_rows:].reshape(-1)
-        vector_sum = flat_sum[:count].reshape(2 * CONV, local_blocks, sub)
-        gain_sum = flat_sum[count : count + 2 * block_rows // tensor_size].reshape(2, -1).T
+        vector_sum = lax.dynamic_slice(small_sum, (gate_rows, dp_at * sub), (vector_rows, sub))
+        vector_sum = vector_sum.reshape(kinds, local_blocks, sub)
+        gain_rows = block_rows // tensor_size
+        gain_sum = lax.dynamic_slice(small_sum, (gate_rows + vector_rows, tensor_at * gain_rows), (2, gain_rows)).T
 
         return (
             hidden_out,

time: 818 us -> 646 us (0.79)
  waiting for transfers between devices: 317 us -> 177 us
  local copies, waits for them, and re-layouts: 137 us -> 54.1 us
  starting transfers between devices: 80.2 us -> 126 us
  Pallas kernels: 191 us -> 232 us
  other arithmetic: 83.2 us -> 48.7 us
    ppermute x54, waiting for transfers between devices: 208 us -> 105 us  [swap_dp(): return lax.ppermute(values, 'dp', [(at, at ^ bit) for at in range(dp_size)])]
    ppermute x22 -> x30, waiting for transfers between devices: 109 us -> 67.1 us  [swap_tensor(): lax.ppermute(values, 'tensor', [(at, at ^ bit) for at in range(tensor_siz...]
    pallas_call x14 -> x21, Pallas kernels: 191 us -> 232 us  [call(): return lambda *args: run(*args, *hold)]
    ppermute x22 -> x30, starting transfers between devices: 37.4 us -> 76.4 us  [swap_tensor(): lax.ppermute(values, 'tensor', [(at, at ^ bit) for at in range(tensor_siz...]
    unnamed x173 -> x175, local copies, waits for them, and re-layouts: 49.1 us -> 23.4 us
    select_n x16 -> x0, local copies, waits for them, and re-layouts: 18.7 us -> none  [relative(): jnp.where(flag, pieces[at ^ place], piece)]
    pallas_call x4 -> x0, local copies, waits for them, and re-layouts: 10.3 us -> none  [the longest x2 5.47 us: per_device(): call(mlp_kernel, mlp_groups, [whole, turned, whole, turned, lanes_of(half...]
    slice x17 -> x5, local copies, waits for them, and re-layouts: 12.2 us -> 2.22 us  [the longest x1 2.12 us: per_device(): igates[part]]
  transfers between devices with their start and end apart: 78 -> 86, of which waited for: 28 -> 26; matrix products, arithmetic and copies ran while one was open for 25% -> 14% of each run, Pallas kernels for 24% -> 36%
where the time goes in v2:
time: 646 us; the launch traced here: 640 us
  Pallas kernels  232 us (36%)
  waiting for transfers between devices  177 us (27%)
  starting transfers between devices  126 us (20%)
  local copies, waits for them, and re-layouts  54.1 us (8%)
  other arithmetic  48.7 us (8%)
    pallas_call x21, Pallas kernels, call(): return lambda *args: run(*args, *hold)  232 us
    ppermute x54, waiting for transfers between devices, swap_dp(): return lax.ppermute(values, 'dp', [(at, at ^ bit) for at in range(dp_size)])  105 us
    ppermute x30, starting transfers between devices, swap_tensor(): lax.ppermute(values, 'tensor', [(at, at ^ bit) for at in range(tensor_siz...  76.4 us
    ppermute x30, waiting for transfers between devices, swap_tensor(): lax.ppermute(values, 'tensor', [(at, at ^ bit) for at in range(tensor_siz...  67.1 us
    ppermute x54, starting transfers between devices, swap_dp(): return lax.ppermute(values, 'dp', [(at, at ^ bit) for at in range(dp_size)])  44.6 us
    unnamed x175, local copies, waits for them, and re-layouts  23.4 us
    convert_element_type x26, other arithmetic, add(): return (one.astype(f32) + two.astype(f32)).astype(bf16)  15.8 us
  transfers between devices with their start and end apart: 86, of which 26 were waited for; matrix products, arithmetic and copies ran while one was open for 14% of the time, Pallas kernels for 36%

profile of v2, /device:TPU:0, one launch (start us, length us, event | category | flops | bytes accessed | tf_op | source)
XLA Modules:
  0.0 639.6 jit_solution(3062400108768716845)
XLA Ops:
  36.3 3.8 collective-permute-start.13
  40.2 9.3 %collective-permute-done.13 = bf16[128,384]{1,0:T(8,128)(2,1)S(1)} collective-permute-done((bf16[128,384]{1,0:T(8,128)(2,1)S(1)}, bf16[128,384]{1,0:T(8,128)(2,1)S(1)}, u32[]{:S(2)}, u32[]{:S(2)}) %collective-permute-start.13) | collective-permute-done | bytes 98336 | tf_op jit(solution)/shard_map/ppermute | solution.py:539
  63.4 9.6 %collective-permute-done.22 = bf16[128,768]{1,0:T(8,128)(2,1)S(1)} collective-permute-done((bf16[128,768]{1,0:T(8,128)(2,1)S(1)}, bf16[128,768]{1,0:T(8,128)(2,1)S(1)}, u32[]{:S(2)}, u32[]{:S(2)}) %collective-permute-start.22) | collective-permute-done | bytes 196640 | tf_op jit(solution)/shard_map/ppermute | solution.py:536
  79.9 5.5 collective-permute-done.10.refs_7_
  111.6 5.9 norm_kernel.1
  128.3 37.6 %collective-permute-done.35.refs_7_ = bf16[128,2304]{1,0:T(8,128)(2,1)S(1)} collective-permute-done((bf16[128,2304]{1,0:T(8,128)(2,1)S(1)}, bf16[128,2304]{1,0:T(8,128)(2,1)S(1)}, u32[]{:S(2)}, u32[]{:S(2)}) %collective-permute-start.35) | collective-permute-done | bytes 589856 | tf_op jit(solution)/shard_map/ppermute | solution.py:536
  172.8 14.2 %mix_in_kernel.3 = (f32[528,768]{1,0:T(8,128)}, f32[512,768]{1,0:T(8,128)}, f32[512,768]{1,0:T(8,128)}, f32[512,768]{1,0:T(8,128)}, f32[512,768]{1,0:T(8,128)}, /*index=5*/f32[512,768]{1,0:T(8,128)}) custom-call(bf16[528,1024]{1,0:T(8,128)(2,1)} %get-tuple-element.100.refs_0_, bf16[512,768]{1,0:T(8,128)(2,1)} %copy-done.20, bf16[512,768]{1,0:T(8,128)(2,1)} %copy-done.40, ...), custom_call_target="tpu_custom_call" | custom-call | tf_op jit(solution)/shard_map/mix_in_kernel/pallas_call | solution.py:524
  189.4 14.2 %mix_in_kernel.2 = (f32[528,768]{1,0:T(8,128)}, f32[512,768]{1,0:T(8,128)}, f32[512,768]{1,0:T(8,128)}, f32[512,768]{1,0:T(8,128)}, f32[512,768]{1,0:T(8,128)}, /*index=5*/f32[512,768]{1,0:T(8,128)}) custom-call(bf16[528,1024]{1,0:T(8,128)(2,1)} %get-tuple-element.100.refs_0_, bf16[512,768]{1,0:T(8,128)(2,1)} %copy-done.17, bf16[512,768]{1,0:T(8,128)(2,1)} %copy-done.39, ...), custom_call_target="tpu_custom_call" | custom-call | tf_op jit(solution)/shard_map/mix_in_kernel/pallas_call | solution.py:524
  205.1 15.8 %collective-permute-start.26 = (f32[2,1536]{1,0:T(2,128)S(1)}, f32[2,1536]{1,0:T(2,128)S(1)}, u32[]{:S(2)}, u32[]{:S(2)}) collective-permute-start(f32[2,1536]{1,0:T(2,128)S(1)} %maximum_maximum_fusion), channel_id=1, source_target_pairs={{0,1},{1,0},{2,3},{3,2},{4,5},{5,4},{6,7},{7,6},{8,9},{9,8},{10,11... | collective-permute-start | bytes 36872 | tf_op jit(solution)/shard_map/ppermute | solution.py:539
  238.3 10.0 %mix_out_kernel.2 = (f32[512,768]{1,0:T(8,128)}, f32[520,768]{1,0:T(8,128)}, bf16[512,768]{1,0:T(8,128)(2,1)}, f32[512,1024]{1,0:T(8,128)}) custom-call(bf16[528,1024]{1,0:T(8,128)(2,1)} %get-tuple-element.100.refs_0_, bf16[512,1536]{1,0:T(8,128)(2,1)} %copy-done.7, bf16[512,1536]{1,0:T(8,128)(2,1)} %collective-permute-done.29.refs_2_.refs_4_, ...), custom_call_target="tpu_custom_call" | custom-call | tf_op jit(solution)/shard_map/mix_out_kernel/pallas_call | solution.py:524
  248.3 10.0 %mix_out_kernel.3 = (f32[512,768]{1,0:T(8,128)}, f32[520,768]{1,0:T(8,128)}, bf16[512,768]{1,0:T(8,128)(2,1)}, f32[512,1024]{1,0:T(8,128)}) custom-call(bf16[528,1024]{1,0:T(8,128)(2,1)} %get-tuple-element.100.refs_0_, bf16[512,1536]{1,0:T(8,128)(2,1)} %copy-done.6, bf16[512,1536]{1,0:T(8,128)(2,1)} %collective-permute-done.12.refs_2_.refs_4_, ...), custom_call_target="tpu_custom_call" | custom-call | tf_op jit(solution)/shard_map/mix_out_kernel/pallas_call | solution.py:524
  258.3 6.1 second_norm_kernel.1
  264.5 16.1 %kernel.4 = (f32[512,1024]{1,0:T(8,128)}, f32[512,1024]{1,0:T(8,128)}, bf16[512,2304]{1,0:T(8,128)(2,1)}, bf16[512,2304]{1,0:T(8,128)(2,1)}) custom-call(bf16[512,1024]{1,0:T(8,128)(2,1)} %get-tuple-element.110.refs_0_, bf16[1024,512]{1,0:T(8,128)(2,1)} %get-tuple-element.111.refs_1_, bf16[512,1024]{1,0:T(8,128)(2,1)} %get-tuple-element.112.refs_2_.refs_4_, ...), custom_call_target="tpu_custom_call" | custom-call | tf_op jit(solution)/shard_map/kernel/pallas_call | solution.py:524
  285.2 17.4 %kernel.5 = (f32[512,1024]{1,0:T(8,128)}, f32[512,1024]{1,0:T(8,128)}, bf16[512,2304]{1,0:T(8,128)(2,1)}, bf16[512,2304]{1,0:T(8,128)(2,1)}) custom-call(bf16[512,1024]{1,0:T(8,128)(2,1)} %get-tuple-element.110.refs_0_, bf16[1024,512]{1,0:T(8,128)(2,1)} %get-tuple-element.111.refs_1_, bf16[512,1024]{1,0:T(8,128)(2,1)} %get-tuple-element.112.refs_2_.refs_4_, ...), custom_call_target="tpu_custom_call" | custom-call | tf_op jit(solution)/shard_map/kernel/pallas_call | solution.py:524
  311.8 17.2 %kernel.6 = (f32[512,1024]{1,0:T(8,128)}, f32[512,1024]{1,0:T(8,128)}, bf16[512,2304]{1,0:T(8,128)(2,1)}, bf16[512,2304]{1,0:T(8,128)(2,1)}) custom-call(bf16[512,1024]{1,0:T(8,128)(2,1)} %get-tuple-element.110.refs_0_, bf16[1024,512]{1,0:T(8,128)(2,1)} %get-tuple-element.111.refs_1_, bf16[512,1024]{1,0:T(8,128)(2,1)} %get-tuple-element.112.refs_2_.refs_4_, ...), custom_call_target="tpu_custom_call" | custom-call | tf_op jit(solution)/shard_map/kernel/pallas_call | solution.py:524
  333.4 17.7 %kernel.7 = (f32[512,1024]{1,0:T(8,128)}, f32[512,1024]{1,0:T(8,128)}, bf16[512,2304]{1,0:T(8,128)(2,1)}, bf16[512,2304]{1,0:T(8,128)(2,1)}) custom-call(bf16[512,1024]{1,0:T(8,128)(2,1)} %get-tuple-element.110.refs_0_, bf16[1024,512]{1,0:T(8,128)(2,1)} %get-tuple-element.111.refs_1_, bf16[512,1024]{1,0:T(8,128)(2,1)} %get-tuple-element.112.refs_2_.refs_4_, ...), custom_call_target="tpu_custom_call" | custom-call | tf_op jit(solution)/shard_map/kernel/pallas_call | solution.py:524
  351.3 6.4 %collective-permute-done.45 = bf16[256,2304]{1,0:T(8,128)(2,1)} collective-permute-done((bf16[256,2304]{1,0:T(8,128)(2,1)}, bf16[256,2304]{1,0:T(8,128)(2,1)}, u32[]{:S(2)}, u32[]{:S(2)}) %collective-permute-start.45) | collective-permute-done | bytes 1179680 | tf_op jit(solution)/shard_map/ppermute | solution.py:536
  371.9 7.8 %collective-permute-done.50 = bf16[128,2304]{1,0:T(8,128)(2,1)S(1)} collective-permute-done((bf16[128,2304]{1,0:T(8,128)(2,1)S(1)}, bf16[128,2304]{1,0:T(8,128)(2,1)S(1)}, u32[]{:S(2)}, u32[]{:S(2)}) %collective-permute-start.50) | collective-permute-done | bytes 589856 | tf_op jit(solution)/shard_map/ppermute | solution.py:536
  380.9 11.6 %middle_kernel.1 = (bf16[512,1024]{1,0:T(8,128)(2,1)}, f32[512,1024]{1,0:T(8,128)}, bf16[512,1024]{1,0:T(8,128)(2,1)}, bf16[1024,512]{1,0:T(8,128)(2,1)}, f32[1,1024]{1,0:T(1,128)}) custom-call(s32[8]{0:T(128)} %broadcast_xor_fusion.refs_0_, f32[512,1024]{1,0:T(8,128)} %get-tuple-element.109.refs_0_.refs_1_, f32[512,1024]{1,0:T(8,128)} %get-tuple-element.124.refs_2_, ...), custom_call_target="tpu_custom_call" | custom-call | tf_op jit(solution)/shard_map/middle_kernel/pallas_call | solution.py:524
  394.1 18.5 %mix_back_kernel.2 = (f32[512,1024]{1,0:T(8,128)}, f32[512,768]{1,0:T(8,128)}, f32[512,768]{1,0:T(8,128)}, f32[8,768]{1,0:T(8,128)}, bf16[512,1536]{1,0:T(8,128)(2,1)}, /*index=5*/bf16[512,1536]{1,0:T(8,128)(2,1)}) custom-call(bf16[512,1024]{1,0:T(8,128)(2,1)} %get-tuple-element.129.refs_0_, bf16[1024,512]{1,0:T(8,128)(2,1)} %get-tuple-element.130.refs_1_, ...), custom_call_target="tpu_custom_call" | custom-call | tf_op jit(solution)/shard_map/mix_back_kernel/pallas_call | solution.py:524
  418.1 12.9 %collective-permute-done.55 = bf16[128,2304]{1,0:T(8,128)(2,1)S(1)} collective-permute-done((bf16[128,2304]{1,0:T(8,128)(2,1)S(1)}, bf16[128,2304]{1,0:T(8,128)(2,1)S(1)}, u32[]{:S(2)}, u32[]{:S(2)}) %collective-permute-start.55) | collective-permute-done | bytes 589856 | tf_op jit(solution)/shard_map/ppermute | solution.py:536
  436.9 35.9 %collective-permute-done.62.refs_8_ = bf16[128,2304]{1,0:T(8,128)(2,1)S(1)} collective-permute-done((bf16[128,2304]{1,0:T(8,128)(2,1)S(1)}, bf16[128,2304]{1,0:T(8,128)(2,1)S(1)}, u32[]{:S(2)}, u32[]{:S(2)}) %collective-permute-start.62) | collective-permute-done | bytes 589856 | tf_op jit(solution)/shard_map/ppermute | solution.py:539
  475.3 18.4 %mix_back_kernel.3 = (f32[512,1024]{1,0:T(8,128)}, f32[512,768]{1,0:T(8,128)}, f32[512,768]{1,0:T(8,128)}, f32[8,768]{1,0:T(8,128)}, bf16[512,1536]{1,0:T(8,128)(2,1)}, /*index=5*/bf16[512,1536]{1,0:T(8,128)(2,1)}) custom-call(bf16[512,1024]{1,0:T(8,128)(2,1)} %get-tuple-element.129.refs_0_, bf16[1024,512]{1,0:T(8,128)(2,1)} %get-tuple-element.130.refs_1_, ...), custom_call_target="tpu_custom_call" | custom-call | tf_op jit(solution)/shard_map/mix_back_kernel/pallas_call | solution.py:524
  497.9 10.8 %collective-permute-start.54 = (f32[2,1536]{1,0:T(2,128)S(1)}, f32[2,1536]{1,0:T(2,128)S(1)}, u32[]{:S(2)}, u32[]{:S(2)}) collective-permute-start(f32[2,1536]{1,0:T(2,128)S(1)} %maximum_maximum_fusion.1), channel_id=1, source_target_pairs={{0,1},{1,0},{2,3},{3,2},{4,5},{5,4},{6,7},{7,6},{8,9},{9,8},{10,11... | collective-permute-start | bytes 36872 | tf_op jit(solution)/shard_map/ppermute | solution.py:539
  514.1 10.7 %gate_back_kernel.3 = (f32[512,768]{1,0:T(8,128)}, f32[6,128,128]{2,1,0:T(8,128)}, f32[6,128,128]{2,1,0:T(8,128)}, f32[8,768]{1,0:T(8,128)}) custom-call(f32[512,768]{1,0:T(8,128)} %get-tuple-element.153.refs_0_, f32[512,768]{1,0:T(8,128)} %get-tuple-element.154.refs_1_, f32[1,768]{1,0:T(1,128)} %get-tuple-element.302.refs_2_, ...), custom_call_target="tpu_custom_call" | custom-call | tf_op jit(solution)/shard_map/gate_back_kernel/pallas_call | solution.py:524
  529.5 10.5 %gate_back_kernel.2 = (f32[512,768]{1,0:T(8,128)}, f32[6,128,128]{2,1,0:T(8,128)}, f32[6,128,128]{2,1,0:T(8,128)}, f32[8,768]{1,0:T(8,128)}) custom-call(f32[512,768]{1,0:T(8,128)} %get-tuple-element.143.refs_0_, f32[512,768]{1,0:T(8,128)} %get-tuple-element.144.refs_1_, f32[1,768]{1,0:T(1,128)} %get-tuple-element.303.refs_2_, ...), custom_call_target="tpu_custom_call" | custom-call | tf_op jit(solution)/shard_map/gate_back_kernel/pallas_call | solution.py:524
  550.7 7.5 %branch_back_kernel.2 = (f32[512,1024]{1,0:T(8,128)}, bf16[512,768]{1,0:T(8,128)(2,1)}, bf16[512,768]{1,0:T(8,128)(2,1)}) custom-call(f32[512,768]{1,0:T(8,128)} %get-tuple-element.160.refs_0_, f32[8,768]{1,0:T(8,128)} %pad_maximum_fusion.39.refs_1_, f32[8,768]{1,0:T(8,128)} %get-tuple-element.270.refs_5_.refs_9_.refs_10_.refs_2_, ...), custom_call_target="tpu_custom_call" | custom-call | tf_op jit(solution)/shard_map/branch_back_kernel/pallas_call | solution.py:524
  562.6 7.4 %branch_back_kernel.3 = (f32[512,1024]{1,0:T(8,128)}, bf16[512,768]{1,0:T(8,128)(2,1)}, bf16[512,768]{1,0:T(8,128)(2,1)}) custom-call(f32[512,768]{1,0:T(8,128)} %get-tuple-element.152.refs_0_, f32[8,768]{1,0:T(8,128)} %pad_maximum_fusion.38.refs_1_, f32[8,768]{1,0:T(8,128)} %get-tuple-element.271.refs_5_.refs_9_.refs_10_.refs_2_, ...), custom_call_target="tpu_custom_call" | custom-call | tf_op jit(solution)/shard_map/branch_back_kernel/pallas_call | solution.py:524
  570.1 10.3 %final_kernel.1 = (f32[512,1024]{1,0:T(8,128)}, f32[1,1024]{1,0:T(1,128)}) custom-call(s32[8]{0:T(128)} %broadcast_xor_fusion.refs_0_, bf16[512,1024]{1,0:T(8,128)(2,1)} %get-tuple-element.98.refs_1_, f32[512,1024]{1,0:T(8,128)} %get-tuple-element.163.refs_2_, f32[512,1024]{1,0:T(8,128)} %get-tuple-element.164.refs_3_, ...), custom_call_target="tpu_custom_call" | custom-call | tf_op jit(solution)/shard_map/final_kernel/pallas_call | solution.py:524
  588.0 8.1 %collective-permute-done.72 = bf16[256,768]{1,0:T(8,128)(2,1)S(1)} collective-permute-done((bf16[256,768]{1,0:T(8,128)(2,1)S(1)}, bf16[256,768]{1,0:T(8,128)(2,1)S(1)}, u32[]{:S(2)}, u32[]{:S(2)}) %collective-permute-start.72) | collective-permute-done | bytes 393248 | tf_op jit(solution)/shard_map/ppermute | solution.py:536
  627.6 4.0 collective-permute-done.77
  634.7 4.0 collective-permute-done.78
  (495 shorter events, 242.0 us)
Async XLA Ops:
  5.9 29.8 %collective-permute-start.1 = (bf16[128,128]{1,0:T(8,128)(2,1)S(1)}, bf16[128,128]{1,0:T(8,128)(2,1)S(1)}, u32[]{:S(2)}, u32[]{:S(2)}) collective-permute-start(bf16[128,128]{1,0:T(8,128)(2,1)S(1)} %concatenate.238), channel_id=1, source_target_pairs={{0,1},{1,0},{2,3},{3,2},{4,5},{5,4},{6,7},{7,6},{8,9},{9,8},{10,11... | collective-permute-start | bytes 98312 | tf_op jit(solution)/shard_map/ppermute | solution.py:539
  13.4 44.5 %collective-permute-start.7 = (bf16[128,768]{1,0:T(8,128)(2,1)S(1)}, bf16[128,768]{1,0:T(8,128)(2,1)S(1)}, u32[]{:S(2)}, u32[]{:S(2)}) collective-permute-start(bf16[128,768]{1,0:T(8,128)(2,1)S(1)} %constant_dynamic-update-slice_fusion), channel_id=1, source_target_pairs={{0,1},{1,0},{2,3},{3,2},{4,5},{5,4},{6,7},{7,6},{8,9},{9,8},{10,11... | collective-permute-start | bytes 589832 | tf_op jit(solution)/shard_map/ppermute | solution.py:539
  14.4 45.5 %collective-permute-start.8 = (bf16[128,768]{1,0:T(8,128)(2,1)S(1)}, bf16[128,768]{1,0:T(8,128)(2,1)S(1)}, u32[]{:S(2)}, u32[]{:S(2)}) collective-permute-start(bf16[128,768]{1,0:T(8,128)(2,1)S(1)} %constant_dynamic-update-slice_fusion), channel_id=1, source_target_pairs={{0,2},{1,3},{2,0},{3,1},{4,6},{5,7},{6,4},{7,5},{8,10},{9,11},{10,... | collective-permute-start | bytes 589832 | tf_op jit(solution)/shard_map/ppermute | solution.py:539
  56.0 42.0 %collective-permute-start.25 = (bf16[128,2304]{1,0:T(8,128)(2,1)S(1)}, bf16[128,2304]{1,0:T(8,128)(2,1)S(1)}, u32[]{:S(2)}, u32[]{:S(2)}) collective-permute-start(bf16[128,2304]{1,0:T(8,128)(2,1)S(1)} %constant_dynamic-update-slice_fusion.16), channel_id=1, source_target_pairs={{0,1},{1,0},{2,3},{3,2},{4,5},{5,4},{6,7},{7,6},{8,9},{9,8},{10,11... | collective-permute-start | bytes 1769480 | tf_op jit(solution)/shard_map/ppermute | solution.py:539
  73.0 37.0 %collective-permute-start.20 = (bf16[128,2304]{1,0:T(8,128)(2,1)S(1)}, bf16[128,2304]{1,0:T(8,128)(2,1)S(1)}, u32[]{:S(2)}, u32[]{:S(2)}) collective-permute-start(bf16[128,2304]{1,0:T(8,128)(2,1)S(1)} %constant_dynamic-update-slice_fusion.16), channel_id=1, source_target_pairs={{0,2},{1,3},{2,0},{3,1},{4,6},{5,7},{6,4},{7,5},{8,10},{9,11},{10,... | collective-permute-start | bytes 1769480 | tf_op jit(solution)/shard_map/ppermute | solution.py:539
  93.2 27.8 %collective-permute-start.32 = (bf16[128,2304]{1,0:T(8,128)(2,1)S(1)}, bf16[128,2304]{1,0:T(8,128)(2,1)S(1)}, u32[]{:S(2)}, u32[]{:S(2)}) collective-permute-start(bf16[128,2304]{1,0:T(8,128)(2,1)S(1)} %constant_dynamic-update-slice_fusion.16), channel_id=1, source_target_pairs={{0,3},{1,2},{2,1},{3,0},{4,7},{5,6},{6,5},{7,4},{8,11},{9,10},{10,... | collective-permute-start | bytes 1769480 | tf_op jit(solution)/shard_map/ppermute | solution.py:539
  98.0 69.1 %collective-permute-start.11 = (bf16[256,1536]{1,0:T(8,128)(2,1)}, bf16[256,1536]{1,0:T(8,128)(2,1)}, u32[]{:S(2)}, u32[]{:S(2)}) collective-permute-start(bf16[256,1536]{1,0:T(8,128)(2,1)} %pad_maximum_fusion.11), channel_id=1, source_target_pairs={{0,8},{4,12},{8,0},{12,4},{16,24},{20,28},{24,16},{28,20},{1,9},{5... | collective-permute-start | bytes 2359304 | tf_op jit(solution)/shard_map/ppermute | solution.py:536
  105.1 63.8 %collective-permute-start.19 = (bf16[256,1536]{1,0:T(8,128)(2,1)}, bf16[256,1536]{1,0:T(8,128)(2,1)}, u32[]{:S(2)}, u32[]{:S(2)}) collective-permute-start(bf16[256,1536]{1,0:T(8,128)(2,1)} %pad_maximum_fusion.13), channel_id=1, source_target_pairs={{0,16},{4,20},{8,24},{12,28},{16,0},{20,4},{24,8},{28,12},{1,17},{... | collective-permute-start | bytes 2359304 | tf_op jit(solution)/shard_map/ppermute | solution.py:536
  121.0 111.7 %collective-permute-start.33 = (bf16[256,2304]{1,0:T(8,128)(2,1)}, bf16[256,2304]{1,0:T(8,128)(2,1)}, u32[]{:S(2)}, u32[]{:S(2)}) collective-permute-start(bf16[256,2304]{1,0:T(8,128)(2,1)} %pad_maximum_fusion.5), channel_id=1, source_target_pairs={{0,16},{4,20},{8,24},{12,28},{16,0},{20,4},{24,8},{28,12},{1,17},{... | collective-permute-start | bytes 3538952 | tf_op jit(solution)/shard_map/ppermute | solution.py:536
  122.6 43.3 %collective-permute-start.35 = (bf16[128,2304]{1,0:T(8,128)(2,1)S(1)}, bf16[128,2304]{1,0:T(8,128)(2,1)S(1)}, u32[]{:S(2)}, u32[]{:S(2)}) collective-permute-start(bf16[128,2304]{1,0:T(8,128)(2,1)S(1)} %collective-permute-done.32.refs_9_), channel_id=1, source_target_pairs={{0,16},{4,20},{8,24},{12,28},{16,0},{20,4},{24,8},{28,12},{1,17},{... | collective-permute-start | bytes 1769480 | tf_op jit(solution)/shard_map/ppermute | solution.py:536
  127.1 44.8 %collective-permute-start.24 = (bf16[512,768]{1,0:T(8,128)(2,1)S(1)}, bf16[512,768]{1,0:T(8,128)(2,1)S(1)}, u32[]{:S(2)}, u32[]{:S(2)}) collective-permute-start(bf16[512,768]{1,0:T(8,128)(2,1)S(1)} %pad_maximum_fusion.14.refs_1_.refs_4_), channel_id=1, source_target_pairs={{0,4},{4,0},{8,12},{12,8},{16,20},{20,16},{24,28},{28,24},{1,5},{5... | collective-permute-start | bytes 2359304 | tf_op jit(solution)/shard_map/ppermute | solution.py:536
  167.1 67.6 %collective-permute-start.34 = (bf16[256,2304]{1,0:T(8,128)(2,1)}, bf16[256,2304]{1,0:T(8,128)(2,1)S(1)}, u32[]{:S(2)}, u32[]{:S(2)}) collective-permute-start(bf16[256,2304]{1,0:T(8,128)(2,1)} %pad_maximum_fusion.6), channel_id=1, source_target_pairs={{0,8},{4,12},{8,0},{12,4},{16,24},{20,28},{24,16},{28,20},{1,9},{5... | collective-permute-start | bytes 3538952 | tf_op jit(solution)/shard_map/ppermute | solution.py:536
  169.0 113.4 %collective-permute-start.39 = (bf16[256,2304]{1,0:T(8,128)(2,1)}, bf16[256,2304]{1,0:T(8,128)(2,1)}, u32[]{:S(2)}, u32[]{:S(2)}) collective-permute-start(bf16[256,2304]{1,0:T(8,128)(2,1)} %pad_maximum_fusion.8), channel_id=1, source_target_pairs={{0,16},{4,20},{8,24},{12,28},{16,0},{20,4},{24,8},{28,12},{1,17},{... | collective-permute-start | bytes 3538952 | tf_op jit(solution)/shard_map/ppermute | solution.py:536
  172.8 65.0 %collective-permute-start.29 = (bf16[512,1536]{1,0:T(8,128)(2,1)S(1)}, bf16[512,1536]{1,0:T(8,128)(2,1)}, u32[]{:S(2)}, u32[]{:S(2)}) collective-permute-start(bf16[512,1536]{1,0:T(8,128)(2,1)S(1)} %pad_maximum_fusion.4.refs_1_.refs_3_), channel_id=1, source_target_pairs={{0,4},{4,0},{8,12},{12,8},{16,20},{20,16},{24,28},{28,24},{1,5},{5... | collective-permute-start | bytes 4718600 | tf_op jit(solution)/shard_map/ppermute | solution.py:536
  234.2 30.3 %collective-permute-start.42 = (bf16[512,2304]{1,0:T(8,128)(2,1)S(1)}, bf16[512,2304]{1,0:T(8,128)(2,1)}, u32[]{:S(2)}, u32[]{:S(2)}) collective-permute-start(bf16[512,2304]{1,0:T(8,128)(2,1)S(1)} %pad_maximum_fusion.2.refs_4_), channel_id=1, source_target_pairs={{0,4},{4,0},{8,12},{12,8},{16,20},{20,16},{24,28},{28,24},{1,5},{5... | collective-permute-start | bytes 7077896 | tf_op jit(solution)/shard_map/ppermute | solution.py:536
  236.4 48.8 %collective-permute-start.41 = (bf16[512,2304]{1,0:T(8,128)(2,1)S(1)}, bf16[512,2304]{1,0:T(8,128)(2,1)}, u32[]{:S(2)}, u32[]{:S(2)}) collective-permute-start(bf16[512,2304]{1,0:T(8,128)(2,1)S(1)} %pad_maximum_fusion.1.refs_4_), channel_id=1, source_target_pairs={{0,4},{4,0},{8,12},{12,8},{16,20},{20,16},{24,28},{28,24},{1,5},{5... | collective-permute-start | bytes 7077896 | tf_op jit(solution)/shard_map/ppermute | solution.py:536
  237.8 65.0 %collective-permute-start.36 = (bf16[256,2304]{1,0:T(8,128)(2,1)}, bf16[256,2304]{1,0:T(8,128)(2,1)}, u32[]{:S(2)}, u32[]{:S(2)}) collective-permute-start(bf16[256,2304]{1,0:T(8,128)(2,1)} %pad_maximum_fusion.7), channel_id=1, source_target_pairs={{0,8},{4,12},{8,0},{12,4},{16,24},{20,28},{24,16},{28,20},{1,9},{5... | collective-permute-start | bytes 3538952 | tf_op jit(solution)/shard_map/ppermute | solution.py:536
  302.7 27.2 %collective-permute-start.44 = (bf16[512,2304]{1,0:T(8,128)(2,1)}, bf16[512,2304]{1,0:T(8,128)(2,1)S(1)}, u32[]{:S(2)}, u32[]{:S(2)}) collective-permute-start(bf16[512,2304]{1,0:T(8,128)(2,1)} %get-tuple-element.123), channel_id=1, source_target_pairs={{0,4},{4,0},{8,12},{12,8},{16,20},{20,16},{24,28},{28,24},{1,5},{5... | collective-permute-start | bytes 7077896 | tf_op jit(solution)/shard_map/ppermute | solution.py:536
  305.8 27.7 %collective-permute-start.37 = (bf16[512,2304]{1,0:T(8,128)(2,1)}, bf16[512,2304]{1,0:T(8,128)(2,1)}, u32[]{:S(2)}, u32[]{:S(2)}) collective-permute-start(bf16[512,2304]{1,0:T(8,128)(2,1)} %pad_maximum_fusion.refs_4_), channel_id=1, source_target_pairs={{0,4},{4,0},{8,12},{12,8},{16,20},{20,16},{24,28},{28,24},{1,5},{5... | collective-permute-start | bytes 7077896 | tf_op jit(solution)/shard_map/ppermute | solution.py:536
  329.0 35.0 %collective-permute-start.46 = (bf16[512,2304]{1,0:T(8,128)(2,1)}, bf16[512,2304]{1,0:T(8,128)(2,1)}, u32[]{:S(2)}, u32[]{:S(2)}) collective-permute-start(bf16[512,2304]{1,0:T(8,128)(2,1)} %get-tuple-element.127), channel_id=1, source_target_pairs={{0,4},{4,0},{8,12},{12,8},{16,20},{20,16},{24,28},{28,24},{1,5},{5... | collective-permute-start | bytes 7077896 | tf_op jit(solution)/shard_map/ppermute | solution.py:536
  329.3 28.4 %collective-permute-start.45 = (bf16[256,2304]{1,0:T(8,128)(2,1)}, bf16[256,2304]{1,0:T(8,128)(2,1)}, u32[]{:S(2)}, u32[]{:S(2)}) collective-permute-start(bf16[256,2304]{1,0:T(8,128)(2,1)} %slice.851), channel_id=1, source_target_pairs={{0,16},{4,20},{8,24},{12,28},{16,0},{20,4},{24,8},{28,12},{1,17},{... | collective-permute-start | bytes 3538952 | tf_op jit(solution)/shard_map/ppermute | solution.py:536
  331.9 29.8 %collective-permute-start.47 = (bf16[256,2304]{1,0:T(8,128)(2,1)S(1)}, bf16[256,2304]{1,0:T(8,128)(2,1)}, u32[]{:S(2)}, u32[]{:S(2)}) collective-permute-start(bf16[256,2304]{1,0:T(8,128)(2,1)S(1)} %pad_maximum_fusion.9), channel_id=1, source_target_pairs={{0,8},{4,12},{8,0},{12,4},{16,24},{20,28},{24,16},{28,20},{1,9},{5... | collective-permute-start | bytes 3538952 | tf_op jit(solution)/shard_map/ppermute | solution.py:536
  360.2 76.7 %collective-permute-start.49 = (bf16[128,2304]{1,0:T(8,128)(2,1)}, bf16[128,2304]{1,0:T(8,128)(2,1)}, u32[]{:S(2)}, u32[]{:S(2)}) collective-permute-start(bf16[128,2304]{1,0:T(8,128)(2,1)} %slice.857), channel_id=1, source_target_pairs={{0,8},{4,12},{8,0},{12,4},{16,24},{20,28},{24,16},{28,20},{1,9},{5... | collective-permute-start | bytes 1769480 | tf_op jit(solution)/shard_map/ppermute | solution.py:536
  367.3 46.2 %collective-permute-start.51 = (bf16[256,2304]{1,0:T(8,128)(2,1)}, bf16[256,2304]{1,0:T(8,128)(2,1)}, u32[]{:S(2)}, u32[]{:S(2)}) collective-permute-start(bf16[256,2304]{1,0:T(8,128)(2,1)} %slice.861), channel_id=1, source_target_pairs={{0,16},{4,20},{8,24},{12,28},{16,0},{20,4},{24,8},{28,12},{1,17},{... | collective-permute-start | bytes 3538952 | tf_op jit(solution)/shard_map/ppermute | solution.py:536
  371.2 44.6 %collective-permute-start.57 = (bf16[256,2304]{1,0:T(8,128)(2,1)S(1)}, bf16[256,2304]{1,0:T(8,128)(2,1)}, u32[]{:S(2)}, u32[]{:S(2)}) collective-permute-start(bf16[256,2304]{1,0:T(8,128)(2,1)S(1)} %pad_maximum_fusion.10), channel_id=1, source_target_pairs={{0,8},{4,12},{8,0},{12,4},{16,24},{20,28},{24,16},{28,20},{1,9},{5... | collective-permute-start | bytes 3538952 | tf_op jit(solution)/shard_map/ppermute | solution.py:536
  379.9 57.0 %collective-permute-start.58 = (bf16[128,2304]{1,0:T(8,128)(2,1)S(1)}, bf16[128,2304]{1,0:T(8,128)(2,1)S(1)}, u32[]{:S(2)}, u32[]{:S(2)}) collective-permute-start(bf16[128,2304]{1,0:T(8,128)(2,1)S(1)} %add_convert_fusion.16.refs_12_), channel_id=1, source_target_pairs={{0,1},{1,0},{2,3},{3,2},{4,5},{5,4},{6,7},{7,6},{8,9},{9,8},{10,11... | collective-permute-start | bytes 1769480 | tf_op jit(solution)/shard_map/ppermute | solution.py:539
  431.1 41.7 %collective-permute-start.62 = (bf16[128,2304]{1,0:T(8,128)(2,1)S(1)}, bf16[128,2304]{1,0:T(8,128)(2,1)S(1)}, u32[]{:S(2)}, u32[]{:S(2)}) collective-permute-start(bf16[128,2304]{1,0:T(8,128)(2,1)S(1)} %add_convert_fusion.15.refs_11_), channel_id=1, source_target_pairs={{0,2},{1,3},{2,0},{3,1},{4,6},{5,7},{6,4},{7,5},{8,10},{9,11},{10,... | collective-permute-start | bytes 1769480 | tf_op jit(solution)/shard_map/ppermute | solution.py:539
  434.3 38.5 %collective-permute-start.85 = (bf16[128,2304]{1,0:T(8,128)(2,1)S(1)}, bf16[128,2304]{1,0:T(8,128)(2,1)S(1)}, u32[]{:S(2)}, u32[]{:S(2)}) collective-permute-start(bf16[128,2304]{1,0:T(8,128)(2,1)S(1)} %add_convert_fusion.14.refs_7_), channel_id=1, source_target_pairs={{0,3},{1,2},{2,1},{3,0},{4,7},{5,6},{6,5},{7,4},{8,11},{9,10},{10,... | collective-permute-start | bytes 1769480 | tf_op jit(solution)/shard_map/ppermute | solution.py:539
  436.2 72.6 %collective-permute-start.63 = (bf16[256,1536]{1,0:T(8,128)(2,1)S(1)}, bf16[256,1536]{1,0:T(8,128)(2,1)}, u32[]{:S(2)}, u32[]{:S(2)}) collective-permute-start(bf16[256,1536]{1,0:T(8,128)(2,1)S(1)} %slice.893), channel_id=1, source_target_pairs={{0,16},{4,20},{8,24},{12,28},{16,0},{20,4},{24,8},{28,12},{1,17},{... | collective-permute-start | bytes 2359304 | tf_op jit(solution)/shard_map/ppermute | solution.py:536
  525.9 74.4 %collective-permute-start.81 = (bf16[128,768]{1,0:T(8,128)(2,1)S(1)}, bf16[128,768]{1,0:T(8,128)(2,1)S(1)}, u32[]{:S(2)}, u32[]{:S(2)}) collective-permute-start(bf16[128,768]{1,0:T(8,128)(2,1)S(1)} %fusion.9), channel_id=1, source_target_pairs={{0,1},{1,0},{2,3},{3,2},{4,5},{5,4},{6,7},{7,6},{8,9},{9,8},{10,11... | collective-permute-start | bytes 589832 | tf_op jit(solution)/shard_map/ppermute | solution.py:539
  570.0 39.8 %collective-permute-start.75 = (bf16[512,768]{1,0:T(8,128)(2,1)}, bf16[512,768]{1,0:T(8,128)(2,1)S(1)}, u32[]{:S(2)}, u32[]{:S(2)}) collective-permute-start(bf16[512,768]{1,0:T(8,128)(2,1)} %get-tuple-element.179), channel_id=1, source_target_pairs={{0,4},{4,0},{8,12},{12,8},{16,20},{20,16},{24,28},{28,24},{1,5},{5... | collective-permute-start | bytes 2359304 | tf_op jit(solution)/shard_map/ppermute | solution.py:536
  604.9 29.8 %collective-permute-start.74 = (bf16[128,384]{1,0:T(8,128)(2,1)S(1)}, bf16[128,384]{1,0:T(8,128)(2,1)S(1)}, u32[]{:S(2)}, u32[]{:S(2)}) collective-permute-start(bf16[128,384]{1,0:T(8,128)(2,1)S(1)} %slice.914), channel_id=1, source_target_pairs={{0,1},{1,0},{2,3},{3,2},{4,5},{5,4},{6,7},{7,6},{8,9},{9,8},{10,11... | collective-permute-start | bytes 294920 | tf_op jit(solution)/shard_map/ppermute | solution.py:539
  (131 other events, 2062.3 us)

commit v3 on v2

--- a/solution.py
+++ b/solution.py
@@ -153,12 +153,13 @@
 
 
 def mlp_kernel(
-    normed_ref, normed_t_ref, cot_ref, cot_t_ref, low_ref, high_ref, sum_ref, back_ref,
+    chunks_ref, normed_ref, normed_t_ref, cot_ref, cot_t_ref, weights_ref, sum_ref, back_ref,
     total_ref, grad_ref, low_grad_ref, high_grad_ref,
-    pre, hidden, pre_low, act, first=False,
+    pre, hidden, pre_low, act,
 ):
-    length = normed_ref.shape[0]
-    half = low_ref.shape[0]
+    length, model = normed_ref.shape
+    half = model // 2
+    first = sum_ref is None
 
     @pl.when(pl.program_id(0) == 0)
     def _():
@@ -169,8 +170,9 @@
             total_ref[...] = sum_ref[...]
             grad_ref[...] = back_ref[...]
 
-    pre[...] = nn(normed_ref[:, :half], low_ref[:, : 2 * GROUP]) + nn(normed_ref[:, half:], high_ref[:, : 2 * GROUP])
-    act[...] = nn(cot_ref[:, :half], low_ref[:, 2 * GROUP :]) + nn(cot_ref[:, half:], high_ref[:, 2 * GROUP :])
+    weights = weights_ref[...].reshape(model, 3 * GROUP)
+    pre[...] = nn(normed_ref[...], weights[:, : 2 * GROUP])
+    act[...] = nn(cot_ref[...], weights[:, 2 * GROUP :])
     for part in range(GROUP // BLOCK):
         lanes = slice(part * BLOCK, (part + 1) * BLOCK)
         up_lanes = slice(GROUP + part * BLOCK, GROUP + (part + 1) * BLOCK)
@@ -185,10 +187,8 @@
             pre_low[rows, up_lanes] = (grad * value).astype(bf16)
 
         tiles(length, activate)
-    total_ref[:, :half] += nt(hidden[...], low_ref[:, 2 * GROUP :])
-    total_ref[:, half:] += nt(hidden[...], high_ref[:, 2 * GROUP :])
-    grad_ref[:, :half] += nt(pre_low[...], low_ref[:, : 2 * GROUP])
-    grad_ref[:, half:] += nt(pre_low[...], high_ref[:, : 2 * GROUP])
+    total_ref[...] += nt(hidden[...], weights[:, 2 * GROUP :])
+    grad_ref[...] += nt(pre_low[...], weights[:, : 2 * GROUP])
     low_grad_ref[:, : 2 * GROUP] = nn(normed_t_ref[:half], pre_low[...]).astype(bf16)
     high_grad_ref[:, : 2 * GROUP] = nn(normed_t_ref[half:], pre_low[...]).astype(bf16)
     low_grad_ref[:, 2 * GROUP :] = nn(cot_t_ref[:half], hidden[...]).astype(bf16)
@@ -235,14 +235,18 @@
     normed_t_ref[...] = normed_ref[HALO:, :].T
 
 
-def second_norm_kernel(middle_ref, gains_ref, normed_ref, normed_t_ref):
+def second_norm_kernel(places_ref, middle_ref, gains_ref, normed_ref, normed_t_ref, buffer):
+    length, model = middle_ref.shape
+
     def body(rows, carry):
         values = middle_ref[rows, :]
-        normed_ref[rows, :] = (values * scale_of(values) * gains_ref[1:2, :]).astype(bf16)
+        buffer[rows, :] = (values * scale_of(values) * gains_ref[1:2, :]).astype(bf16)
         return carry
 
-    row_loop(middle_ref.shape[0], 16, body, 0)
-    normed_t_ref[...] = normed_ref[...].T
+    row_loop(length, 16, body, 0)
+    normed_t_ref[...] = buffer[...].T
+    for place in range(model // BLOCK):
+        normed_ref[:, lane_block(places_ref[place])] = buffer[:, place * BLOCK : (place + 1) * BLOCK]
 
 
 def norm_back(values, grad, gain):
@@ -259,17 +263,21 @@
 
 def middle_kernel(
     places_ref, middle_ref, total_ref, grad_ref, cot_ref, gains_ref,
-    out_ref, middle_grad_ref, low_ref, low_t_ref, gain_ref, buffer,
+    out_ref, middle_grad_ref, low_ref, low_t_ref, gain_ref, buffer, own_total, own_grad,
 ):
     length, model = middle_ref.shape
+    for place in range(model // BLOCK):
+        lanes = slice(place * BLOCK, (place + 1) * BLOCK)
+        own_total[:, lanes] = total_ref[:, lane_block(places_ref[place])]
+        own_grad[:, lanes] = grad_ref[:, lane_block(places_ref[place])]
 
     def body(rows, carry):
         middle = middle_ref[rows, :]
-        change, part = norm_back(middle, grad_ref[rows, :], gains_ref[1:2, :])
+        change, part = norm_back(middle, own_grad[rows, :], gains_ref[1:2, :])
         middle_grad = cot_ref[rows, :].astype(f32) + change
         middle_grad_ref[rows, :] = middle_grad
         low_ref[rows, :] = middle_grad.astype(bf16)
-        buffer[rows, :] = (middle + total_ref[rows, :]).astype(bf16)
+        buffer[rows, :] = (middle + own_total[rows, :]).astype(bf16)
         return carry + fold_rows(part)
 
     total = row_loop(length, 16, body, jnp.zeros((8, model), f32))
@@ -320,12 +328,12 @@
                 table_ref[kind : kind + 1, column : column + BLOCK] = sums[at][row : row + 1]
 
 
-def small_grads_kernel(places_ref, rgrad_ref, igrad_ref, sums_ref, gains_ref, low_ref, high_ref, *, sub, local_blocks, chunks):
+def small_grads_kernel(places_ref, rgrad_ref, igrad_ref, sums_ref, low_ref, high_ref, *, sub, local_blocks, chunks):
     kinds = 2 * CONV
     rows_each = 2 * local_blocks * sub
     count = places_ref.shape[0]
     size = low_ref.shape[0] * 2 // count
-    spare = size - rows_each - kinds * local_blocks - 2
+    spare = size - rows_each - kinds * local_blocks
     vectors = []
     for at in range(chunks):
         rows = []
@@ -338,7 +346,6 @@
         target = low_ref if place < count // 2 else high_ref
         top = (place % (count // 2)) * size
         natural = places_ref[place]
-        gains = gains_ref[:, place * BLOCK : (place + 1) * BLOCK]
         for at in range(chunks):
             lanes = slice(at * BLOCK, (at + 1) * BLOCK)
             for which, grad_ref in enumerate((rgrad_ref, igrad_ref)):
@@ -347,7 +354,7 @@
                     target[start : start + sub, lanes] = grad_ref[
                         at * local_blocks + block, pl.ds(pl.multiple_of(natural * sub, sub), sub), :
                     ].astype(bf16)
-            rest = jnp.concatenate([vectors[at], gains, jnp.zeros((spare, BLOCK), f32)], axis=0)
+            rest = jnp.concatenate([vectors[at], jnp.zeros((spare, BLOCK), f32)], axis=0)
             target[top + rows_each : top + size, lanes] = rest.astype(bf16)
 
 
@@ -482,6 +489,18 @@
     high_grad_ref[...] = nn(normed_t_ref[half:], branch_low[...]).astype(bf16)
 
 
+def join_kernel(*refs, columns):
+    parts, outs = refs[: -len(columns)], refs[-len(columns) :]
+    for out_ref, places in zip(outs, columns):
+        to = 0
+        for start, size in places:
+            total = parts[0][:, start : start + size].astype(f32)
+            for part in parts[1:]:
+                total = total + part[:, start : start + size].astype(f32)
+            out_ref[:, to : to + size] = total
+            to += size
+
+
 def fixed(shape):
     return pl.BlockSpec(shape, lambda g: (0,) * len(shape))
 
@@ -505,8 +524,16 @@
 SCALARS = pl.BlockSpec(memory_space=pltpu.SMEM)
 
 
+SPANS = {
+    "order_kernel": 4, "tables_of": 2, "norm_kernel": 6, "mix_in_kernel": 14, "mix_out_kernel": 10,
+    "second_norm_kernel": 6, "mlp_kernel": 17, "middle_kernel": 12, "mix_back_kernel": 18, "gate_back_kernel": 11,
+    "branch_back_kernel": 8, "final_kernel": 10, "small_grads": 3, "join": 2,
+}
+
+
 def call(kernel, steps, in_specs, out_specs, out_shape, scratch, hold=()):
     count = len(in_specs)
+    name = getattr(kernel, "func", kernel).__name__
 
     def body(*refs):
         kernel(*refs[:count], *refs[count + len(hold) :])
@@ -519,7 +546,8 @@
         out_shape=out_shape,
         scratch_shapes=scratch,
         compiler_params=PARAMS,
-        name=getattr(kernel, "func", kernel).__name__,
+        name=name,
+        cost_estimate=pl.CostEstimate(flops=SPANS[name] * 1150 * 10**6, bytes_accessed=0, transcendentals=0),
     )
     return lambda *args: run(*args, *hold)
 
@@ -573,7 +601,7 @@
         return values, last, marks + [last]
 
     def add(one, two):
-        return (one.astype(f32) + two.astype(f32)).astype(bf16)
+        return (one.astype(f32) + two.astype(f32)).astype(one.dtype)
 
     def scatter_dp(own, other, order, block_rows):
         values = add(own, swap_dp(other, order[-1]))
@@ -597,6 +625,20 @@
 
     def spread_tensor(values):
         return [values] + [swap_tensor(values, other) for other in range(1, tensor_size)]
+
+    def join_parts(own, others, columns, hold):
+        received = {other: swap_tensor(part, other) for other, part in others.items()}
+        parts = [own] + [received[other] for other in range(1, tensor_size)]
+
+        def join(*refs):
+            join_kernel(*refs, columns=columns)
+
+        rows = own.shape[0]
+        widths = [sum(size for _, size in places) for places in columns]
+        return call(
+            join, 1, [fixed(own.shape)] * tensor_size, [fixed((rows, width)) for width in widths],
+            [shaped(rows, width) for width in widths], [], hold=hold,
+        )(*parts)
 
     def join_tensor(parts):
         total = parts[0].astype(f32)
@@ -684,8 +726,8 @@
         mlp_pieces = []
         for at in range(mlp_groups):
             mlp_pieces += [w[:, at * GROUP : (at + 1) * GROUP] for w in (mlp_gate, mlp_up, mlp_down)]
-        mlp_near = spread_tensor(jnp.concatenate(mlp_pieces, axis=1))
-        mlp_chunks = [gather_dp(values, orders[at % 2]) for at, values in enumerate(mlp_near)]
+        mlp_weights = lax.all_gather(jnp.concatenate(mlp_pieces, axis=1), ("dp", "tensor"), axis=0, tiled=False)
+        mlp_weights = mlp_weights.reshape(dp_size, tensor_size, block_rows, 3 * hidden_chunk)
 
         whole = fixed((length, model))
         turned = fixed((model, length))
@@ -728,8 +770,8 @@
 
         fed = []
         fed_holds = [
-            [out_pairs[0][2][0], out_pairs[1][2][0], mlp_near[1]],
-            [out_pairs[0][2][1], out_pairs[1][2][1], mlp_near[2]],
+            [out_pairs[0][2][0], out_pairs[1][2][0]],
+            [out_pairs[0][2][1], out_pairs[1][2][1]],
         ]
         for pair in range(pairs):
             low, high, _ = in_pairs[pair]
@@ -768,10 +810,6 @@
         )
         middle = hidden_low.astype(f32)
         mixed = []
-        mixed_holds = [
-            [mlp_chunks[0][2][0], mlp_chunks[1][2][0], mlp_near[3]],
-            [mlp_chunks[0][2][1], mlp_chunks[1][2][1]],
-        ]
         for pair in range(pairs):
             low, high, _ = out_pairs[pair]
             lanes = slice(pair * pair_width, (pair + 1) * pair_width)
@@ -782,70 +820,68 @@
                 [lanes_of(length), lanes_of(length + 8), lanes_of(length), whole],
                 [shaped(length, pair_width), shaped(length + 8, pair_width), shaped(length, pair_width, kind=bf16), shaped(length, model)],
                 [],
-                hold=mixed_holds[pair],
             )(normed_one, low, high, fed[pair][4], fed[pair][5], enter[:, lanes], middle)
             mixed.append((gate_pre, states, mixed_low))
         normed_two, normed_two_t = call(
-            second_norm_kernel, 1, [whole, fixed((2, model))], [whole, turned],
-            [shaped(length, model, kind=bf16), shaped(model, length, kind=bf16)], [],
-        )(middle, gains)
-
-        total = normed_grad = None
+            second_norm_kernel, 1, [SCALARS, whole, fixed((2, model))], [whole, turned],
+            [shaped(length, model, kind=bf16), shaped(model, length, kind=bf16)], [pltpu.VMEM((length, model), bf16)],
+        )(places, middle, gains)
+        normed_two = features(normed_two, True)
+
+        chunk_at = jnp.arange(tensor_size, dtype=jnp.int32) ^ tensor_at
+        before = []
         moved = []
-        sums = []
-        for at, (low, high, _) in enumerate(mlp_chunks):
-            holds = [
-                [mlp_chunks[2][2][0], mlp_chunks[3][2][0]],
-                [mlp_chunks[2][2][1]],
-                [lambda: moved[0][1][0]],
-                [lambda: moved[1][1][0]],
-            ][at]
-            holds = [hold() if callable(hold) else hold for hold in holds]
-            before = [] if at == 0 else [total, normed_grad]
-            width = 3 * GROUP
-
-            def kernel(*refs, at=at):
-                if at == 0:
-                    mlp_kernel(*refs[:6], None, None, *refs[6:], first=True)
-                else:
-                    mlp_kernel(*refs)
-
-            total, normed_grad, low_grad, high_grad = call(
+        width = 3 * GROUP
+        whole_at = pl.BlockSpec((length, model), lambda g, chunks: (0, 0))
+        turned_at = pl.BlockSpec((model, length), lambda g, chunks: (0, 0))
+        half_at = pl.BlockSpec((half, width), lambda g, chunks: (0, g))
+        for at in reversed(range(tensor_size)):
+            hold = [moved[-2][1][0]] if len(moved) >= 2 else []
+
+            def kernel(*refs, count=len(before), held=len(hold)):
+                sums = refs[6 : 6 + count] if count else (None, None)
+                mlp_kernel(*refs[:6], *sums, *refs[6 + count + held :])
+
+            total, normed_grad, low_grad, high_grad = pl.pallas_call(
                 kernel,
-                mlp_groups,
-                [whole, turned, whole, turned, lanes_of(half, width), lanes_of(half, width)] + [whole] * len(before),
-                [whole, whole, lanes_of(half, width), lanes_of(half, width)],
-                [shaped(length, model), shaped(length, model), shaped(half, 3 * hidden_chunk, kind=bf16), shaped(half, 3 * hidden_chunk, kind=bf16)],
-                [pltpu.VMEM((length, 2 * GROUP), f32), pltpu.VMEM((length, GROUP), bf16), pltpu.VMEM((length, 2 * GROUP), bf16), pltpu.VMEM((length, GROUP), f32)],
-                hold=holds,
-            )(normed_two, normed_two_t, cot_low, cot_t, low, high, *before)
+                grid_spec=pltpu.PrefetchScalarGridSpec(
+                    num_scalar_prefetch=1,
+                    grid=(mlp_groups,),
+                    in_specs=[
+                        whole_at, turned_at, whole_at, turned_at,
+                        pl.BlockSpec((dp_size, 1, block_rows, width), lambda g, chunks, at=at: (0, chunks[at], 0, g)),
+                    ] + [whole_at] * len(before) + [ANYWHERE] * len(hold),
+                    out_specs=[whole_at, whole_at, half_at, half_at],
+                    scratch_shapes=[
+                        pltpu.VMEM((length, 2 * GROUP), f32), pltpu.VMEM((length, GROUP), bf16),
+                        pltpu.VMEM((length, 2 * GROUP), bf16), pltpu.VMEM((length, GROUP), f32),
+                    ],
+                ),
+                out_shape=[shaped(length, model), shaped(length, model)] + [shaped(half, 3 * hidden_chunk, kind=bf16)] * 2,
+                compiler_params=PARAMS,
+                name="mlp_kernel",
+                cost_estimate=pl.CostEstimate(flops=SPANS["mlp_kernel"] * 1150 * 10**6, bytes_accessed=0, transcendentals=0),
+            )(chunk_at, normed_two, normed_two_t, cotangent, cot_t, mlp_weights, *before, *hold)
+            before = [total, normed_grad]
             moved.append(scatter_dp(low_grad, high_grad, orders[at % 2], block_rows))
-        mlp_sum, mlp_far = join_tensor([one[0] for one in moved])
-        mlp_grads = [
-            jnp.concatenate(
-                [mlp_sum[:, (3 * at + which) * GROUP : (3 * at + which + 1) * GROUP] for at in range(mlp_groups)], axis=1
-            )
-            for which in range(3)
-        ]
-
         hidden_out, middle_grad, middle_low, middle_low_t, gain_two = call(
             middle_kernel, 1, [SCALARS, whole, whole, whole, whole, fixed((2, model))],
             [whole, whole, whole, turned, fixed((1, model))],
             [shaped(length, model, kind=bf16), shaped(length, model), shaped(length, model, kind=bf16), shaped(model, length, kind=bf16), shaped(1, model)],
-            [pltpu.VMEM((length, model), bf16)],
-            hold=[moved[0][1][1], moved[2][1][0]],
-        )(places, middle, total, normed_grad, cot_low, gains)
+            [pltpu.VMEM((length, model), bf16), pltpu.VMEM((length, model), f32), pltpu.VMEM((length, model), f32)],
+            hold=[moved[2][1][0], moved[0][1][1]],
+        )(places, middle, features(total), features(normed_grad), cot_low, gains)
         hidden_out = features(hidden_out, True)
 
         normed_grad = jnp.zeros((length, model), f32)
-        backs = []
-        out_grads = []
-        out_moved = []
+        backs = {}
+        out_moved = {}
         back_holds = [
-            [moved[1][1][1], moved[3][1][0]],
-            [moved[0][1][2], moved[1][1][2], moved[2][1][1]],
+            [moved[3][1][0], moved[1][1][1]],
+            [moved[2][1][1], moved[0][1][2]],
         ]
-        for pair in range(pairs):
+        backward = list(reversed(range(pairs)))
+        for step, pair in enumerate(backward):
             low, high, _ = out_pairs[pair]
             gate_pre, states, mixed_low = mixed[pair]
             lanes = slice(pair * pair_width, (pair + 1) * pair_width)
@@ -856,10 +892,10 @@
                 [whole, lanes_of(length), lanes_of(length), lanes_of(8), lanes_of(half, 2 * GROUP), lanes_of(half, 2 * GROUP)],
                 [shaped(length, model), shaped(length, pair_width), shaped(length, pair_width), shaped(8, pair_width), shaped(half, 2 * pair_width, kind=bf16), shaped(half, 2 * pair_width, kind=bf16)],
                 [pltpu.VMEM((length, GROUP), f32), pltpu.VMEM((length, GROUP), f32), pltpu.VMEM((length, GROUP), bf16), pltpu.VMEM((length + 8, GROUP), f32)],
-                hold=back_holds[pair],
+                hold=back_holds[step],
             )(middle_low, middle_low_t, normed_one_t, low, high, gate_pre, states, mixed_low, fed[pair][2], table[:, lanes], normed_grad)
-            backs.append((local, product, edge))
-            out_moved.append(scatter_dp(low_grad, high_grad, orders[pair % 2], block_rows))
+            backs[pair] = (local, product, edge)
+            out_moved[pair] = scatter_dp(low_grad, high_grad, orders[step % 2], block_rows)
 
         def separate(values):
             gate = [values[:, 2 * at * GROUP : (2 * at + 1) * GROUP] for at in range(groups)]
@@ -867,24 +903,23 @@
             gate, out = jnp.concatenate(gate, axis=1), jnp.concatenate(out, axis=1)
             return [jnp.concatenate([gate[:, :chunk], out[:, :chunk]], axis=1), jnp.concatenate([gate[:, chunk:], out[:, chunk:]], axis=1)]
 
-        out_sum, out_back = join_tensor([part for one in out_moved for part in separate(one[0])])
-
         leave = exchange(
-            jnp.concatenate([one[2][1:2] for one in backs], axis=1),
-            jnp.concatenate([one[2][0:1] for one in backs], axis=1),
+            jnp.concatenate([one[2][1:2] for _, one in sorted(backs.items())], axis=1),
+            jnp.concatenate([one[2][0:1] for _, one in sorted(backs.items())], axis=1),
             True,
         )
-        gate_backs = []
+        gate_backs = {}
+        out_marks = [out_moved[pair][1] for pair in backward]
         gate_holds = [
-            [moved[3][1][1], mlp_far[0], out_moved[0][1][0]],
-            [moved[2][1][2], out_moved[1][1][0]],
+            [moved[3][1][1], moved[1][1][2], out_marks[0][0]],
+            [moved[2][1][2], out_marks[1][0]],
         ]
-        for pair in range(pairs):
+        for step, pair in enumerate(backward):
             part = slice(2 * pair * local_blocks, 2 * (pair + 1) * local_blocks)
             lanes = slice(pair * pair_width, (pair + 1) * pair_width)
             branch, conv_out, recur_open, inflow = fed[pair][:4]
             local, product, _ = backs[pair]
-            gate_backs.append(
+            gate_backs[pair] = (
                 call(
                     gate_back_kernel,
                     groups,
@@ -892,19 +927,47 @@
                     [lanes_of(length), blocks_of(), blocks_of(), lanes_of(8)],
                     [shaped(length, pair_width), shaped(2 * local_blocks, BLOCK, BLOCK), shaped(2 * local_blocks, BLOCK, BLOCK), shaped(8, pair_width)],
                     [pltpu.VMEM((length, GROUP), bf16)] * 3,
-                    hold=gate_holds[pair],
+                    hold=gate_holds[step],
                 )(local, product, leave[:, lanes], mixed[pair][1], recur_open, inflow, conv_out, branch, rgates[part], igates[part], table[:, lanes])
             )
-        heads = jnp.concatenate([one[0][:8] for one in gate_backs], axis=1)
+        gate_list = [gate_backs[pair] for pair in range(pairs)]
+        heads = jnp.concatenate([one[0][:8] for one in gate_list], axis=1)
         heads = jnp.concatenate(relative(split_lanes(heads, tensor_size), tensor_at), axis=1)
         heads = lax.ppermute(heads, "tensor", [(at + 1, at) for at in range(tensor_size - 1)])
         after = jnp.concatenate(relative(split_lanes(heads, tensor_size), tensor_at), axis=1)
-        in_parts = []
+        rgrads = jnp.concatenate([one[1] for one in gate_list], axis=0)
+        igrads = jnp.concatenate([one[2] for one in gate_list], axis=0)
+        rows = jnp.concatenate([one[3] for one in gate_list], axis=1)
+        decay_row = rows[3:4] * (8.0 * jax.nn.sigmoid(-decay_rates))
+        rows = jnp.concatenate([rows[4:8], rows[0:3], decay_row], axis=0)
+        if fast:
+            def small_grads(*args, **sizes):
+                small_grads_kernel(*args, sub=sub, local_blocks=local_blocks, chunks=tensor_size)
+            small_own, small_other = call(
+                small_grads, 1, [SCALARS, gate_spec, gate_spec, fixed((kinds, channels))], [small_spec, small_spec],
+                [shaped(*small_spec.block_shape, kind=bf16)] * 2, [],
+            )(places, rgrads, igrads, rows)
+        else:
+            gate_grads = jnp.stack([rgrads, igrads], axis=0).reshape(2, tensor_size, local_blocks, dp_size, sub, BLOCK)
+            gate_grads = gate_grads.transpose(3, 0, 2, 4, 1, 5).reshape(dp_size, gate_rows, tensor_size * BLOCK)
+            gate_grads = jnp.take(gate_grads, natural_at, axis=0)
+            rows = rows.reshape(kinds, tensor_size, local_blocks, BLOCK).transpose(0, 2, 1, 3).reshape(1, vector_rows, -1)
+            rest = small_rows - gate_rows - vector_rows
+            pieces = [
+                gate_grads,
+                jnp.broadcast_to(rows, (dp_size,) + rows.shape[1:]),
+                jnp.zeros((dp_size, rest, tensor_size * BLOCK), f32),
+            ]
+            small_grads = jnp.concatenate(pieces, axis=1).reshape(dp_size * small_rows, -1).astype(bf16)
+            small_own, small_other = jnp.split(small_grads, 2, axis=0)
+        small_sum, small_marks = scatter_dp(small_own, small_other, order_one, small_rows)
+
+        in_parts = {}
         branch_holds = [
-            [moved[3][1][2], mlp_far[1], out_moved[0][1][1]],
-            [out_moved[1][1][1]],
+            [moved[3][1][2], out_marks[0][1], out_marks[1][1]],
+            [out_marks[0][2], out_marks[1][2], small_marks[0]],
         ]
-        for pair in range(pairs):
+        for step, pair in enumerate(backward):
             low, high, _ = in_pairs[pair]
             lanes = slice(pair * pair_width, (pair + 1) * pair_width)
             normed_grad, low_grad, high_grad = call(
@@ -914,62 +977,50 @@
                 [whole, lanes_of(half), lanes_of(half)],
                 [shaped(length, model), shaped(half, pair_width, kind=bf16), shaped(half, pair_width, kind=bf16)],
                 [pltpu.VMEM((length + 8, GROUP), f32), pltpu.VMEM((length, GROUP), bf16)],
-                hold=branch_holds[pair],
+                hold=branch_holds[step],
             )(gate_backs[pair][0], after[:, lanes], table[:, lanes], normed_one_t, low, high, normed_grad)
-            in_parts += split_lanes(scatter_dp(low_grad, high_grad, orders[pair % 2], block_rows)[0], 2)
-        in_sum, _ = join_tensor(in_parts)
+            in_parts[pair] = scatter_dp(low_grad, high_grad, orders[step % 2], block_rows)
+        final_holds = [small_marks[1], in_parts[backward[0]][1][0]]
 
         hidden_grad, gain_one = call(
             final_kernel, 1, [SCALARS, whole, whole, whole, fixed((2, model))], [whole, fixed((1, model))],
             [shaped(length, model), shaped(1, model)], [pltpu.VMEM((length, model), f32)],
-            hold=[],
+            hold=final_holds,
         )(places, hidden_low, normed_grad, middle_grad, gains)
+        in_sum, _ = join_tensor([part for pair in range(pairs) for part in split_lanes(in_parts[pair][0], 2)])
+
+        late = [gain_one]
+        mlp_columns = [[((3 * at + which) * GROUP, GROUP) for at in range(mlp_groups)] for which in range(3)]
+        mlp_others = {tensor_size - 1 - step: one[0] for step, one in enumerate(moved[:-1])}
+        mlp_grads = join_parts(moved[-1][0], mlp_others, mlp_columns, late)
+        out_parts = [part for pair in range(pairs) for part in separate(out_moved[pair][0])]
+        out_columns = [[(0, chunk)], [(chunk, chunk)]]
+        gate_grad, out_grad = join_parts(out_parts[0], dict(enumerate(out_parts[1:], 1)), out_columns, late)
+
+        gain_parts = jnp.concatenate([gain_one, gain_two], axis=0).reshape(2, dp_size, block_rows)
+        if not fast:
+            gain_parts = jnp.take(gain_parts, natural_at, axis=1)
+        gain_parts = jnp.pad(gain_parts.transpose(1, 0, 2), ((0, 0), (0, 6), (0, BLOCK - block_rows)))
+        gain_parts = gain_parts.reshape(8 * dp_size, BLOCK)
+        gain_sum, _ = scatter_dp(gain_parts[: 4 * dp_size], gain_parts[4 * dp_size :], order_one, 8)
+        gain_sum = sum(spread_tensor(gain_sum)[1:], gain_sum)
+        gain_rows = block_rows // tensor_size
+        gain_sum = lax.dynamic_slice(gain_sum, (0, tensor_at * gain_rows), (2, gain_rows)).T
+
         hidden_grad = features(hidden_grad, True)
-
-        rgrads = jnp.concatenate([one[1] for one in gate_backs], axis=0)
-        igrads = jnp.concatenate([one[2] for one in gate_backs], axis=0)
-        rows = jnp.concatenate([one[3] for one in gate_backs], axis=1)
-        decay_row = rows[3:4] * (8.0 * jax.nn.sigmoid(-decay_rates))
-        rows = jnp.concatenate([rows[4:8], rows[0:3], decay_row], axis=0)
-        gain_parts = jnp.concatenate([gain_one, gain_two], axis=0)
-        if fast:
-            def small_grads(*args, **sizes):
-                small_grads_kernel(*args, sub=sub, local_blocks=local_blocks, chunks=tensor_size)
-            small_own, small_other = call(
-                small_grads, 1, [SCALARS, gate_spec, gate_spec, fixed((kinds, channels)), fixed((2, model))], [small_spec, small_spec],
-                [shaped(*small_spec.block_shape, kind=bf16)] * 2, [],
-            )(places, rgrads, igrads, rows, gain_parts)
-        else:
-            gate_grads = jnp.stack([rgrads, igrads], axis=0).reshape(2, tensor_size, local_blocks, dp_size, sub, BLOCK)
-            gate_grads = gate_grads.transpose(3, 0, 2, 4, 1, 5).reshape(dp_size, gate_rows, tensor_size * BLOCK)
-            gate_grads = jnp.take(gate_grads, natural_at, axis=0)
-            rows = rows.reshape(kinds, tensor_size, local_blocks, BLOCK).transpose(0, 2, 1, 3).reshape(1, vector_rows, -1)
-            gain_parts = gain_parts.reshape(2, dp_size, block_rows).transpose(1, 0, 2)
-            gain_parts = jnp.pad(gain_parts, ((0, 0), (0, 0), (0, BLOCK - block_rows)))
-            rest = small_rows - gate_rows - vector_rows - 2
-            pieces = [
-                gate_grads,
-                jnp.broadcast_to(rows, (dp_size,) + rows.shape[1:]),
-                jnp.tile(gain_parts, (1, 1, tensor_size)),
-                jnp.zeros((dp_size, rest, tensor_size * BLOCK), f32),
-            ]
-            small_grads = jnp.concatenate(pieces, axis=1).reshape(dp_size * small_rows, -1).astype(bf16)
-            small_own, small_other = jnp.split(small_grads, 2, axis=0)
-        small_sum, _ = scatter_dp(small_own, small_other, order_one, small_rows)
         small_sum, _ = join_tensor(split_lanes(small_sum, tensor_size))
+
         gate_sum = small_sum[:gate_rows].reshape(2, local_blocks, sub, BLOCK).transpose(0, 2, 1, 3)
         vector_sum = lax.dynamic_slice(small_sum, (gate_rows, dp_at * sub), (vector_rows, sub))
         vector_sum = vector_sum.reshape(kinds, local_blocks, sub)
-        gain_rows = block_rows // tensor_size
-        gain_sum = lax.dynamic_slice(small_sum, (gate_rows + vector_rows, tensor_at * gain_rows), (2, gain_rows)).T
 
         return (
             hidden_out,
             hidden_grad,
             gain_sum,
             in_sum,
-            out_sum[:, :chunk],
-            out_sum[:, chunk:],
+            gate_grad,
+            out_grad,
             gate_sum[1],
             gate_sum[0],
             vector_sum[:CONV].transpose(2, 0, 1),

time: 646 us -> 561 us (0.87)
  starting transfers between devices: 126 us -> 85.9 us
  waiting for transfers between devices: 177 us -> 142 us
  local copies, waits for them, and re-layouts: 54.1 us -> 34.7 us
  between operations: 2.4 us -> 15.8 us
  other arithmetic: 48.7 us -> 38 us
  Pallas kernels: 232 us -> 241 us
    pallas_call x0 -> x4, Pallas kernels: none -> 69.9 us  [per_device(): pl.pallas_call(kernel, grid_spec=pltpu.PrefetchScalarGridSpec(num_scalar_...]
    pallas_call x21 -> x19, Pallas kernels: 232 us -> 171 us  [call(): return lambda *args: run(*args, *hold)]
    ppermute x30, starting transfers between devices: 76.4 us -> 46.7 us  [swap_tensor(): lax.ppermute(values, 'tensor', [(at, at ^ bit) for at in range(tensor_siz...]
    ppermute x30, waiting for transfers between devices: 67.1 us -> 39.4 us  [swap_tensor(): lax.ppermute(values, 'tensor', [(at, at ^ bit) for at in range(tensor_siz...]
    concatenate x13 -> x8, other arithmetic: 10.6 us -> 0.37 us  [gather_dp(): values = jnp.concatenate([values, received], axis=0)]
    ppermute x54 -> x45, starting transfers between devices: 44.6 us -> 36.5 us  [swap_dp(): return lax.ppermute(values, 'dp', [(at, at ^ bit) for at in range(dp_size)])]
    convert_element_type x26 -> x27, other arithmetic: 15.8 us -> 22.8 us  [add(): return (one.astype(f32) + two.astype(f32)).astype(one.dtype)]
    unnamed x175 -> x162, local copies, waits for them, and re-layouts: 23.4 us -> 18.5 us
  transfers between devices with their start and end apart: 86 -> 78, of which waited for: 26 -> 33; matrix products, arithmetic and copies ran while one was open for 14% -> 10% of each run, Pallas kernels for 36% -> 40%
where the time goes in v3:
time: 561 us; the launch traced here: 557 us
  Pallas kernels  241 us (43%)
  waiting for transfers between devices  142 us (25%)
  starting transfers between devices  85.9 us (15%)
  other arithmetic  38 us (7%)
  local copies, waits for them, and re-layouts  34.7 us (6%)
  between operations  15.8 us (3%)
    pallas_call x19, Pallas kernels, call(): return lambda *args: run(*args, *hold)  171 us
    ppermute x45, waiting for transfers between devices, swap_dp(): return lax.ppermute(values, 'dp', [(at, at ^ bit) for at in range(dp_size)])  102 us
    pallas_call x4, Pallas kernels, per_device(): pl.pallas_call(kernel, grid_spec=pltpu.PrefetchScalarGridSpec(num_scalar_...  69.9 us
    ppermute x30, starting transfers between devices, swap_tensor(): lax.ppermute(values, 'tensor', [(at, at ^ bit) for at in range(tensor_siz...  46.7 us
    ppermute x30, waiting for transfers between devices, swap_tensor(): lax.ppermute(values, 'tensor', [(at, at ^ bit) for at in range(tensor_siz...  39.4 us
    ppermute x45, starting transfers between devices, swap_dp(): return lax.ppermute(values, 'dp', [(at, at ^ bit) for at in range(dp_size)])  36.5 us
    convert_element_type x27, other arithmetic, add(): return (one.astype(f32) + two.astype(f32)).astype(one.dtype)  22.8 us
    unnamed x162, local copies, waits for them, and re-layouts  18.5 us
  transfers between devices with their start and end apart: 78, of which 33 were waited for; matrix products, arithmetic and copies ran while one was open for 10% of the time, Pallas kernels for 40%

profile of v3, /device:TPU:0, one launch (start us, length us, event | category | flops | bytes accessed | tf_op | source)
XLA Modules:
  0.0 557.0 jit_solution(5122532408911423969)
XLA Ops:
  35.4 3.9 collective-permute-start.13
  39.3 21.0 %collective-permute-done.13 = bf16[128,384]{1,0:T(8,128)(2,1)S(1)} collective-permute-done((bf16[128,384]{1,0:T(8,128)(2,1)S(1)}, bf16[128,384]{1,0:T(8,128)(2,1)S(1)}, u32[]{:S(2)}, u32[]{:S(2)}) %collective-permute-start.13) | collective-permute-done | bytes 98336 | tf_op jit(solution)/shard_map/ppermute | solution.py:567
  75.9 5.1 collective-permute-done.21
  87.4 7.1 %collective-permute-done.10.refs_7_ = bf16[128,1536]{1,0:T(8,128)(2,1)S(1)} collective-permute-done((bf16[128,1536]{1,0:T(8,128)(2,1)S(1)}, bf16[128,1536]{1,0:T(8,128)(2,1)S(1)}, u32[]{:S(2)}, u32[]{:S(2)}) %collective-permute-start.10) | collective-permute-done | bytes 393248 | tf_op jit(solution)/shard_map/ppermute | solution.py:564
  94.5 4.0 collective-permute-done.18.refs_6_
  101.8 5.2 collective-permute-done.16
  111.3 6.4 %norm_kernel.1 = (bf16[528,1024]{1,0:T(8,128)(2,1)}, bf16[1024,512]{1,0:T(8,128)(2,1)}) custom-call(s32[8]{0:T(128)} %broadcast_xor_fusion.refs_0_, bf16[512,1024]{1,0:T(8,128)(2,1)} %get-tuple-element.103.refs_1_, bf16[16,1024]{1,0:T(8,128)(2,1)} %copy-done.69, f32[2,1024]{1,0:T(2,128)} %get-tuple-element.104.refs_3_.refs_2_.refs_5_.refs_4_), custom_call_target="tpu_custom_call" | custom-call | flops 6899999744 | tf_op jit(solution)/shard_map/norm_kernel/pallas_call | solution.py:552
  119.2 8.5 %collective-permute-done.19.refs_6_ = bf16[256,1536]{1,0:T(8,128)(2,1)S(1)} collective-permute-done((bf16[256,1536]{1,0:T(8,128)(2,1)S(1)}, bf16[256,1536]{1,0:T(8,128)(2,1)S(1)}, u32[]{:S(2)}, u32[]{:S(2)}) %collective-permute-start.19) | collective-permute-done | bytes 786464 | tf_op jit(solution)/shard_map/ppermute | solution.py:564
  128.6 3.9 collective-permute-done.11.refs_7_
  132.6 14.4 %mix_in_kernel.3 = (f32[528,768]{1,0:T(8,128)}, f32[512,768]{1,0:T(8,128)}, f32[512,768]{1,0:T(8,128)}, f32[512,768]{1,0:T(8,128)}, f32[512,768]{1,0:T(8,128)}, /*index=5*/f32[512,768]{1,0:T(8,128)}) custom-call(bf16[528,1024]{1,0:T(8,128)(2,1)} %get-tuple-element.105.refs_0_, bf16[512,768]{1,0:T(8,128)(2,1)} %copy-done.29, ...), custom_call_target="tpu_custom_call" | custom-call | flops 16099999744 | tf_op jit(solution)/shard_map/mix_in_kernel/pallas_call | solution.py:552
  148.4 14.3 %mix_in_kernel.2 = (f32[528,768]{1,0:T(8,128)}, f32[512,768]{1,0:T(8,128)}, f32[512,768]{1,0:T(8,128)}, f32[512,768]{1,0:T(8,128)}, f32[512,768]{1,0:T(8,128)}, /*index=5*/f32[512,768]{1,0:T(8,128)}) custom-call(bf16[528,1024]{1,0:T(8,128)(2,1)} %get-tuple-element.105.refs_0_, bf16[512,768]{1,0:T(8,128)(2,1)} %copy-done.30, ...), custom_call_target="tpu_custom_call" | custom-call | flops 16099999744 | tf_op jit(solution)/shard_map/mix_in_kernel/pallas_call | solution.py:552
  172.9 10.3 %mix_out_kernel.2 = (f32[512,768]{1,0:T(8,128)}, f32[520,768]{1,0:T(8,128)}, bf16[512,768]{1,0:T(8,128)(2,1)}, f32[512,1024]{1,0:T(8,128)}) custom-call(bf16[528,1024]{1,0:T(8,128)(2,1)} %get-tuple-element.105.refs_0_, bf16[512,1536]{1,0:T(8,128)(2,1)} %copy-done.19, bf16[512,1536]{1,0:T(8,128)(2,1)} %collective-permute-done.27.refs_2_.refs_4_, ...), custom_call_target="tpu_custom_call" | custom-call | flops 11500000256 | tf_op jit(solution)/shard_map/mix_out_kernel/pallas_call | solution.py:552
  184.4 10.0 %mix_out_kernel.3 = (f32[512,768]{1,0:T(8,128)}, f32[520,768]{1,0:T(8,128)}, bf16[512,768]{1,0:T(8,128)(2,1)}, f32[512,1024]{1,0:T(8,128)}) custom-call(bf16[528,1024]{1,0:T(8,128)(2,1)} %get-tuple-element.105.refs_0_, bf16[512,1536]{1,0:T(8,128)(2,1)} %copy-done.20, bf16[512,1536]{1,0:T(8,128)(2,1)} %copy-done.62, f32[512,768]{1,0:T(8,128)} %get-tuple-element.109.refs_3_, ...), custom_call_target="tpu_custom_call" | custom-call | flops 11500000256 | tf_op jit(solution)/shard_map/mix_out_kernel/pallas_call | solution.py:552
  194.4 6.7 %second_norm_kernel.1 = (bf16[512,1024]{1,0:T(8,128)(2,1)}, bf16[1024,512]{1,0:T(8,128)(2,1)}) custom-call(s32[8]{0:T(128)} %broadcast_xor_fusion.refs_0_, f32[512,1024]{1,0:T(8,128)} %get-tuple-element.114.refs_1_, f32[2,1024]{1,0:T(2,128)} %get-tuple-element.104.refs_3_.refs_2_.refs_5_.refs_4_), custom_call_target="tpu_custom_call" | custom-call | flops 6899999744 | tf_op jit(solution)/shard_map/second_norm_kernel/pallas_call | solution.py:552
  201.1 16.3 %mlp_kernel.4 = (f32[512,1024]{1,0:T(8,128)}, f32[512,1024]{1,0:T(8,128)}, bf16[512,2304]{1,0:T(8,128)(2,1)}, bf16[512,2304]{1,0:T(8,128)(2,1)}) custom-call(s32[4]{0:T(128)} %iota_xor_fusion.refs_0_, bf16[512,1024]{1,0:T(8,128)(2,1)} %get-tuple-element.115.refs_1_, bf16[1024,512]{1,0:T(8,128)(2,1)} %get-tuple-element.116.refs_2_, ...), custom_call_target="tpu_custom_call" | custom-call | flops 19549999104 | tf_op jit(solution)/shard_map/mlp_kernel/pallas_call | solution.py:845
  217.4 17.9 %mlp_kernel.5 = (f32[512,1024]{1,0:T(8,128)}, f32[512,1024]{1,0:T(8,128)}, bf16[512,2304]{1,0:T(8,128)(2,1)}, bf16[512,2304]{1,0:T(8,128)(2,1)}) custom-call(s32[4]{0:T(128)} %iota_xor_fusion.refs_0_, bf16[512,1024]{1,0:T(8,128)(2,1)} %get-tuple-element.115.refs_1_, bf16[1024,512]{1,0:T(8,128)(2,1)} %get-tuple-element.116.refs_2_, ...), custom_call_target="tpu_custom_call" | custom-call | flops 19549999104 | tf_op jit(solution)/shard_map/mlp_kernel/pallas_call | solution.py:845
  239.8 17.7 %mlp_kernel.6 = (f32[512,1024]{1,0:T(8,128)}, f32[512,1024]{1,0:T(8,128)}, bf16[512,2304]{1,0:T(8,128)(2,1)}, bf16[512,2304]{1,0:T(8,128)(2,1)}) custom-call(s32[4]{0:T(128)} %iota_xor_fusion.refs_0_, bf16[512,1024]{1,0:T(8,128)(2,1)} %get-tuple-element.115.refs_1_, bf16[1024,512]{1,0:T(8,128)(2,1)} %get-tuple-element.116.refs_2_, ...), custom_call_target="tpu_custom_call" | custom-call | flops 19549999104 | tf_op jit(solution)/shard_map/mlp_kernel/pallas_call | solution.py:845
  261.5 17.9 %mlp_kernel.7 = (f32[512,1024]{1,0:T(8,128)}, f32[512,1024]{1,0:T(8,128)}, bf16[512,2304]{1,0:T(8,128)(2,1)}, bf16[512,2304]{1,0:T(8,128)(2,1)}) custom-call(s32[4]{0:T(128)} %iota_xor_fusion.refs_0_, bf16[512,1024]{1,0:T(8,128)(2,1)} %get-tuple-element.115.refs_1_, bf16[1024,512]{1,0:T(8,128)(2,1)} %get-tuple-element.116.refs_2_, ...), custom_call_target="tpu_custom_call" | custom-call | flops 19549999104 | tf_op jit(solution)/shard_map/mlp_kernel/pallas_call | solution.py:845
  279.7 8.6 %collective-permute-done.33 = bf16[256,2304]{1,0:T(8,128)(2,1)S(1)} collective-permute-done((bf16[256,2304]{1,0:T(8,128)(2,1)S(1)}, bf16[256,2304]{1,0:T(8,128)(2,1)S(1)}, u32[]{:S(2)}, u32[]{:S(2)}) %collective-permute-start.33) | collective-permute-done | bytes 1179680 | tf_op jit(solution)/shard_map/ppermute | solution.py:564
  294.0 10.9 %collective-permute-done.42 = bf16[128,2304]{1,0:T(8,128)(2,1)S(1)} collective-permute-done((bf16[128,2304]{1,0:T(8,128)(2,1)S(1)}, bf16[128,2304]{1,0:T(8,128)(2,1)S(1)}, u32[]{:S(2)}, u32[]{:S(2)}) %collective-permute-start.42) | collective-permute-done | bytes 589856 | tf_op jit(solution)/shard_map/ppermute | solution.py:564
  315.5 12.4 %middle_kernel.1 = (bf16[512,1024]{1,0:T(8,128)(2,1)}, f32[512,1024]{1,0:T(8,128)}, bf16[512,1024]{1,0:T(8,128)(2,1)}, bf16[1024,512]{1,0:T(8,128)(2,1)}, f32[1,1024]{1,0:T(1,128)}) custom-call(s32[8]{0:T(128)} %broadcast_xor_fusion.refs_0_, f32[512,1024]{1,0:T(8,128)} %get-tuple-element.114.refs_1_, f32[512,1024]{1,0:T(8,128)} %get-tuple-element.128.refs_2_, ...), custom_call_target="tpu_custom_call" | custom-call | flops 13799999488 | tf_op jit(solution)/shard_map/middle_kernel/pallas_call | solution.py:552
  331.5 18.4 %mix_back_kernel.2 = (f32[512,1024]{1,0:T(8,128)}, f32[512,768]{1,0:T(8,128)}, f32[512,768]{1,0:T(8,128)}, f32[8,768]{1,0:T(8,128)}, bf16[512,1536]{1,0:T(8,128)(2,1)}, /*index=5*/bf16[512,1536]{1,0:T(8,128)(2,1)}) custom-call(bf16[512,1024]{1,0:T(8,128)(2,1)} %get-tuple-element.134.refs_0_, bf16[1024,512]{1,0:T(8,128)(2,1)} %get-tuple-element.135.refs_1_, ...), custom_call_target="tpu_custom_call" | custom-call | flops 20700000256 | tf_op jit(solution)/shard_map/mix_back_kernel/pallas_call | solution.py:552
  354.4 18.4 %mix_back_kernel.3 = (f32[512,1024]{1,0:T(8,128)}, f32[512,768]{1,0:T(8,128)}, f32[512,768]{1,0:T(8,128)}, f32[8,768]{1,0:T(8,128)}, bf16[512,1536]{1,0:T(8,128)(2,1)}, /*index=5*/bf16[512,1536]{1,0:T(8,128)(2,1)}) custom-call(bf16[512,1024]{1,0:T(8,128)(2,1)} %get-tuple-element.134.refs_0_, bf16[1024,512]{1,0:T(8,128)(2,1)} %get-tuple-element.135.refs_1_, ...), custom_call_target="tpu_custom_call" | custom-call | flops 20700000256 | tf_op jit(solution)/shard_map/mix_back_kernel/pallas_call | solution.py:552
  391.7 10.6 %gate_back_kernel.3 = (f32[512,768]{1,0:T(8,128)}, f32[6,128,128]{2,1,0:T(8,128)}, f32[6,128,128]{2,1,0:T(8,128)}, f32[8,768]{1,0:T(8,128)}) custom-call(f32[512,768]{1,0:T(8,128)} %get-tuple-element.158.refs_0_, f32[512,768]{1,0:T(8,128)} %get-tuple-element.159.refs_1_, f32[1,768]{1,0:T(1,128)} %get-tuple-element.299.refs_2_, ...), custom_call_target="tpu_custom_call" | custom-call | flops 12650000384 | tf_op jit(solution)/shard_map/gate_back_kernel/pallas_call | solution.py:552
  407.7 11.9 %collective-permute-done.46 = bf16[256,1536]{1,0:T(8,128)(2,1)S(1)} collective-permute-done((bf16[256,1536]{1,0:T(8,128)(2,1)S(1)}, bf16[256,1536]{1,0:T(8,128)(2,1)S(1)}, u32[]{:S(2)}, u32[]{:S(2)}) %collective-permute-start.46) | collective-permute-done | bytes 786464 | tf_op jit(solution)/shard_map/ppermute | solution.py:564
  422.4 10.6 %gate_back_kernel.2 = (f32[512,768]{1,0:T(8,128)}, f32[6,128,128]{2,1,0:T(8,128)}, f32[6,128,128]{2,1,0:T(8,128)}, f32[8,768]{1,0:T(8,128)}) custom-call(f32[512,768]{1,0:T(8,128)} %get-tuple-element.148.refs_0_, f32[512,768]{1,0:T(8,128)} %get-tuple-element.149.refs_1_, f32[1,768]{1,0:T(1,128)} %get-tuple-element.300.refs_2_, ...), custom_call_target="tpu_custom_call" | custom-call | flops 12650000384 | tf_op jit(solution)/shard_map/gate_back_kernel/pallas_call | solution.py:552
  447.6 6.3 %collective-permute-done.51 = bf16[256,512]{1,0:T(8,128)(2,1)S(1)} collective-permute-done((bf16[256,512]{1,0:T(8,128)(2,1)S(1)}, bf16[256,512]{1,0:T(8,128)(2,1)S(1)}, u32[]{:S(2)}, u32[]{:S(2)}) %collective-permute-start.51) | collective-permute-done | bytes 262176 | tf_op jit(solution)/shard_map/ppermute | solution.py:564
  464.2 7.5 %branch_back_kernel.2 = (f32[512,1024]{1,0:T(8,128)}, bf16[512,768]{1,0:T(8,128)(2,1)}, bf16[512,768]{1,0:T(8,128)(2,1)}) custom-call(f32[512,768]{1,0:T(8,128)} %get-tuple-element.165.refs_0_, f32[8,768]{1,0:T(8,128)} %pad_maximum_fusion.29.refs_1_, f32[8,768]{1,0:T(8,128)} %get-tuple-element.266.refs_5_.refs_9_.refs_10_.refs_2_, ...), custom_call_target="tpu_custom_call" | custom-call | flops 9200000000 | tf_op jit(solution)/shard_map/branch_back_kernel/pallas_call | solution.py:552
  478.8 5.0 collective-permute-done.49
  484.6 7.6 %branch_back_kernel.3 = (f32[512,1024]{1,0:T(8,128)}, bf16[512,768]{1,0:T(8,128)(2,1)}, bf16[512,768]{1,0:T(8,128)(2,1)}) custom-call(f32[512,768]{1,0:T(8,128)} %get-tuple-element.157.refs_0_, f32[8,768]{1,0:T(8,128)} %pad_maximum_fusion.28.refs_1_, f32[8,768]{1,0:T(8,128)} %get-tuple-element.265.refs_5_.refs_9_.refs_10_.refs_2_, ...), custom_call_target="tpu_custom_call" | custom-call | flops 9200000000 | tf_op jit(solution)/shard_map/branch_back_kernel/pallas_call | solution.py:552
  493.3 10.3 %final_kernel.1 = (f32[512,1024]{1,0:T(8,128)}, f32[1,1024]{1,0:T(1,128)}) custom-call(s32[8]{0:T(128)} %broadcast_xor_fusion.refs_0_, bf16[512,1024]{1,0:T(8,128)(2,1)} %get-tuple-element.103.refs_1_, f32[512,1024]{1,0:T(8,128)} %get-tuple-element.176.refs_2_, f32[512,1024]{1,0:T(8,128)} %get-tuple-element.177.refs_3_, ...), custom_call_target="tpu_custom_call" | custom-call | flops 11500000256 | tf_op jit(solution)/shard_map/final_kernel/pallas_call | solution.py:552
  528.3 10.3 %collective-permute-done.64 = bf16[128,768]{1,0:T(8,128)(2,1)S(1)} collective-permute-done((bf16[128,768]{1,0:T(8,128)(2,1)S(1)}, bf16[128,768]{1,0:T(8,128)(2,1)S(1)}, u32[]{:S(2)}, u32[]{:S(2)}) %collective-permute-start.64) | collective-permute-done | bytes 196640 | tf_op jit(solution)/shard_map/ppermute | solution.py:564
  (462 shorter events, 202.0 us)
Async XLA Ops:
  7.3 193.8 %all-gather.3.cloned.1.call-start = ((), (), s32[]{:S(2)}) async-start(), calls=%async_computation | async-start | bytes 19464192 | tf_op jit(solution)/shard_map/all_gather | solution.py:729
  16.4 18.5 %collective-permute-start.1 = (bf16[128,128]{1,0:T(8,128)(2,1)S(1)}, bf16[128,128]{1,0:T(8,128)(2,1)S(1)}, u32[]{:S(2)}, u32[]{:S(2)}) collective-permute-start(bf16[128,128]{1,0:T(8,128)(2,1)S(1)} %concatenate.203), channel_id=1, source_target_pairs={{0,1},{1,0},{2,3},{3,2},{4,5},{5,4},{6,7},{7,6},{8,9},{9,8},{10,11... | collective-permute-start | bytes 98312 | tf_op jit(solution)/shard_map/ppermute | solution.py:567
  22.1 52.2 %collective-permute-start.7 = (bf16[128,768]{1,0:T(8,128)(2,1)S(1)}, bf16[128,768]{1,0:T(8,128)(2,1)S(1)}, u32[]{:S(2)}, u32[]{:S(2)}) collective-permute-start(bf16[128,768]{1,0:T(8,128)(2,1)S(1)} %constant_dynamic-update-slice_fusion), channel_id=1, source_target_pairs={{0,1},{1,0},{2,3},{3,2},{4,5},{5,4},{6,7},{7,6},{8,9},{9,8},{10,11... | collective-permute-start | bytes 589832 | tf_op jit(solution)/shard_map/ppermute | solution.py:567
  23.1 48.9 %collective-permute-start.8 = (bf16[128,768]{1,0:T(8,128)(2,1)S(1)}, bf16[128,768]{1,0:T(8,128)(2,1)S(1)}, u32[]{:S(2)}, u32[]{:S(2)}) collective-permute-start(bf16[128,768]{1,0:T(8,128)(2,1)S(1)} %constant_dynamic-update-slice_fusion), channel_id=1, source_target_pairs={{0,2},{1,3},{2,0},{3,1},{4,6},{5,7},{6,4},{7,5},{8,10},{9,11},{10,... | collective-permute-start | bytes 589832 | tf_op jit(solution)/shard_map/ppermute | solution.py:567
  34.9 38.6 %collective-permute-start.9 = (bf16[128,768]{1,0:T(8,128)(2,1)S(1)}, bf16[128,768]{1,0:T(8,128)(2,1)S(1)}, u32[]{:S(2)}, u32[]{:S(2)}) collective-permute-start(bf16[128,768]{1,0:T(8,128)(2,1)S(1)} %constant_dynamic-update-slice_fusion), channel_id=1, source_target_pairs={{0,3},{1,2},{2,1},{3,0},{4,7},{5,6},{6,5},{7,4},{8,11},{9,10},{10,... | collective-permute-start | bytes 589832 | tf_op jit(solution)/shard_map/ppermute | solution.py:567
  34.9 27.6 %collective-permute-start.20 = (bf16[128,384]{1,0:T(8,128)(2,1)S(1)}, bf16[128,384]{1,0:T(8,128)(2,1)S(1)}, u32[]{:S(2)}, u32[]{:S(2)}) collective-permute-start(bf16[128,384]{1,0:T(8,128)(2,1)S(1)} %copy-done.50), channel_id=1, source_target_pairs={{0,1},{1,0},{2,3},{3,2},{4,5},{5,4},{6,7},{7,6},{8,9},{9,8},{10,11... | collective-permute-start | bytes 294920 | tf_op jit(solution)/shard_map/ppermute | solution.py:567
  35.4 24.9 %collective-permute-start.13 = (bf16[128,384]{1,0:T(8,128)(2,1)S(1)}, bf16[128,384]{1,0:T(8,128)(2,1)S(1)}, u32[]{:S(2)}, u32[]{:S(2)}) collective-permute-start(bf16[128,384]{1,0:T(8,128)(2,1)S(1)} %copy-done.50), channel_id=1, source_target_pairs={{0,2},{1,3},{2,0},{3,1},{4,6},{5,7},{6,4},{7,5},{8,10},{9,11},{10,... | collective-permute-start | bytes 294920 | tf_op jit(solution)/shard_map/ppermute | solution.py:567
  66.7 43.9 %collective-permute-start = (bf16[16,1024]{1,0:T(8,128)(2,1)S(1)}, bf16[16,1024]{1,0:T(8,128)(2,1)S(1)}, u32[]{:S(2)}, u32[]{:S(2)}) collective-permute-start(bf16[16,1024]{1,0:T(8,128)(2,1)S(1)} %slice.598), channel_id=1, source_target_pairs={{0,1},{1,2},{2,3},{4,5},{5,6},{6,7},{8,9},{9,10},{10,11},{12,13},{... | collective-permute-start | bytes 98312 | tf_op jit(solution)/shard_map/ppermute | solution.py:679
  74.3 20.2 %collective-permute-start.10 = (bf16[128,1536]{1,0:T(8,128)(2,1)S(1)}, bf16[128,1536]{1,0:T(8,128)(2,1)S(1)}, u32[]{:S(2)}, u32[]{:S(2)}) collective-permute-start(bf16[128,1536]{1,0:T(8,128)(2,1)S(1)} %slice_dynamic-update-slice_fusion.2), channel_id=1, source_target_pairs={{0,16},{4,20},{8,24},{12,28},{16,0},{20,4},{24,8},{28,12},{1,17},{... | collective-permute-start | bytes 1179656 | tf_op jit(solution)/shard_map/ppermute | solution.py:564
  86.0 20.9 %collective-permute-start.16 = (bf16[256,768]{1,0:T(8,128)(2,1)S(1)}, bf16[256,768]{1,0:T(8,128)(2,1)S(1)}, u32[]{:S(2)}, u32[]{:S(2)}) collective-permute-start(bf16[256,768]{1,0:T(8,128)(2,1)S(1)} %pad_maximum_fusion.12), channel_id=1, source_target_pairs={{0,8},{4,12},{8,0},{12,4},{16,24},{20,28},{24,16},{28,20},{1,9},{5... | collective-permute-start | bytes 1179656 | tf_op jit(solution)/shard_map/ppermute | solution.py:564
  98.5 34.0 %collective-permute-start.11 = (bf16[256,1536]{1,0:T(8,128)(2,1)S(1)}, bf16[256,1536]{1,0:T(8,128)(2,1)S(1)}, u32[]{:S(2)}, u32[]{:S(2)}) collective-permute-start(bf16[256,1536]{1,0:T(8,128)(2,1)S(1)} %pad_maximum_fusion.4), channel_id=1, source_target_pairs={{0,8},{4,12},{8,0},{12,4},{16,24},{20,28},{24,16},{28,20},{1,9},{5... | collective-permute-start | bytes 2359304 | tf_op jit(solution)/shard_map/ppermute | solution.py:564
  101.4 26.3 %collective-permute-start.19 = (bf16[256,1536]{1,0:T(8,128)(2,1)S(1)}, bf16[256,1536]{1,0:T(8,128)(2,1)S(1)}, u32[]{:S(2)}, u32[]{:S(2)}) collective-permute-start(bf16[256,1536]{1,0:T(8,128)(2,1)S(1)} %pad_maximum_fusion.6), channel_id=1, source_target_pairs={{0,16},{4,20},{8,24},{12,28},{16,0},{20,4},{24,8},{28,12},{1,17},{... | collective-permute-start | bytes 2359304 | tf_op jit(solution)/shard_map/ppermute | solution.py:564
  107.0 25.6 %collective-permute-start.23 = (bf16[512,768]{1,0:T(8,128)(2,1)S(1)}, bf16[512,768]{1,0:T(8,128)(2,1)}, u32[]{:S(2)}, u32[]{:S(2)}) collective-permute-start(bf16[512,768]{1,0:T(8,128)(2,1)S(1)} %pad_maximum_fusion.7.refs_1_.refs_4_), channel_id=1, source_target_pairs={{0,4},{4,0},{8,12},{12,8},{16,20},{20,16},{24,28},{28,24},{1,5},{5... | collective-permute-start | bytes 2359304 | tf_op jit(solution)/shard_map/ppermute | solution.py:564
  107.9 40.5 %collective-permute-start.17 = (bf16[512,768]{1,0:T(8,128)(2,1)S(1)}, bf16[512,768]{1,0:T(8,128)(2,1)}, u32[]{:S(2)}, u32[]{:S(2)}) collective-permute-start(bf16[512,768]{1,0:T(8,128)(2,1)S(1)} %pad_maximum_fusion.5.refs_1_.refs_4_), channel_id=1, source_target_pairs={{0,4},{4,0},{8,12},{12,8},{16,20},{20,16},{24,28},{28,24},{1,5},{5... | collective-permute-start | bytes 2359304 | tf_op jit(solution)/shard_map/ppermute | solution.py:564
  128.6 44.3 %collective-permute-start.27 = (bf16[512,1536]{1,0:T(8,128)(2,1)S(1)}, bf16[512,1536]{1,0:T(8,128)(2,1)}, u32[]{:S(2)}, u32[]{:S(2)}) collective-permute-start(bf16[512,1536]{1,0:T(8,128)(2,1)S(1)} %pad_maximum_fusion.1.refs_1_.refs_3_), channel_id=1, source_target_pairs={{0,4},{4,0},{8,12},{12,8},{16,20},{20,16},{24,28},{28,24},{1,5},{5... | collective-permute-start | bytes 4718600 | tf_op jit(solution)/shard_map/ppermute | solution.py:564
  164.5 18.8 %collective-permute-start.12 = (bf16[512,1536]{1,0:T(8,128)(2,1)S(1)}, bf16[512,1536]{1,0:T(8,128)(2,1)S(1)}, u32[]{:S(2)}, u32[]{:S(2)}) collective-permute-start(bf16[512,1536]{1,0:T(8,128)(2,1)S(1)} %pad_maximum_fusion.refs_1_.refs_3_), channel_id=1, source_target_pairs={{0,4},{4,0},{8,12},{12,8},{16,20},{20,16},{24,28},{28,24},{1,5},{5... | collective-permute-start | bytes 4718600 | tf_op jit(solution)/shard_map/ppermute | solution.py:564
  217.4 18.4 %collective-permute-start.28 = (bf16[512,2304]{1,0:T(8,128)(2,1)}, bf16[512,2304]{1,0:T(8,128)(2,1)S(1)}, u32[]{:S(2)}, u32[]{:S(2)}) collective-permute-start(bf16[512,2304]{1,0:T(8,128)(2,1)} %get-tuple-element.123), channel_id=1, source_target_pairs={{0,4},{4,0},{8,12},{12,8},{16,20},{20,16},{24,28},{28,24},{1,5},{5... | collective-permute-start | bytes 7077896 | tf_op jit(solution)/shard_map/ppermute | solution.py:564
  235.3 22.3 %collective-permute-start.29 = (bf16[512,2304]{1,0:T(8,128)(2,1)}, bf16[512,2304]{1,0:T(8,128)(2,1)}, u32[]{:S(2)}, u32[]{:S(2)}) collective-permute-start(bf16[512,2304]{1,0:T(8,128)(2,1)} %get-tuple-element.127), channel_id=1, source_target_pairs={{0,4},{4,0},{8,12},{12,8},{16,20},{20,16},{24,28},{28,24},{1,5},{5... | collective-permute-start | bytes 7077896 | tf_op jit(solution)/shard_map/ppermute | solution.py:564
  238.8 52.2 %collective-permute-start.31 = (bf16[256,2304]{1,0:T(8,128)(2,1)}, bf16[256,2304]{1,0:T(8,128)(2,1)}, u32[]{:S(2)}, u32[]{:S(2)}) collective-permute-start(bf16[256,2304]{1,0:T(8,128)(2,1)} %pad_maximum_fusion.2), channel_id=1, source_target_pairs={{0,8},{4,12},{8,0},{12,4},{16,24},{20,28},{24,16},{28,20},{1,9},{5... | collective-permute-start | bytes 3538952 | tf_op jit(solution)/shard_map/ppermute | solution.py:564
  257.6 52.0 %collective-permute-start.30 = (bf16[512,2304]{1,0:T(8,128)(2,1)}, bf16[512,2304]{1,0:T(8,128)(2,1)}, u32[]{:S(2)}, u32[]{:S(2)}) collective-permute-start(bf16[512,2304]{1,0:T(8,128)(2,1)} %get-tuple-element.132), channel_id=1, source_target_pairs={{0,4},{4,0},{8,12},{12,8},{16,20},{20,16},{24,28},{28,24},{1,5},{5... | collective-permute-start | bytes 7077896 | tf_op jit(solution)/shard_map/ppermute | solution.py:564
  259.9 28.4 %collective-permute-start.33 = (bf16[256,2304]{1,0:T(8,128)(2,1)S(1)}, bf16[256,2304]{1,0:T(8,128)(2,1)S(1)}, u32[]{:S(2)}, u32[]{:S(2)}) collective-permute-start(bf16[256,2304]{1,0:T(8,128)(2,1)S(1)} %slice.823), channel_id=1, source_target_pairs={{0,16},{4,20},{8,24},{12,28},{16,0},{20,4},{24,8},{28,12},{1,17},{... | collective-permute-start | bytes 3538952 | tf_op jit(solution)/shard_map/ppermute | solution.py:564
  279.4 48.5 %collective-permute-start.32 = (bf16[512,2304]{1,0:T(8,128)(2,1)}, bf16[512,2304]{1,0:T(8,128)(2,1)S(1)}, u32[]{:S(2)}, u32[]{:S(2)}) collective-permute-start(bf16[512,2304]{1,0:T(8,128)(2,1)} %get-tuple-element.146), channel_id=1, source_target_pairs={{0,4},{4,0},{8,12},{12,8},{16,20},{20,16},{24,28},{28,24},{1,5},{5... | collective-permute-start | bytes 7077896 | tf_op jit(solution)/shard_map/ppermute | solution.py:564
  305.8 200.4 %collective-permute-start.75 = (bf16[128,2304]{1,0:T(8,128)(2,1)}, bf16[128,2304]{1,0:T(8,128)(2,1)}, u32[]{:S(2)}, u32[]{:S(2)}) collective-permute-start(bf16[128,2304]{1,0:T(8,128)(2,1)} %add_convert_fusion.15.refs_12_), channel_id=1, source_target_pairs={{0,2},{1,3},{2,0},{3,1},{4,6},{5,7},{6,4},{7,5},{8,10},{9,11},{10,... | collective-permute-start | bytes 1769480 | tf_op jit(solution)/shard_map/ppermute | solution.py:567
  308.3 198.4 %collective-permute-start.76 = (bf16[128,2304]{1,0:T(8,128)(2,1)}, bf16[128,2304]{1,0:T(8,128)(2,1)}, u32[]{:S(2)}, u32[]{:S(2)}) collective-permute-start(bf16[128,2304]{1,0:T(8,128)(2,1)} %add_convert_fusion.17.refs_12_), channel_id=1, source_target_pairs={{0,3},{1,2},{2,1},{3,0},{4,7},{5,6},{6,5},{7,4},{8,11},{9,10},{10,... | collective-permute-start | bytes 1769480 | tf_op jit(solution)/shard_map/ppermute | solution.py:567
  314.4 38.7 %collective-permute-start.34 = (bf16[256,2304]{1,0:T(8,128)(2,1)}, bf16[256,2304]{1,0:T(8,128)(2,1)S(1)}, u32[]{:S(2)}, u32[]{:S(2)}) collective-permute-start(bf16[256,2304]{1,0:T(8,128)(2,1)} %pad_maximum_fusion.3), channel_id=1, source_target_pairs={{0,8},{4,12},{8,0},{12,4},{16,24},{20,28},{24,16},{28,20},{1,9},{5... | collective-permute-start | bytes 3538952 | tf_op jit(solution)/shard_map/ppermute | solution.py:564
  351.0 37.5 %collective-permute-start.43 = (bf16[512,1536]{1,0:T(8,128)(2,1)}, bf16[512,1536]{1,0:T(8,128)(2,1)S(1)}, u32[]{:S(2)}, u32[]{:S(2)}) collective-permute-start(bf16[512,1536]{1,0:T(8,128)(2,1)} %get-tuple-element.164), channel_id=1, source_target_pairs={{0,4},{4,0},{8,12},{12,8},{16,20},{20,16},{24,28},{28,24},{1,5},{5... | collective-permute-start | bytes 4718600 | tf_op jit(solution)/shard_map/ppermute | solution.py:564
  351.0 28.6 %collective-permute-start.41 = (bf16[256,2304]{1,0:T(8,128)(2,1)}, bf16[256,2304]{1,0:T(8,128)(2,1)S(1)}, u32[]{:S(2)}, u32[]{:S(2)}) collective-permute-start(bf16[256,2304]{1,0:T(8,128)(2,1)} %slice.851), channel_id=1, source_target_pairs={{0,16},{4,20},{8,24},{12,28},{16,0},{20,4},{24,8},{28,12},{1,17},{... | collective-permute-start | bytes 3538952 | tf_op jit(solution)/shard_map/ppermute | solution.py:564
  384.7 36.2 %collective-permute-start.40 = (bf16[512,1536]{1,0:T(8,128)(2,1)}, bf16[512,1536]{1,0:T(8,128)(2,1)S(1)}, u32[]{:S(2)}, u32[]{:S(2)}) collective-permute-start(bf16[512,1536]{1,0:T(8,128)(2,1)} %get-tuple-element.156), channel_id=1, source_target_pairs={{0,4},{4,0},{8,12},{12,8},{16,20},{20,16},{24,28},{28,24},{1,5},{5... | collective-permute-start | bytes 4718600 | tf_op jit(solution)/shard_map/ppermute | solution.py:564
  419.8 23.3 %collective-permute-start.48 = (bf16[128,1536]{1,0:T(8,128)(2,1)S(1)}, bf16[128,1536]{1,0:T(8,128)(2,1)S(1)}, u32[]{:S(2)}, u32[]{:S(2)}) collective-permute-start(bf16[128,1536]{1,0:T(8,128)(2,1)S(1)} %slice.867), channel_id=1, source_target_pairs={{0,8},{4,12},{8,0},{12,4},{16,24},{20,28},{24,16},{28,20},{1,9},{5... | collective-permute-start | bytes 1179656 | tf_op jit(solution)/shard_map/ppermute | solution.py:564
  434.8 20.2 %collective-permute-start.47 = (bf16[256,1536]{1,0:T(8,128)(2,1)S(1)}, bf16[256,1536]{1,0:T(8,128)(2,1)S(1)}, u32[]{:S(2)}, u32[]{:S(2)}) collective-permute-start(bf16[256,1536]{1,0:T(8,128)(2,1)S(1)} %pad_maximum_fusion.8), channel_id=1, source_target_pairs={{0,8},{4,12},{8,0},{12,4},{16,24},{20,28},{24,16},{28,20},{1,9},{5... | collective-permute-start | bytes 2359304 | tf_op jit(solution)/shard_map/ppermute | solution.py:564
  471.8 34.9 %collective-permute-start.74 = (bf16[128,2304]{1,0:T(8,128)(2,1)S(1)}, bf16[128,2304]{1,0:T(8,128)(2,1)S(1)}, u32[]{:S(2)}, u32[]{:S(2)}) collective-permute-start(bf16[128,2304]{1,0:T(8,128)(2,1)S(1)} %copy-done.38), channel_id=1, source_target_pairs={{0,1},{1,0},{2,3},{3,2},{4,5},{5,4},{6,7},{7,6},{8,9},{9,8},{10,11... | collective-permute-start | bytes 1769480 | tf_op jit(solution)/shard_map/ppermute | solution.py:567
  473.0 38.7 %collective-permute-start.68 = (bf16[128,768]{1,0:T(8,128)(2,1)S(1)}, bf16[128,768]{1,0:T(8,128)(2,1)S(1)}, u32[]{:S(2)}, u32[]{:S(2)}) collective-permute-start(bf16[128,768]{1,0:T(8,128)(2,1)S(1)} %get-tuple-element.258), channel_id=1, source_target_pairs={{0,2},{1,3},{2,0},{3,1},{4,6},{5,7},{6,4},{7,5},{8,10},{9,11},{10,... | collective-permute-start | bytes 589832 | tf_op jit(solution)/shard_map/ppermute | solution.py:567
  (117 other events, 1088.0 us)
Sparse Core Ops, SparseCore 0:
  16.0 163.1 all-gather.2
